TPU v7x, 768 devices: a whole 4x8x12 slice. The times are simulated.
768 devices in a mesh: loop: 24 (over z_lo, x), grp: 32 (over z_hi, y, core).
Axes of the slice: x: 4, y: 8, z: 12 (z_hi: 2, z_lo: 6; z = z_hi * 6 + z_lo), core: 2. Of those that a mesh axis runs over, the one named last changes fastest.
Arguments:
- queries: bfloat16 [12288, 1024], P(('loop', 'grp')), may hold values from -100 to 100
- landmarks: bfloat16 [49152, 1024], P(('loop', 'grp')), may hold values from -20 to 20
- labels: bfloat16 [49152, 128], P(('loop', 'grp')), may hold values from -6 to 6
- tile_mask: int32 [24, 768], replicated, may hold values from 0 to 1, as said below
Outputs:
- label_scores: bfloat16 [12288, 128], P(('loop', 'grp'))
Inputs may be any that keep to these rules, and one draw needn't show every extreme that they name: `tile_mask`: every query tile lists at least one landmark tile.
All inputs are finite; a program needn't handle non-finite values.
Results may differ from a plain program's by a relative error of at most 0.0065.
Values may be sent and summed in bfloat16 or wider, within the bound.
No kernel may reach another device: no remote copies, remote signals or barrier semaphores. Data moves between devices by JAX's collectives and lax.ppermute only.
A program may use at most 32 MiB of HBM per device.

v0:
```python
import math

import jax
import jax.numpy as jnp
from jax import lax
from jax.sharding import PartitionSpec as P


def from_behind(value, axis, steps):
    count = lax.axis_size(axis)
    pairs = [(source, (source + steps) % count) for source in range(count)]
    return lax.ppermute(value, axis, pairs)


def combined_all(part, axis, combine):
    gathered = jax.tree.map(lambda a: lax.all_gather(a, axis), part)

    def take(source):
        return jax.tree.map(lambda a: lax.dynamic_index_in_dim(a, source, 0, False), gathered)

    return lax.fori_loop(
        1, lax.axis_size(axis), lambda source, state: combine(state, take(source)), take(0)
    )


def combine(first, second):
    first_max, first_sum, first_labels = first
    second_max, second_sum, second_labels = second
    joint_max = jnp.maximum(first_max, second_max)
    first_keep = jnp.exp(first_max - joint_max)
    second_keep = jnp.exp(second_max - joint_max)
    return (
        joint_max,
        first_sum * first_keep + second_sum * second_keep,
        first_labels * first_keep[:, None] + second_labels * second_keep[:, None],
    )


def local(queries, landmarks, labels, tile_mask):
    query_slab = lax.all_gather(queries, "grp", axis=0, tiled=True)
    n_loop = lax.axis_size("loop")
    n_grp = lax.axis_size("grp")
    cycle_pos = lax.axis_index("loop")
    column = lax.axis_index("grp")
    feature_width = landmarks.shape[1]
    slab_rows = query_slab.shape[0]
    classes = labels.shape[1]
    scale_factor = 4.0 / math.sqrt(feature_width)
    listed_row = lax.dynamic_index_in_dim(tile_mask, cycle_pos, 0, keepdims=False)
    packed = jnp.concatenate([landmarks, labels], axis=1)

    def absorb(carried, packed_tile, source):
        listed = (
            lax.dynamic_index_in_dim(listed_row, source * n_grp + column, 0, keepdims=False) > 0
        )
        row_max, weight_sum, label_sum = carried
        land_rows = packed_tile[:, :feature_width]
        label_rows = packed_tile[:, feature_width:]
        land_f = land_rows.astype(jnp.float32)
        half_norm = 0.5 * jnp.sum(land_f * land_f, axis=1)
        logits = lax.dot_general(
            query_slab, land_rows, (((1,), (1,)), ((), ())), preferred_element_type=jnp.float32
        )
        logits = (logits - half_norm[None, :]) * scale_factor
        new_max = jnp.where(listed, jnp.maximum(row_max, jnp.max(logits, axis=1)), row_max)
        kernel = jnp.where(listed, jnp.exp(logits - new_max[:, None]), jnp.float32(0.0))
        rescale = jnp.exp(row_max - new_max)
        new_labels = label_sum * rescale[:, None] + jnp.dot(
            kernel.astype(jnp.bfloat16), label_rows, preferred_element_type=jnp.float32
        )
        return (new_max, weight_sum * rescale + jnp.sum(kernel, axis=1), new_labels)

    initial = (
        jnp.full((slab_rows,), -1e30, jnp.float32),
        jnp.zeros((slab_rows,), jnp.float32),
        jnp.zeros((slab_rows, classes), jnp.float32),
    )
    carried = absorb(initial, packed, cycle_pos)

    def cycle_step(offset, state):
        current, moving = state
        moving = from_behind(moving, "loop", 1)
        current = absorb(current, moving, (cycle_pos - offset) % n_loop)
        return (current, moving)

    carried, moving = lax.fori_loop(1, n_loop, cycle_step, (carried, packed))
    row_max, weight_sum, label_sum = combined_all(carried, "grp", combine)
    result = (label_sum / weight_sum[:, None]).astype(jnp.bfloat16)
    return lax.dynamic_slice_in_dim(result, column * queries.shape[0], queries.shape[0], 0)


def solution(mesh):
    in_specs = (P(("loop", "grp"), None), P(("loop", "grp"), None), P(("loop", "grp"), None), P())
    out_specs = P(("loop", "grp"), None)
    return jax.shard_map(local, mesh=mesh, in_specs=in_specs, out_specs=out_specs, check_vma=False)
```

profile of v0, /device:TPU:1, one launch (start us, length us, event | category | flops | bytes accessed | tf_op | source)
XLA Modules:
  0.0 701.6 jit_solution(16013751103156871248)
XLA Ops:
  11.9 107.4 %all-gather.8.cloned.1.call-done = bf16[512,1024]{1,0:T(8,128)(2,1)} async-done(((bf16[16,1024]{1,0:T(8,128)(2,1)}), bf16[512,1024]{1,0:T(8,128)(2,1)}) %all-gather.8.cloned.1.call-update) | async-done | bytes 1048592 | tf_op jit(solution)/shard_map/all_gather | solution.py:40
  122.1 349.4 %while.40 = (s32[]{:T(128)}, f32[512]{0:T(512)S(1)}, f32[512]{0:T(512)S(1)}, f32[512,128]{1,0:T(8,128)S(1)}, bf16[64,1152]{1,0:T(8,128)(2,1)S(1)}, /*index=5*/s3...) while((s32[]{:T(128)}, f32[512]{0:T(512)S(1)}, ...), condition=%wide.region_7.8_spmd, body=%wide.region_3.7_spmd.sunk | while | flops 76121600 | bytes 3163725 | solution.py:86
  122.1 3.1 collective-permute-start
  126.4 9.6 %collective-permute-done = bf16[64,1152]{1,0:T(8,128)(2,1)S(1)} collective-permute-done((bf16[64,1152]{1,0:T(8,128)(2,1)S(1)}, bf16[64,1152]{1,0:T(8,128)(2,1)S(1)}, u32[]{:S(2)}, u32[]{:S(2)}) %collective-permute-start) | collective-permute-done | bytes 147488 | tf_op jit(solution)/shard_map/while/body/eval_jaxpr/ppermute | solution.py:12
  138.2 1.9 collective-permute-start
  141.3 9.7 %collective-permute-done = bf16[64,1152]{1,0:T(8,128)(2,1)S(1)} collective-permute-done((bf16[64,1152]{1,0:T(8,128)(2,1)S(1)}, bf16[64,1152]{1,0:T(8,128)(2,1)S(1)}, u32[]{:S(2)}, u32[]{:S(2)}) %collective-permute-start) | collective-permute-done | bytes 147488 | tf_op jit(solution)/shard_map/while/body/eval_jaxpr/ppermute | solution.py:12
  153.2 1.9 collective-permute-start
  156.3 9.7 %collective-permute-done = bf16[64,1152]{1,0:T(8,128)(2,1)S(1)} collective-permute-done((bf16[64,1152]{1,0:T(8,128)(2,1)S(1)}, bf16[64,1152]{1,0:T(8,128)(2,1)S(1)}, u32[]{:S(2)}, u32[]{:S(2)}) %collective-permute-start) | collective-permute-done | bytes 147488 | tf_op jit(solution)/shard_map/while/body/eval_jaxpr/ppermute | solution.py:12
  168.2 1.9 collective-permute-start
  171.3 9.7 %collective-permute-done = bf16[64,1152]{1,0:T(8,128)(2,1)S(1)} collective-permute-done((bf16[64,1152]{1,0:T(8,128)(2,1)S(1)}, bf16[64,1152]{1,0:T(8,128)(2,1)S(1)}, u32[]{:S(2)}, u32[]{:S(2)}) %collective-permute-start) | collective-permute-done | bytes 147488 | tf_op jit(solution)/shard_map/while/body/eval_jaxpr/ppermute | solution.py:12
  183.3 1.9 collective-permute-start
  186.4 9.7 %collective-permute-done = bf16[64,1152]{1,0:T(8,128)(2,1)S(1)} collective-permute-done((bf16[64,1152]{1,0:T(8,128)(2,1)S(1)}, bf16[64,1152]{1,0:T(8,128)(2,1)S(1)}, u32[]{:S(2)}, u32[]{:S(2)}) %collective-permute-start) | collective-permute-done | bytes 147488 | tf_op jit(solution)/shard_map/while/body/eval_jaxpr/ppermute | solution.py:12
  198.3 1.9 collective-permute-start
  201.4 9.7 %collective-permute-done = bf16[64,1152]{1,0:T(8,128)(2,1)S(1)} collective-permute-done((bf16[64,1152]{1,0:T(8,128)(2,1)S(1)}, bf16[64,1152]{1,0:T(8,128)(2,1)S(1)}, u32[]{:S(2)}, u32[]{:S(2)}) %collective-permute-start) | collective-permute-done | bytes 147488 | tf_op jit(solution)/shard_map/while/body/eval_jaxpr/ppermute | solution.py:12
  213.3 1.9 collective-permute-start
  216.4 9.7 %collective-permute-done = bf16[64,1152]{1,0:T(8,128)(2,1)S(1)} collective-permute-done((bf16[64,1152]{1,0:T(8,128)(2,1)S(1)}, bf16[64,1152]{1,0:T(8,128)(2,1)S(1)}, u32[]{:S(2)}, u32[]{:S(2)}) %collective-permute-start) | collective-permute-done | bytes 147488 | tf_op jit(solution)/shard_map/while/body/eval_jaxpr/ppermute | solution.py:12
  228.3 1.9 collective-permute-start
  231.4 9.7 %collective-permute-done = bf16[64,1152]{1,0:T(8,128)(2,1)S(1)} collective-permute-done((bf16[64,1152]{1,0:T(8,128)(2,1)S(1)}, bf16[64,1152]{1,0:T(8,128)(2,1)S(1)}, u32[]{:S(2)}, u32[]{:S(2)}) %collective-permute-start) | collective-permute-done | bytes 147488 | tf_op jit(solution)/shard_map/while/body/eval_jaxpr/ppermute | solution.py:12
  243.3 1.9 collective-permute-start
  246.4 9.7 %collective-permute-done = bf16[64,1152]{1,0:T(8,128)(2,1)S(1)} collective-permute-done((bf16[64,1152]{1,0:T(8,128)(2,1)S(1)}, bf16[64,1152]{1,0:T(8,128)(2,1)S(1)}, u32[]{:S(2)}, u32[]{:S(2)}) %collective-permute-start) | collective-permute-done | bytes 147488 | tf_op jit(solution)/shard_map/while/body/eval_jaxpr/ppermute | solution.py:12
  258.3 1.9 collective-permute-start
  261.4 9.7 %collective-permute-done = bf16[64,1152]{1,0:T(8,128)(2,1)S(1)} collective-permute-done((bf16[64,1152]{1,0:T(8,128)(2,1)S(1)}, bf16[64,1152]{1,0:T(8,128)(2,1)S(1)}, u32[]{:S(2)}, u32[]{:S(2)}) %collective-permute-start) | collective-permute-done | bytes 147488 | tf_op jit(solution)/shard_map/while/body/eval_jaxpr/ppermute | solution.py:12
  273.3 1.9 collective-permute-start
  276.4 9.7 %collective-permute-done = bf16[64,1152]{1,0:T(8,128)(2,1)S(1)} collective-permute-done((bf16[64,1152]{1,0:T(8,128)(2,1)S(1)}, bf16[64,1152]{1,0:T(8,128)(2,1)S(1)}, u32[]{:S(2)}, u32[]{:S(2)}) %collective-permute-start) | collective-permute-done | bytes 147488 | tf_op jit(solution)/shard_map/while/body/eval_jaxpr/ppermute | solution.py:12
  288.4 1.9 collective-permute-start
  291.5 9.7 %collective-permute-done = bf16[64,1152]{1,0:T(8,128)(2,1)S(1)} collective-permute-done((bf16[64,1152]{1,0:T(8,128)(2,1)S(1)}, bf16[64,1152]{1,0:T(8,128)(2,1)S(1)}, u32[]{:S(2)}, u32[]{:S(2)}) %collective-permute-start) | collective-permute-done | bytes 147488 | tf_op jit(solution)/shard_map/while/body/eval_jaxpr/ppermute | solution.py:12
  303.4 1.9 collective-permute-start
  306.5 9.7 %collective-permute-done = bf16[64,1152]{1,0:T(8,128)(2,1)S(1)} collective-permute-done((bf16[64,1152]{1,0:T(8,128)(2,1)S(1)}, bf16[64,1152]{1,0:T(8,128)(2,1)S(1)}, u32[]{:S(2)}, u32[]{:S(2)}) %collective-permute-start) | collective-permute-done | bytes 147488 | tf_op jit(solution)/shard_map/while/body/eval_jaxpr/ppermute | solution.py:12
  318.4 1.9 collective-permute-start
  321.5 10.5 %collective-permute-done = bf16[64,1152]{1,0:T(8,128)(2,1)S(1)} collective-permute-done((bf16[64,1152]{1,0:T(8,128)(2,1)S(1)}, bf16[64,1152]{1,0:T(8,128)(2,1)S(1)}, u32[]{:S(2)}, u32[]{:S(2)}) %collective-permute-start) | collective-permute-done | bytes 147488 | tf_op jit(solution)/shard_map/while/body/eval_jaxpr/ppermute | solution.py:12
  334.2 1.9 collective-permute-start
  337.3 11.2 %collective-permute-done = bf16[64,1152]{1,0:T(8,128)(2,1)S(1)} collective-permute-done((bf16[64,1152]{1,0:T(8,128)(2,1)S(1)}, bf16[64,1152]{1,0:T(8,128)(2,1)S(1)}, u32[]{:S(2)}, u32[]{:S(2)}) %collective-permute-start) | collective-permute-done | bytes 147488 | tf_op jit(solution)/shard_map/while/body/eval_jaxpr/ppermute | solution.py:12
  350.7 1.9 collective-permute-start
  353.8 10.3 %collective-permute-done = bf16[64,1152]{1,0:T(8,128)(2,1)S(1)} collective-permute-done((bf16[64,1152]{1,0:T(8,128)(2,1)S(1)}, bf16[64,1152]{1,0:T(8,128)(2,1)S(1)}, u32[]{:S(2)}, u32[]{:S(2)}) %collective-permute-start) | collective-permute-done | bytes 147488 | tf_op jit(solution)/shard_map/while/body/eval_jaxpr/ppermute | solution.py:12
  366.4 1.9 collective-permute-start
  369.5 9.7 %collective-permute-done = bf16[64,1152]{1,0:T(8,128)(2,1)S(1)} collective-permute-done((bf16[64,1152]{1,0:T(8,128)(2,1)S(1)}, bf16[64,1152]{1,0:T(8,128)(2,1)S(1)}, u32[]{:S(2)}, u32[]{:S(2)}) %collective-permute-start) | collective-permute-done | bytes 147488 | tf_op jit(solution)/shard_map/while/body/eval_jaxpr/ppermute | solution.py:12
  381.4 1.9 collective-permute-start
  384.5 9.7 %collective-permute-done = bf16[64,1152]{1,0:T(8,128)(2,1)S(1)} collective-permute-done((bf16[64,1152]{1,0:T(8,128)(2,1)S(1)}, bf16[64,1152]{1,0:T(8,128)(2,1)S(1)}, u32[]{:S(2)}, u32[]{:S(2)}) %collective-permute-start) | collective-permute-done | bytes 147488 | tf_op jit(solution)/shard_map/while/body/eval_jaxpr/ppermute | solution.py:12
  399.5 9.7 %collective-permute-done = bf16[64,1152]{1,0:T(8,128)(2,1)S(1)} collective-permute-done((bf16[64,1152]{1,0:T(8,128)(2,1)S(1)}, bf16[64,1152]{1,0:T(8,128)(2,1)S(1)}, u32[]{:S(2)}, u32[]{:S(2)}) %collective-permute-start) | collective-permute-done | bytes 147488 | tf_op jit(solution)/shard_map/while/body/eval_jaxpr/ppermute | solution.py:12
  414.5 9.7 %collective-permute-done = bf16[64,1152]{1,0:T(8,128)(2,1)S(1)} collective-permute-done((bf16[64,1152]{1,0:T(8,128)(2,1)S(1)}, bf16[64,1152]{1,0:T(8,128)(2,1)S(1)}, u32[]{:S(2)}, u32[]{:S(2)}) %collective-permute-start) | collective-permute-done | bytes 147488 | tf_op jit(solution)/shard_map/while/body/eval_jaxpr/ppermute | solution.py:12
  429.5 9.7 %collective-permute-done = bf16[64,1152]{1,0:T(8,128)(2,1)S(1)} collective-permute-done((bf16[64,1152]{1,0:T(8,128)(2,1)S(1)}, bf16[64,1152]{1,0:T(8,128)(2,1)S(1)}, u32[]{:S(2)}, u32[]{:S(2)}) %collective-permute-start) | collective-permute-done | bytes 147488 | tf_op jit(solution)/shard_map/while/body/eval_jaxpr/ppermute | solution.py:12
  441.4 1.9 collective-permute-start
  444.6 9.7 %collective-permute-done = bf16[64,1152]{1,0:T(8,128)(2,1)S(1)} collective-permute-done((bf16[64,1152]{1,0:T(8,128)(2,1)S(1)}, bf16[64,1152]{1,0:T(8,128)(2,1)S(1)}, u32[]{:S(2)}, u32[]{:S(2)}) %collective-permute-start) | collective-permute-done | bytes 147488 | tf_op jit(solution)/shard_map/while/body/eval_jaxpr/ppermute | solution.py:12
  459.6 9.7 %collective-permute-done = bf16[64,1152]{1,0:T(8,128)(2,1)S(1)} collective-permute-done((bf16[64,1152]{1,0:T(8,128)(2,1)S(1)}, bf16[64,1152]{1,0:T(8,128)(2,1)S(1)}, u32[]{:S(2)}, u32[]{:S(2)}) %collective-permute-start) | collective-permute-done | bytes 147488 | tf_op jit(solution)/shard_map/while/body/eval_jaxpr/ppermute | solution.py:12
  472.2 84.1 %all-gather.3 = f32[32,1,512]{2,1,0:T(1,128)S(1)} all-gather(f32[1,1,512]{2,1,0:T(1,128)S(1)} %bitcast.33), channel_id=2, replica_groups=mesh['loop'=24,'grp'=32] {'grp'}, dimensions={0}, use_global_device_ids=true | all-gather | bytes 67584 | tf_op jit(solution)/shard_map/all_gather | solution.py:16
  556.3 89.3 %all-gather.4 = f32[32,1,512]{2,1,0:T(1,128)S(1)} all-gather(f32[1,1,512]{2,1,0:T(1,128)S(1)} %bitcast.37), channel_id=3, replica_groups=mesh['loop'=24,'grp'=32] {'grp'}, dimensions={0}, use_global_device_ids=true | all-gather | bytes 67584 | tf_op jit(solution)/shard_map/all_gather | solution.py:16
  645.7 7.9 %all-gather.10.cloned.1.call-done = f32[16384,128]{1,0:T(8,128)} async-done(((f32[512,128]{1,0:T(8,128)}), f32[16384,128]{1,0:T(8,128)}) %all-gather.10.cloned.1.call-update) | async-done | bytes 8388624 | tf_op jit(solution)/shard_map/all_gather | solution.py:16
  654.6 39.4 %while.41 = (s32[]{:T(128)}, f32[512]{0:T(512)S(1)}, f32[512]{0:T(512)S(1)}, f32[512,128]{1,0:T(8,128)S(1)}, f32[32,512]{1,0:T(8,128)S(1)}, /*index=5*/f32[32,51...) while((s32[]{:T(128)}, f32[512]{0:T(512)S(1)}, f32[512]{0:T(512)S(1)}, ...), condition=%wide.region_9.10_spmd, body=%wide.region_8.9_spmd.sunk | while | flops 199685 | bytes 815247 | solution.py:21
  (350 shorter events, 119.3 us)
Async XLA Ops:
  6.5 112.8 %all-gather.8.cloned.1.call-start = ((), (), s32[]{:S(2)}) async-start(), calls=%async_computation | async-start | bytes 1081344 | tf_op jit(solution)/shard_map/all_gather | solution.py:40
  7.3 646.4 %all-gather.10.cloned.1.call-start = ((), (), s32[]{:S(2)}) async-start(), calls=%async_computation.1 | async-start | bytes 8650752 | tf_op jit(solution)/shard_map/all_gather | solution.py:16
  122.1 13.9 %collective-permute-start = (bf16[64,1152]{1,0:T(8,128)(2,1)S(1)}, bf16[64,1152]{1,0:T(8,128)(2,1)S(1)}, u32[]{:S(2)}, u32[]{:S(2)}) collective-permute-start(bf16[64,1152]{1,0:T(8,128)(2,1)S(1)} %get-tuple-element.593), channel_id=1, source_target_pairs={{0,32},{32,64},{64,96},{96,128},{128,160},{160,192},{192,224},{224... | collective-permute-start | bytes 442376 | tf_op jit(solution)/shard_map/while/body/eval_jaxpr/ppermute | solution.py:12
  138.2 12.8 %collective-permute-start = (bf16[64,1152]{1,0:T(8,128)(2,1)S(1)}, bf16[64,1152]{1,0:T(8,128)(2,1)S(1)}, u32[]{:S(2)}, u32[]{:S(2)}) collective-permute-start(bf16[64,1152]{1,0:T(8,128)(2,1)S(1)} %get-tuple-element.593), channel_id=1, source_target_pairs={{0,32},{32,64},{64,96},{96,128},{128,160},{160,192},{192,224},{224... | collective-permute-start | bytes 442376 | tf_op jit(solution)/shard_map/while/body/eval_jaxpr/ppermute | solution.py:12
  153.2 12.8 %collective-permute-start = (bf16[64,1152]{1,0:T(8,128)(2,1)S(1)}, bf16[64,1152]{1,0:T(8,128)(2,1)S(1)}, u32[]{:S(2)}, u32[]{:S(2)}) collective-permute-start(bf16[64,1152]{1,0:T(8,128)(2,1)S(1)} %get-tuple-element.593), channel_id=1, source_target_pairs={{0,32},{32,64},{64,96},{96,128},{128,160},{160,192},{192,224},{224... | collective-permute-start | bytes 442376 | tf_op jit(solution)/shard_map/while/body/eval_jaxpr/ppermute | solution.py:12
  168.2 12.8 %collective-permute-start = (bf16[64,1152]{1,0:T(8,128)(2,1)S(1)}, bf16[64,1152]{1,0:T(8,128)(2,1)S(1)}, u32[]{:S(2)}, u32[]{:S(2)}) collective-permute-start(bf16[64,1152]{1,0:T(8,128)(2,1)S(1)} %get-tuple-element.593), channel_id=1, source_target_pairs={{0,32},{32,64},{64,96},{96,128},{128,160},{160,192},{192,224},{224... | collective-permute-start | bytes 442376 | tf_op jit(solution)/shard_map/while/body/eval_jaxpr/ppermute | solution.py:12
  183.3 12.8 %collective-permute-start = (bf16[64,1152]{1,0:T(8,128)(2,1)S(1)}, bf16[64,1152]{1,0:T(8,128)(2,1)S(1)}, u32[]{:S(2)}, u32[]{:S(2)}) collective-permute-start(bf16[64,1152]{1,0:T(8,128)(2,1)S(1)} %get-tuple-element.593), channel_id=1, source_target_pairs={{0,32},{32,64},{64,96},{96,128},{128,160},{160,192},{192,224},{224... | collective-permute-start | bytes 442376 | tf_op jit(solution)/shard_map/while/body/eval_jaxpr/ppermute | solution.py:12
  198.3 12.8 %collective-permute-start = (bf16[64,1152]{1,0:T(8,128)(2,1)S(1)}, bf16[64,1152]{1,0:T(8,128)(2,1)S(1)}, u32[]{:S(2)}, u32[]{:S(2)}) collective-permute-start(bf16[64,1152]{1,0:T(8,128)(2,1)S(1)} %get-tuple-element.593), channel_id=1, source_target_pairs={{0,32},{32,64},{64,96},{96,128},{128,160},{160,192},{192,224},{224... | collective-permute-start | bytes 442376 | tf_op jit(solution)/shard_map/while/body/eval_jaxpr/ppermute | solution.py:12
  213.3 12.8 %collective-permute-start = (bf16[64,1152]{1,0:T(8,128)(2,1)S(1)}, bf16[64,1152]{1,0:T(8,128)(2,1)S(1)}, u32[]{:S(2)}, u32[]{:S(2)}) collective-permute-start(bf16[64,1152]{1,0:T(8,128)(2,1)S(1)} %get-tuple-element.593), channel_id=1, source_target_pairs={{0,32},{32,64},{64,96},{96,128},{128,160},{160,192},{192,224},{224... | collective-permute-start | bytes 442376 | tf_op jit(solution)/shard_map/while/body/eval_jaxpr/ppermute | solution.py:12
  228.3 12.8 %collective-permute-start = (bf16[64,1152]{1,0:T(8,128)(2,1)S(1)}, bf16[64,1152]{1,0:T(8,128)(2,1)S(1)}, u32[]{:S(2)}, u32[]{:S(2)}) collective-permute-start(bf16[64,1152]{1,0:T(8,128)(2,1)S(1)} %get-tuple-element.593), channel_id=1, source_target_pairs={{0,32},{32,64},{64,96},{96,128},{128,160},{160,192},{192,224},{224... | collective-permute-start | bytes 442376 | tf_op jit(solution)/shard_map/while/body/eval_jaxpr/ppermute | solution.py:12
  243.3 12.8 %collective-permute-start = (bf16[64,1152]{1,0:T(8,128)(2,1)S(1)}, bf16[64,1152]{1,0:T(8,128)(2,1)S(1)}, u32[]{:S(2)}, u32[]{:S(2)}) collective-permute-start(bf16[64,1152]{1,0:T(8,128)(2,1)S(1)} %get-tuple-element.593), channel_id=1, source_target_pairs={{0,32},{32,64},{64,96},{96,128},{128,160},{160,192},{192,224},{224... | collective-permute-start | bytes 442376 | tf_op jit(solution)/shard_map/while/body/eval_jaxpr/ppermute | solution.py:12
  258.3 12.8 %collective-permute-start = (bf16[64,1152]{1,0:T(8,128)(2,1)S(1)}, bf16[64,1152]{1,0:T(8,128)(2,1)S(1)}, u32[]{:S(2)}, u32[]{:S(2)}) collective-permute-start(bf16[64,1152]{1,0:T(8,128)(2,1)S(1)} %get-tuple-element.593), channel_id=1, source_target_pairs={{0,32},{32,64},{64,96},{96,128},{128,160},{160,192},{192,224},{224... | collective-permute-start | bytes 442376 | tf_op jit(solution)/shard_map/while/body/eval_jaxpr/ppermute | solution.py:12
  273.3 12.8 %collective-permute-start = (bf16[64,1152]{1,0:T(8,128)(2,1)S(1)}, bf16[64,1152]{1,0:T(8,128)(2,1)S(1)}, u32[]{:S(2)}, u32[]{:S(2)}) collective-permute-start(bf16[64,1152]{1,0:T(8,128)(2,1)S(1)} %get-tuple-element.593), channel_id=1, source_target_pairs={{0,32},{32,64},{64,96},{96,128},{128,160},{160,192},{192,224},{224... | collective-permute-start | bytes 442376 | tf_op jit(solution)/shard_map/while/body/eval_jaxpr/ppermute | solution.py:12
  288.4 12.8 %collective-permute-start = (bf16[64,1152]{1,0:T(8,128)(2,1)S(1)}, bf16[64,1152]{1,0:T(8,128)(2,1)S(1)}, u32[]{:S(2)}, u32[]{:S(2)}) collective-permute-start(bf16[64,1152]{1,0:T(8,128)(2,1)S(1)} %get-tuple-element.593), channel_id=1, source_target_pairs={{0,32},{32,64},{64,96},{96,128},{128,160},{160,192},{192,224},{224... | collective-permute-start | bytes 442376 | tf_op jit(solution)/shard_map/while/body/eval_jaxpr/ppermute | solution.py:12
  303.4 12.8 %collective-permute-start = (bf16[64,1152]{1,0:T(8,128)(2,1)S(1)}, bf16[64,1152]{1,0:T(8,128)(2,1)S(1)}, u32[]{:S(2)}, u32[]{:S(2)}) collective-permute-start(bf16[64,1152]{1,0:T(8,128)(2,1)S(1)} %get-tuple-element.593), channel_id=1, source_target_pairs={{0,32},{32,64},{64,96},{96,128},{128,160},{160,192},{192,224},{224... | collective-permute-start | bytes 442376 | tf_op jit(solution)/shard_map/while/body/eval_jaxpr/ppermute | solution.py:12
  318.4 13.6 %collective-permute-start = (bf16[64,1152]{1,0:T(8,128)(2,1)S(1)}, bf16[64,1152]{1,0:T(8,128)(2,1)S(1)}, u32[]{:S(2)}, u32[]{:S(2)}) collective-permute-start(bf16[64,1152]{1,0:T(8,128)(2,1)S(1)} %get-tuple-element.593), channel_id=1, source_target_pairs={{0,32},{32,64},{64,96},{96,128},{128,160},{160,192},{192,224},{224... | collective-permute-start | bytes 442376 | tf_op jit(solution)/shard_map/while/body/eval_jaxpr/ppermute | solution.py:12
  334.2 14.3 %collective-permute-start = (bf16[64,1152]{1,0:T(8,128)(2,1)S(1)}, bf16[64,1152]{1,0:T(8,128)(2,1)S(1)}, u32[]{:S(2)}, u32[]{:S(2)}) collective-permute-start(bf16[64,1152]{1,0:T(8,128)(2,1)S(1)} %get-tuple-element.593), channel_id=1, source_target_pairs={{0,32},{32,64},{64,96},{96,128},{128,160},{160,192},{192,224},{224... | collective-permute-start | bytes 442376 | tf_op jit(solution)/shard_map/while/body/eval_jaxpr/ppermute | solution.py:12
  350.7 13.4 %collective-permute-start = (bf16[64,1152]{1,0:T(8,128)(2,1)S(1)}, bf16[64,1152]{1,0:T(8,128)(2,1)S(1)}, u32[]{:S(2)}, u32[]{:S(2)}) collective-permute-start(bf16[64,1152]{1,0:T(8,128)(2,1)S(1)} %get-tuple-element.593), channel_id=1, source_target_pairs={{0,32},{32,64},{64,96},{96,128},{128,160},{160,192},{192,224},{224... | collective-permute-start | bytes 442376 | tf_op jit(solution)/shard_map/while/body/eval_jaxpr/ppermute | solution.py:12
  366.4 12.8 %collective-permute-start = (bf16[64,1152]{1,0:T(8,128)(2,1)S(1)}, bf16[64,1152]{1,0:T(8,128)(2,1)S(1)}, u32[]{:S(2)}, u32[]{:S(2)}) collective-permute-start(bf16[64,1152]{1,0:T(8,128)(2,1)S(1)} %get-tuple-element.593), channel_id=1, source_target_pairs={{0,32},{32,64},{64,96},{96,128},{128,160},{160,192},{192,224},{224... | collective-permute-start | bytes 442376 | tf_op jit(solution)/shard_map/while/body/eval_jaxpr/ppermute | solution.py:12
  381.4 12.8 %collective-permute-start = (bf16[64,1152]{1,0:T(8,128)(2,1)S(1)}, bf16[64,1152]{1,0:T(8,128)(2,1)S(1)}, u32[]{:S(2)}, u32[]{:S(2)}) collective-permute-start(bf16[64,1152]{1,0:T(8,128)(2,1)S(1)} %get-tuple-element.593), channel_id=1, source_target_pairs={{0,32},{32,64},{64,96},{96,128},{128,160},{160,192},{192,224},{224... | collective-permute-start | bytes 442376 | tf_op jit(solution)/shard_map/while/body/eval_jaxpr/ppermute | solution.py:12
  396.4 12.8 %collective-permute-start = (bf16[64,1152]{1,0:T(8,128)(2,1)S(1)}, bf16[64,1152]{1,0:T(8,128)(2,1)S(1)}, u32[]{:S(2)}, u32[]{:S(2)}) collective-permute-start(bf16[64,1152]{1,0:T(8,128)(2,1)S(1)} %get-tuple-element.593), channel_id=1, source_target_pairs={{0,32},{32,64},{64,96},{96,128},{128,160},{160,192},{192,224},{224... | collective-permute-start | bytes 442376 | tf_op jit(solution)/shard_map/while/body/eval_jaxpr/ppermute | solution.py:12
  411.4 12.8 %collective-permute-start = (bf16[64,1152]{1,0:T(8,128)(2,1)S(1)}, bf16[64,1152]{1,0:T(8,128)(2,1)S(1)}, u32[]{:S(2)}, u32[]{:S(2)}) collective-permute-start(bf16[64,1152]{1,0:T(8,128)(2,1)S(1)} %get-tuple-element.593), channel_id=1, source_target_pairs={{0,32},{32,64},{64,96},{96,128},{128,160},{160,192},{192,224},{224... | collective-permute-start | bytes 442376 | tf_op jit(solution)/shard_map/while/body/eval_jaxpr/ppermute | solution.py:12
  426.4 12.8 %collective-permute-start = (bf16[64,1152]{1,0:T(8,128)(2,1)S(1)}, bf16[64,1152]{1,0:T(8,128)(2,1)S(1)}, u32[]{:S(2)}, u32[]{:S(2)}) collective-permute-start(bf16[64,1152]{1,0:T(8,128)(2,1)S(1)} %get-tuple-element.593), channel_id=1, source_target_pairs={{0,32},{32,64},{64,96},{96,128},{128,160},{160,192},{192,224},{224... | collective-permute-start | bytes 442376 | tf_op jit(solution)/shard_map/while/body/eval_jaxpr/ppermute | solution.py:12
  441.4 12.8 %collective-permute-start = (bf16[64,1152]{1,0:T(8,128)(2,1)S(1)}, bf16[64,1152]{1,0:T(8,128)(2,1)S(1)}, u32[]{:S(2)}, u32[]{:S(2)}) collective-permute-start(bf16[64,1152]{1,0:T(8,128)(2,1)S(1)} %get-tuple-element.593), channel_id=1, source_target_pairs={{0,32},{32,64},{64,96},{96,128},{128,160},{160,192},{192,224},{224... | collective-permute-start | bytes 442376 | tf_op jit(solution)/shard_map/while/body/eval_jaxpr/ppermute | solution.py:12
  456.5 12.8 %collective-permute-start = (bf16[64,1152]{1,0:T(8,128)(2,1)S(1)}, bf16[64,1152]{1,0:T(8,128)(2,1)S(1)}, u32[]{:S(2)}, u32[]{:S(2)}) collective-permute-start(bf16[64,1152]{1,0:T(8,128)(2,1)S(1)} %get-tuple-element.593), channel_id=1, source_target_pairs={{0,32},{32,64},{64,96},{96,128},{128,160},{160,192},{192,224},{224... | collective-permute-start | bytes 442376 | tf_op jit(solution)/shard_map/while/body/eval_jaxpr/ppermute | solution.py:12
  471.5 0.7 copy-start
Sparse Core Ops, SparseCore 0:
  11.3 108.0 all-gather.7
  472.3 181.2 all-gather.9
where the time goes:
time: 705 us; the launch traced here: 702 us
  waiting for transfers between devices  342 us (49%)
  blocking collectives  173 us (25%)
  matrix products  47.6 us (7%)
  starting transfers between devices  45.4 us (6%)
  other arithmetic  45.3 us (6%)
  local copies, waits for them, and re-layouts  18 us (3%)
  loops' own time  15.9 us (2%)
  between operations  14.1 us (2%)
    ppermute x23, waiting for transfers between devices, from_behind(): return lax.ppermute(value, axis, pairs)  226 us
    all_gather x2, blocking collectives, combined_all(): gathered = jax.tree.map(lambda a: lax.all_gather(a, axis), part)  173 us
    all_gather x1, waiting for transfers between devices, local(): query_slab = lax.all_gather(queries, 'grp', axis=0, tiled=True)  107 us
    ppermute x23, starting transfers between devices, from_behind(): return lax.ppermute(value, axis, pairs)  45.3 us
    dot_general x24, matrix products, absorb(): lax.dot_general(query_slab, land_rows, (((1,), (1,)), ((), ())), preferre...  40.5 us
    add x31, other arithmetic, combine(): first_labels * first_keep[:, None] + second_labels * second_keep[:, None]  37.4 us
    another operation x1, loops' own time, local(): carried, moving = lax.fori_loop(1, n_loop, cycle_step, (carried, packed))  14.9 us
    dynamic_slice x24, local copies, waits for them, and re-layouts, absorb(): lax.dynamic_index_in_dim(listed_row, source * n_grp + column, 0, keepdims...  14.8 us
  transfers between devices with their start and end apart: 25, of which 25 were waited for; matrix products, arithmetic and copies ran while one was open for 2% of the time, Pallas kernels for 0%

commit v1 on v0

v1 whole, which is shorter than its diff:
```python
import math

import jax
import jax.numpy as jnp
from jax import lax
from jax.experimental import pallas as pl
from jax.experimental.pallas import tpu as pltpu
from jax.sharding import Mesh, PartitionSpec as P

ZL, X, ZH, Y, CORE = 6, 4, 2, 8, 2
NAMES = ("zl", "x", "zh", "y", "c")
Q_AXES = ("x", "zl", "zh")
SOURCES = X * ZL * ZH
UNLISTED = -1e30


def gather_direct(value, axes, count):
    copies = jnp.broadcast_to(value[None], (count,) + value.shape)
    return lax.all_to_all(copies, axes, 0, 0, tiled=True)


def split3(value):
    high = value.astype(jnp.bfloat16)
    rest = value - high.astype(jnp.float32)
    middle = rest.astype(jnp.bfloat16)
    low = (rest - middle.astype(jnp.float32)).astype(jnp.bfloat16)
    return high, middle, low


def score_kernel(queries_ref, land_ref, bias_ref, out_ref, *, width, chunk, tile_rows, scale):
    rows = queries_ref.shape[0]
    lands = land_ref.shape[0]
    tiles = chunk // tile_rows

    def step(index):
        start = pl.multiple_of(index * chunk, chunk)
        logits = lax.dot_general(
            queries_ref[pl.ds(start, chunk), :],
            land_ref[:, :width],
            (((1,), (1,)), ((), ())),
            preferred_element_type=jnp.float32,
        )
        bias = bias_ref[index]
        logits = (logits * scale).reshape(tiles, tile_rows, lands) + bias[:, None, :]
        logits = logits.reshape(chunk, lands)
        row_max = jnp.max(logits, axis=1, keepdims=True)
        kernel = jnp.exp(logits - row_max)
        weight_sum = jnp.sum(kernel, axis=1, keepdims=True)
        label_sum = jnp.dot(
            kernel.astype(jnp.bfloat16), land_ref[:, width:], preferred_element_type=jnp.float32
        )
        out_ref[pl.ds(start, chunk), :128] = (label_sum / weight_sum).astype(jnp.bfloat16)
        lane = lax.broadcasted_iota(jnp.int32, (chunk, 128), 1)
        stats = jnp.zeros((chunk, 128), jnp.float32)
        for place, piece in enumerate(split3(row_max) + split3(weight_sum)):
            stats = jnp.where(lane == place, piece.astype(jnp.float32), stats)
        out_ref[pl.ds(start, chunk), 128:] = stats.astype(jnp.bfloat16)

    pl.loop(0, rows // chunk)(step)


def score(queries, land, bias, width, tile_rows, scale):
    rows = queries.shape[0]
    lands = land.shape[0]
    classes = land.shape[1] - width
    chunk = 8 * tile_rows
    kernel = lambda *refs: score_kernel(
        *refs, width=width, chunk=chunk, tile_rows=tile_rows, scale=scale
    )
    return pl.pallas_call(
        kernel,
        out_shape=jax.ShapeDtypeStruct((rows, classes + 128), jnp.bfloat16),
        in_specs=[pl.BlockSpec(memory_space=pltpu.VMEM)] * 3,
        out_specs=pl.BlockSpec(memory_space=pltpu.VMEM),
        cost_estimate=pl.CostEstimate(
            flops=2 * rows * lands * (width + classes),
            bytes_accessed=2 * (rows * width + lands * (width + classes) + rows * 256),
            transcendentals=rows * lands,
        ),
        name="score",
    )(queries, land, bias.reshape(rows // chunk, 8, lands))


def merge_kernel(parts_ref, out_ref):
    stats = parts_ref[:, :, 128:].astype(jnp.float32)
    row_max = stats[:, :, 0:1] + stats[:, :, 1:2] + stats[:, :, 2:3]
    weight = stats[:, :, 3:4] + stats[:, :, 4:5] + stats[:, :, 5:6]
    joint = jnp.max(row_max, axis=0, keepdims=True)
    weight = weight * jnp.exp(row_max - joint)
    total = jnp.sum(weight, axis=0)
    labels = jnp.sum(parts_ref[:, :, :128].astype(jnp.float32) * weight, axis=0)
    out_ref[...] = (labels / total).astype(jnp.bfloat16)


def local(queries, landmarks, labels, tile_mask):
    rows, width = queries.shape
    tile_lands, classes = labels.shape
    scale = 4.0 / math.sqrt(width)
    packed = jnp.concatenate([landmarks, labels], axis=1)
    own = gather_direct(packed, "y", Y).reshape(Y * tile_lands, width + classes)
    other = lax.ppermute(own, "c", [(0, 1), (1, 0)])
    land = jnp.concatenate([own, other], axis=0)

    gathered = gather_direct(queries, ("zl", "zh"), ZL * ZH).reshape(ZL * ZH * rows, width)
    gathered = gather_direct(gathered, "x", X).reshape(SOURCES * rows, width)

    place = lax.axis_index("zl") * X + lax.axis_index("x")
    first = (place * ZH + lax.axis_index("zh")) * (Y * CORE)
    listed = lax.dynamic_slice_in_dim(tile_mask, first, Y * CORE, 1)
    listed = listed.reshape(ZL, X, Y, CORE).transpose(1, 0, 3, 2)
    listed = jnp.where(lax.axis_index("c") == 0, listed, listed[:, :, ::-1])
    listed = listed.reshape(X * ZL, CORE * Y) > 0
    land_f = land[:, :width].astype(jnp.float32)
    half_norm = 0.5 * jnp.sum(land_f * land_f, axis=1)
    bias = jnp.where(
        jnp.repeat(listed, tile_lands, axis=1), -scale * half_norm[None, :], jnp.float32(UNLISTED)
    )

    parts = score(gathered, land, bias, width, ZH * rows, scale)
    parts = lax.all_to_all(parts.reshape(SOURCES, rows, classes + 128), Q_AXES, 0, 0, tiled=True)
    return pl.pallas_call(
        merge_kernel,
        out_shape=jax.ShapeDtypeStruct((rows, classes), jnp.bfloat16),
        in_specs=[pl.BlockSpec(memory_space=pltpu.VMEM)],
        out_specs=pl.BlockSpec(memory_space=pltpu.VMEM),
        name="merge",
    )(parts)


def solution(mesh):
    physical = Mesh(mesh.devices.reshape(ZL, X, ZH, Y, CORE), NAMES)
    split = P(NAMES, None)
    return jax.shard_map(
        local, mesh=physical, in_specs=(split, split, split, P()), out_specs=split, check_vma=False
    )
```

time: 705 us -> 132 us (0.19)
  the two profiles are of different devices: /device:TPU:1 before, /device:TPU:2 now
where the time goes in v1:
time: 132 us; the launch traced here: 131 us
  blocking collectives  68 us (52%)
  waiting for transfers between devices  26.1 us (20%)
  starting transfers between devices  21.9 us (17%)
  Pallas kernels  8.24 us (6%)
  other arithmetic  3.73 us (3%)
  local copies, waits for them, and re-layouts  3.26 us (2%)
    all_to_all x1, blocking collectives, gather_direct(): return lax.all_to_all(copies, axes, 0, 0, tiled=True)  38.4 us
    all_to_all x1, blocking collectives, local(): lax.all_to_all(parts.reshape(SOURCES, rows, classes + 128), Q_AXES, 0, 0,...  29.5 us
    all_to_all x2, waiting for transfers between devices, gather_direct(): return lax.all_to_all(copies, axes, 0, 0, tiled=True)  26.1 us
    all_to_all x2, starting transfers between devices, gather_direct(): return lax.all_to_all(copies, axes, 0, 0, tiled=True)  20 us
    pallas_call x1, Pallas kernels, score(): pl.pallas_call(kernel, out_shape=jax.ShapeDtypeStruct((rows, classes + 12...  6.19 us
  transfers between devices with their start and end apart: 3, of which 2 were waited for; matrix products, arithmetic and copies ran while one was open for 4% of the time, Pallas kernels for 0%

profile of v1, /device:TPU:2, one launch (start us, length us, event | category | flops | bytes accessed | tf_op | source)
XLA Modules:
  0.0 131.3 jit_solution(9508098733024670013)
XLA Ops:
  0.0 0.0 copy-start
  0.0 0.0 copy-start.1
  0.0 1.0 pad_maximum_fusion.1
  1.0 0.1 broadcast_in_dim.38
  1.1 38.4 %all_to_all.20 = bf16[8,64,1152]{2,1,0:T(8,128)(2,1)S(1)} all-to-all(bf16[8,64,1152]{2,1,0:T(8,128)(2,1)S(1)} %broadcast_in_dim.38), channel_id=1, replica_groups=mesh['zl'=6,'x'=4,'zh'=2,'y'=8,'c'=2] {'y'}, dimensions={0} | all-to-all | bytes 2359296 | tf_op jit(solution)/shard_map/all_to_all | solution.py:19
  39.6 0.0 copy-done.1
  39.6 0.8 broadcast_in_dim.35
  40.4 15.2 %all-to-all-start = ((bf16[12,16,1024]{2,1,0:T(8,128)(2,1)}), bf16[12,16,1024]{2,1,0:T(8,128)(2,1)S(1)}, u32[]{:S(2)}, u32[]{:S(2)}) async-start(bf16[12,16,1024]{2,1,0:T(8,128)(2,1)} %broadcast_in_dim.35), calls=%async_computation | async-start | bytes 786432 | tf_op jit(solution)/shard_map/all_to_all | solution.py:19
  55.5 1.9 %collective-permute-start = (bf16[512,1152]{1,0:T(8,128)(2,1)S(1)}, bf16[512,1152]{1,0:T(8,128)(2,1)S(1)}, u32[]{:S(2)}, u32[]{:S(2)}) collective-permute-start(bf16[512,1152]{1,0:T(8,128)(2,1)S(1)} %bitcast.9), channel_id=1, source_target_pairs={{0,1},{1,0},{2,3},{3,2},{4,5},{5,4},{6,7},{7,6},{8,9},{9,8},{10,11... | collective-permute-start | bytes 3538952 | tf_op jit(solution)/shard_map/ppermute | solution.py:101
  57.5 0.0 copy-done
  57.5 0.1 constant_dynamic-slice_fusion
  57.6 0.1 copy.8
  57.6 0.1 reshape.34
  57.7 0.2 copy.9
  57.9 15.3 %all-to-all-done = bf16[12,16,1024]{2,1,0:T(8,128)(2,1)S(1)} async-done(((bf16[12,16,1024]{2,1,0:T(8,128)(2,1)}), bf16[12,16,1024]{2,1,0:T(8,128)(2,1)S(1)}, u32[]{:S(2)}, u32[]{:S(2)}) %all-to-all-start) | async-done | bytes 393248 | tf_op jit(solution)/shard_map/all_to_all | solution.py:19
  73.2 1.4 %broadcast_in_dim.37 = bf16[4,192,1024]{2,1,0:T(8,128)(2,1)} broadcast(bf16[192,1024]{1,0:T(8,128)(2,1)S(1)} %bitcast.12), dimensions={1,2} | broadcast | bytes 1966080 | tf_op jit(solution)/shard_map/broadcast_in_dim | solution.py:18
  74.5 4.8 %all-to-all-start.1 = ((bf16[4,192,1024]{2,1,0:T(8,128)(2,1)}), bf16[4,192,1024]{2,1,0:T(8,128)(2,1)}, u32[]{:S(2)}, u32[]{:S(2)}) async-start(bf16[4,192,1024]{2,1,0:T(8,128)(2,1)} %broadcast_in_dim.37), calls=%async_computation.1 | async-start | bytes 3145728 | tf_op jit(solution)/shard_map/all_to_all | solution.py:19
  79.4 0.1 copy.10
  79.5 0.1 gt.11
  79.6 0.1 copy.11
  79.7 0.1 broadcast_in_dim.39
  79.8 0.1 reshape.35
  80.0 0.0 collective-permute-done
  80.0 0.5 multiply_reduce_fusion
  80.5 0.7 broadcast_select_fusion.refs_2_
  81.1 1.6 %pad_maximum_fusion.refs_1_ = bf16[1024,1152]{1,0:T(8,128)(2,1)} fusion(bf16[512,1152]{1,0:T(8,128)(2,1)S(1)} %collective-permute-done, bf16[512,1152]{1,0:T(8,128)(2,1)S(1)} %bitcast.11), kind=kLoop, calls=%fused_computation.2 | loop fusion | flops 4718592 | bytes 4718592 | tf_op jit(solution)/shard_map/concatenate | solution.py:102
  82.7 10.8 %all-to-all-done.1 = bf16[4,192,1024]{2,1,0:T(8,128)(2,1)} async-done(((bf16[4,192,1024]{2,1,0:T(8,128)(2,1)}), bf16[4,192,1024]{2,1,0:T(8,128)(2,1)}, u32[]{:S(2)}, u32[]{:S(2)}) %all-to-all-start.1) | async-done | bytes 1572896 | tf_op jit(solution)/shard_map/all_to_all | solution.py:19
  93.6 6.2 %score.1 = bf16[768,256]{1,0:T(8,128)(2,1)} custom-call(bf16[768,1024]{1,0:T(8,128)(2,1)} %bitcast.1.refs_0_, bf16[1024,1152]{1,0:T(8,128)(2,1)} %pad_maximum_fusion.refs_1_, f32[3,8,1024]{2,1,0:T(8,128)} %broadcast_select_fusion.refs_2_), custom_call_target="tpu_custom_call" | custom-call | flops 1811939328 | bytes 4325376 | tf_op jit(solution)/shard_map/score/pallas_call | solution.py:70
  99.8 29.5 %all_to_all.21.parts_ref = bf16[48,16,256]{2,1,0:T(8,128)(2,1)} all-to-all(bf16[48,16,256]{2,1,0:T(8,128)(2,1)} %bitcast.13), channel_id=1, replica_groups=mesh['zl'=6,'x'=4,'zh'=2,'y'=8,'c'=2] {'x','zl','zh'}, dimensions={0} | all-to-all | bytes 786432 | tf_op jit(solution)/shard_map/all_to_all | solution.py:120
  129.3 2.0 %merge.1 = bf16[16,128]{1,0:T(8,128)(2,1)} custom-call(bf16[48,16,256]{2,1,0:T(8,128)(2,1)} %all_to_all.21.parts_ref), custom_call_target="tpu_custom_call" | custom-call | tf_op jit(solution)/shard_map/merge/pallas_call | solution.py:121
  (2 shorter events, 0.0 us)
Async XLA Ops:
  0.0 57.5 %copy-start = (s32[24,768]{1,0:T(8,128)S(1)}, s32[24,768]{1,0:T(8,128)}, u32[]{:S(2)}) copy-start(s32[24,768]{1,0:T(8,128)} %param.7) | copy-start | bytes 221188
  0.0 39.6 %copy-start.1 = (bf16[16,1024]{1,0:T(8,128)(2,1)S(1)}, bf16[16,1024]{1,0:T(8,128)(2,1)}, u32[]{:S(2)}) copy-start(bf16[16,1024]{1,0:T(8,128)(2,1)} %param.4) | copy-start | bytes 98308
  40.4 32.8 %all-to-all-start = ((bf16[12,16,1024]{2,1,0:T(8,128)(2,1)}), bf16[12,16,1024]{2,1,0:T(8,128)(2,1)S(1)}, u32[]{:S(2)}, u32[]{:S(2)}) async-start(bf16[12,16,1024]{2,1,0:T(8,128)(2,1)} %broadcast_in_dim.35), calls=%async_computation | async-start | bytes 786432 | tf_op jit(solution)/shard_map/all_to_all | solution.py:19
  55.5 24.4 %collective-permute-start = (bf16[512,1152]{1,0:T(8,128)(2,1)S(1)}, bf16[512,1152]{1,0:T(8,128)(2,1)S(1)}, u32[]{:S(2)}, u32[]{:S(2)}) collective-permute-start(bf16[512,1152]{1,0:T(8,128)(2,1)S(1)} %bitcast.9), channel_id=1, source_target_pairs={{0,1},{1,0},{2,3},{3,2},{4,5},{5,4},{6,7},{7,6},{8,9},{9,8},{10,11... | collective-permute-start | bytes 3538952 | tf_op jit(solution)/shard_map/ppermute | solution.py:101
  74.5 19.1 %all-to-all-start.1 = ((bf16[4,192,1024]{2,1,0:T(8,128)(2,1)}), bf16[4,192,1024]{2,1,0:T(8,128)(2,1)}, u32[]{:S(2)}, u32[]{:S(2)}) async-start(bf16[4,192,1024]{2,1,0:T(8,128)(2,1)} %broadcast_in_dim.37), calls=%async_computation.1 | async-start | bytes 3145728 | tf_op jit(solution)/shard_map/all_to_all | solution.py:19

commit v2 on v1

v2 whole, which is shorter than its diff:
```python
import math

import jax
import jax.numpy as jnp
from jax import lax
from jax.experimental import pallas as pl
from jax.experimental.pallas import tpu as pltpu
from jax.sharding import Mesh, PartitionSpec as P


ZL, X, ZH, Y, CORE = 6, 4, 2, 8, 2
NAMES = ("zl", "x", "zh", "y", "c")
Z_AXES = ("zl", "zh")
Z = ZL * ZH
UNLISTED = -1e30
LANES = 128
VMEM = pl.BlockSpec(memory_space=pltpu.VMEM)


def gather_direct(value, axes, count):
    copies = jnp.broadcast_to(value[None], (count,) + value.shape)
    gathered = lax.all_to_all(copies, axes, 0, 0, tiled=True)
    return gathered.reshape((count * value.shape[0],) + value.shape[1:])


def gather_by_permutes(value, axis, count):
    blocks = [value]
    for steps in range(1, count):
        pairs = [(source, (source + steps) % count) for source in range(count)]
        blocks.append(lax.ppermute(value, axis, pairs))
    return jnp.concatenate(blocks, axis=0)


def split3(value):
    high = value.astype(jnp.bfloat16)
    rest = value - high.astype(jnp.float32)
    middle = rest.astype(jnp.bfloat16)
    low = (rest - middle.astype(jnp.float32)).astype(jnp.bfloat16)
    return high, middle, low


def pack_stats(row_max, weight_sum, rows):
    lane = lax.broadcasted_iota(jnp.int32, (rows, LANES), 1)
    stats = jnp.zeros((rows, LANES), jnp.float32)
    for place, piece in enumerate(split3(row_max) + split3(weight_sum)):
        stats = jnp.where(lane == place, piece.astype(jnp.float32), stats)
    return stats.astype(jnp.bfloat16)


def score_kernel(queries_ref, own_ref, other_ref, bias_ref, out_ref, *, width, tile_rows, scale):
    rows = queries_ref.shape[0]
    lands = own_ref.shape[0]
    tiles = bias_ref.shape[1]
    chunk = tiles * tile_rows

    def step(index):
        start = pl.multiple_of(index * chunk, chunk)
        queries = queries_ref[pl.ds(start, chunk), :]
        bias = bias_ref[index]

        def logits_of(land_ref, first):
            logits = lax.dot_general(
                queries,
                land_ref[:, :width],
                (((1,), (1,)), ((), ())),
                preferred_element_type=jnp.float32,
            )
            logits = (logits * scale).reshape(tiles, tile_rows, lands)
            return (logits + bias[:, None, first : first + lands]).reshape(chunk, lands)

        own = logits_of(own_ref, 0)
        other = logits_of(other_ref, lands)
        row_max = jnp.max(jnp.maximum(own, other), axis=1, keepdims=True)
        own = jnp.exp(own - row_max)
        other = jnp.exp(other - row_max)
        weight_sum = jnp.sum(own + other, axis=1, keepdims=True)
        label_sum = jnp.dot(
            own.astype(jnp.bfloat16), own_ref[:, width:], preferred_element_type=jnp.float32
        ) + jnp.dot(
            other.astype(jnp.bfloat16), other_ref[:, width:], preferred_element_type=jnp.float32
        )
        out_ref[pl.ds(start, chunk), :LANES] = (label_sum / weight_sum).astype(jnp.bfloat16)
        out_ref[pl.ds(start, chunk), LANES:] = pack_stats(row_max, weight_sum, chunk)

    pl.loop(0, rows // chunk)(step)


def score(queries, own, other, bias, width, tile_rows, scale):
    rows = queries.shape[0]
    lands = own.shape[0] + other.shape[0]
    classes = own.shape[1] - width
    tiles = 8
    return pl.pallas_call(
        lambda *refs: score_kernel(*refs, width=width, tile_rows=tile_rows, scale=scale),
        out_shape=jax.ShapeDtypeStruct((rows, classes + LANES), jnp.bfloat16),
        in_specs=[VMEM] * 4,
        out_specs=VMEM,
        cost_estimate=pl.CostEstimate(
            flops=2 * rows * lands * (width + classes),
            bytes_accessed=2 * (rows * width + lands * (width + classes) + rows * 256),
            transcendentals=rows * lands,
        ),
        compiler_params=pltpu.CompilerParams(vmem_limit_bytes=24 << 20),
        name="score",
    )(queries, own, other, bias.reshape(rows // (tiles * tile_rows), tiles, lands))


def merge_kernel(parts_ref, out_ref):
    sources, rows, _ = parts_ref.shape
    piece = lax.broadcasted_iota(jnp.int32, (LANES, 2 * LANES), 0)
    lane = lax.broadcasted_iota(jnp.int32, (LANES, 2 * LANES), 1)
    first = jnp.where(lane < LANES, 0, 3)
    spread = jnp.where((piece >= first) & (piece < first + 3), 1.0, 0.0).astype(jnp.bfloat16)
    stats = [
        jnp.dot(parts_ref[source, :, LANES:], spread, preferred_element_type=jnp.float32)
        for source in range(sources)
    ]
    joint = stats[0][:, :LANES]
    for stat in stats[1:]:
        joint = jnp.maximum(joint, stat[:, :LANES])
    total = jnp.zeros((rows, LANES), jnp.float32)
    labels = jnp.zeros((rows, LANES), jnp.float32)
    for source, stat in enumerate(stats):
        weight = stat[:, LANES:] * jnp.exp(stat[:, :LANES] - joint)
        total = total + weight
        labels = labels + parts_ref[source, :, :LANES].astype(jnp.float32) * weight
    out_ref[:, :LANES] = (labels / total).astype(jnp.bfloat16)
    if out_ref.shape[1] > LANES:
        out_ref[:, LANES:] = pack_stats(joint, total, rows)


def merge(parts, width):
    return pl.pallas_call(
        merge_kernel,
        out_shape=jax.ShapeDtypeStruct((parts.shape[1], width), jnp.bfloat16),
        in_specs=[VMEM],
        out_specs=VMEM,
        compiler_params=pltpu.CompilerParams(vmem_limit_bytes=8 << 20),
        name="merge",
    )(parts)


def local(queries, landmarks, labels, tile_mask):
    rows, width = queries.shape
    tile_lands, classes = labels.shape
    scale = 4.0 / math.sqrt(width)
    gathered = gather_direct(queries, Z_AXES, Z)
    packed = jnp.concatenate([landmarks, labels], axis=1)
    own = gather_by_permutes(packed, "y", Y)
    other = lax.ppermute(own, "c", [(0, 1), (1, 0)])
    gathered = gather_direct(gathered, "x", X)

    place = lax.axis_index("zl") * X + lax.axis_index("x")
    first = (place * ZH + lax.axis_index("zh")) * (Y * CORE)
    steps = jnp.arange(Y, dtype=jnp.int32)
    behind = (lax.axis_index("y") - steps) % Y
    wanted = lax.axis_index("c") ^ jnp.arange(CORE, dtype=jnp.int32)
    tiles = (behind[None, :] * CORE + wanted[:, None]).reshape(1, CORE * Y)
    pick = tiles == lax.broadcasted_iota(jnp.int32, (Y * CORE, 1), 0)
    listed = lax.dynamic_slice_in_dim(tile_mask, first, Y * CORE, 1).astype(jnp.float32)
    listed = listed.reshape(ZL, X, Y * CORE).transpose(1, 0, 2).reshape(X * ZL, Y * CORE)
    pick = jnp.repeat(pick.astype(jnp.float32), tile_lands, axis=1)
    listed = jnp.dot(listed, pick, preferred_element_type=jnp.float32) > 0.5

    def half_norm(land):
        land_f = land[:, :width].astype(jnp.float32)
        return 0.5 * jnp.sum(land_f * land_f, axis=1)

    norms = jnp.concatenate([half_norm(own), half_norm(other)])
    bias = jnp.where(listed, -scale * norms[None, :], jnp.float32(UNLISTED))

    parts = score(gathered, own, other, bias, width, ZH * rows, scale)
    parts = lax.all_to_all(parts.reshape(X, Z * rows, classes + LANES), "x", 0, 0, tiled=True)
    parts = merge(parts, classes + LANES)
    parts = lax.all_to_all(parts.reshape(Z, rows, classes + LANES), Z_AXES, 0, 0, tiled=True)
    return merge(parts, classes)


def solution(mesh):
    physical = Mesh(mesh.devices.reshape(ZL, X, ZH, Y, CORE), NAMES)
    split = P(NAMES, None)

    return jax.shard_map(
        local, mesh=physical, in_specs=(split, split, split, P()), out_specs=split, check_vma=False
    )
```

time: 132 us -> 119 us (0.902)
  the two profiles are of different devices: /device:TPU:2 before, /device:TPU:1 now
where the time goes in v2:
time: 119 us; the launch traced here: 117 us
  starting transfers between devices  51.5 us (43%)
  blocking collectives  29.4 us (25%)
  waiting for transfers between devices  22.5 us (19%)
  Pallas kernels  5.74 us (5%)
  local copies, waits for them, and re-layouts  5 us (4%)
  other arithmetic  2.69 us (2%)
    ppermute x7, starting transfers between devices, gather_by_permutes(): blocks.append(lax.ppermute(value, axis, pairs))  29.2 us
    all_to_all x1, blocking collectives, local(): lax.all_to_all(parts.reshape(Z, rows, classes + LANES), Z_AXES, 0, 0, til...  20.8 us
    all_to_all x2, starting transfers between devices, gather_direct(): gathered = lax.all_to_all(copies, axes, 0, 0, tiled=True)  18.9 us
    all_to_all x2, waiting for transfers between devices, gather_direct(): gathered = lax.all_to_all(copies, axes, 0, 0, tiled=True)  16.7 us
    all_to_all x1, blocking collectives, local(): lax.all_to_all(parts.reshape(X, Z * rows, classes + LANES), 'x', 0, 0, ti...  8.62 us
    ppermute x7, waiting for transfers between devices, gather_by_permutes(): blocks.append(lax.ppermute(value, axis, pairs))  5.77 us
    pallas_call x1, Pallas kernels, score(): pl.pallas_call(lambda *refs: score_kernel(*refs, width=width, tile_rows=t...  4.59 us
    ppermute x1, starting transfers between devices, local(): other = lax.ppermute(own, 'c', [(0, 1), (1, 0)])  3.34 us
  transfers between devices with their start and end apart: 10, of which 3 were waited for; matrix products, arithmetic and copies ran while one was open for 5% of the time, Pallas kernels for 0%

profile of v2, /device:TPU:1, one launch (start us, length us, event | category | flops | bytes accessed | tf_op | source)
XLA Modules:
  0.0 117.1 jit_solution(13424549437226810112)
XLA Ops:
  0.0 0.9 constant_dynamic-update-slice_fusion.1
  0.9 0.7 constant_dynamic-update-slice_fusion
  1.7 4.0 %collective-permute-start = (bf16[64,1152]{1,0:T(8,128)(2,1)S(1)}, bf16[64,1152]{1,0:T(8,128)(2,1)S(1)}, u32[]{:S(2)}, u32[]{:S(2)}) collective-permute-start(bf16[64,1152]{1,0:T(8,128)(2,1)S(1)} %get-tuple-element.7), channel_id=1, source_target_pairs={{0,2},{2,4},{4,6},{6,8},{8,10},{10,12},{12,14},{14,0},{1,3},{3,5},... | collective-permute-start | bytes 442376 | tf_op jit(solution)/shard_map/ppermute | solution.py:30
  5.7 4.2 %collective-permute-start.1 = (bf16[64,1152]{1,0:T(8,128)(2,1)S(1)}, bf16[64,1152]{1,0:T(8,128)(2,1)S(1)}, u32[]{:S(2)}, u32[]{:S(2)}) collective-permute-start(bf16[64,1152]{1,0:T(8,128)(2,1)S(1)} %get-tuple-element.7), channel_id=1, source_target_pairs={{0,4},{2,6},{4,8},{6,10},{8,12},{10,14},{12,0},{14,2},{1,5},{3,7},... | collective-permute-start | bytes 442376 | tf_op jit(solution)/shard_map/ppermute | solution.py:30
  9.9 4.6 %collective-permute-start.2 = (bf16[64,1152]{1,0:T(8,128)(2,1)S(1)}, bf16[64,1152]{1,0:T(8,128)(2,1)S(1)}, u32[]{:S(2)}, u32[]{:S(2)}) collective-permute-start(bf16[64,1152]{1,0:T(8,128)(2,1)S(1)} %get-tuple-element.7), channel_id=1, source_target_pairs={{0,6},{2,8},{4,10},{6,12},{8,14},{10,0},{12,2},{14,4},{1,7},{3,9},... | collective-permute-start | bytes 442376 | tf_op jit(solution)/shard_map/ppermute | solution.py:30
  14.6 3.5 %collective-permute-start.3 = (bf16[64,1152]{1,0:T(8,128)(2,1)S(1)}, bf16[64,1152]{1,0:T(8,128)(2,1)S(1)}, u32[]{:S(2)}, u32[]{:S(2)}) collective-permute-start(bf16[64,1152]{1,0:T(8,128)(2,1)S(1)} %get-tuple-element.7), channel_id=1, source_target_pairs={{0,8},{2,10},{4,12},{6,14},{8,0},{10,2},{12,4},{14,6},{1,9},{3,11}... | collective-permute-start | bytes 442376 | tf_op jit(solution)/shard_map/ppermute | solution.py:30
  18.1 4.9 %collective-permute-start.4 = (bf16[64,1152]{1,0:T(8,128)(2,1)S(1)}, bf16[64,1152]{1,0:T(8,128)(2,1)S(1)}, u32[]{:S(2)}, u32[]{:S(2)}) collective-permute-start(bf16[64,1152]{1,0:T(8,128)(2,1)S(1)} %get-tuple-element.7), channel_id=1, source_target_pairs={{0,10},{2,12},{4,14},{6,0},{8,2},{10,4},{12,6},{14,8},{1,11},{3,13... | collective-permute-start | bytes 442376 | tf_op jit(solution)/shard_map/ppermute | solution.py:30
  23.0 1.5 %broadcast_in_dim.31 = bf16[12,16,1024]{2,1,0:T(8,128)(2,1)} broadcast(bf16[16,1024]{1,0:T(8,128)(2,1)} %param.4), dimensions={1,2} | broadcast | bytes 425984 | tf_op jit(solution)/shard_map/broadcast_in_dim | solution.py:21
  24.5 14.9 %all-to-all-start = ((bf16[12,16,1024]{2,1,0:T(8,128)(2,1)}), bf16[12,16,1024]{2,1,0:T(8,128)(2,1)S(1)}, u32[]{:S(2)}, u32[]{:S(2)}) async-start(bf16[12,16,1024]{2,1,0:T(8,128)(2,1)} %broadcast_in_dim.31), calls=%async_computation | async-start | bytes 786432 | tf_op jit(solution)/shard_map/all_to_all | solution.py:22
  39.4 0.0 collective-permute-done
  39.4 5.0 %collective-permute-start.5 = (bf16[64,1152]{1,0:T(8,128)(2,1)S(1)}, bf16[64,1152]{1,0:T(8,128)(2,1)S(1)}, u32[]{:S(2)}, u32[]{:S(2)}) collective-permute-start(bf16[64,1152]{1,0:T(8,128)(2,1)S(1)} %get-tuple-element.7), channel_id=1, source_target_pairs={{0,12},{2,14},{4,0},{6,2},{8,4},{10,6},{12,8},{14,10},{1,13},{3,15... | collective-permute-start | bytes 442376 | tf_op jit(solution)/shard_map/ppermute | solution.py:30
  44.4 0.0 collective-permute-done.1
  44.5 3.0 %collective-permute-start.6 = (bf16[64,1152]{1,0:T(8,128)(2,1)S(1)}, bf16[64,1152]{1,0:T(8,128)(2,1)S(1)}, u32[]{:S(2)}, u32[]{:S(2)}) collective-permute-start(bf16[64,1152]{1,0:T(8,128)(2,1)S(1)} %get-tuple-element.7), channel_id=1, source_target_pairs={{0,14},{2,0},{4,2},{6,4},{8,6},{10,8},{12,10},{14,12},{1,15},{3,1}... | collective-permute-start | bytes 442376 | tf_op jit(solution)/shard_map/ppermute | solution.py:30
  47.5 0.0 collective-permute-done.2
  47.5 0.0 collective-permute-done.3
  47.5 0.0 collective-permute-done.4
  47.6 1.0 collective-permute-done.5
  48.6 4.8 %collective-permute-done.6 = bf16[64,1152]{1,0:T(8,128)(2,1)S(1)} collective-permute-done((bf16[64,1152]{1,0:T(8,128)(2,1)S(1)}, bf16[64,1152]{1,0:T(8,128)(2,1)S(1)}, u32[]{:S(2)}, u32[]{:S(2)}) %collective-permute-start.6) | collective-permute-done | bytes 147488 | tf_op jit(solution)/shard_map/ppermute | solution.py:30
  53.4 3.3 %collective-permute-start.7 = (bf16[512,1152]{1,0:T(8,128)(2,1)S(1)}, bf16[512,1152]{1,0:T(8,128)(2,1)}, u32[]{:S(2)}, u32[]{:S(2)}) collective-permute-start(bf16[512,1152]{1,0:T(8,128)(2,1)S(1)} %constant_dynamic-update-slice_fusion.2.refs_1_), channel_id=1, source_target_pairs={{0,1},{1,0},{2,3},{3,2},{4,5},{5,4},{6,7},{7,6},{8,9},{9,8},{10,11... | collective-permute-start | bytes 3538952 | tf_op jit(solution)/shard_map/ppermute | solution.py:150
  56.7 0.8 dynamic-slice_convert_fusion
  57.6 0.1 broadcast_add_fusion
  57.6 0.1 add.46
  57.7 0.0 all-to-all-done
  57.7 1.3 %broadcast_in_dim.33 = bf16[4,192,1024]{2,1,0:T(8,128)(2,1)} broadcast(bf16[192,1024]{1,0:T(8,128)(2,1)S(1)} %bitcast.15), dimensions={1,2} | broadcast | bytes 1966080 | tf_op jit(solution)/shard_map/broadcast_in_dim | solution.py:21
  59.1 4.0 %all-to-all-start.1 = ((bf16[4,192,1024]{2,1,0:T(8,128)(2,1)}), bf16[4,192,1024]{2,1,0:T(8,128)(2,1)S(1)}, u32[]{:S(2)}, u32[]{:S(2)}) async-start(bf16[4,192,1024]{2,1,0:T(8,128)(2,1)} %broadcast_in_dim.33), calls=%async_computation.1 | async-start | bytes 3145728 | tf_op jit(solution)/shard_map/all_to_all | solution.py:22
  63.1 0.1 broadcast_in_dim.34
  63.2 0.1 reshape.76
  63.3 0.3 multiply_reduce_fusion.1
  63.6 0.0 collective-permute-done.7.refs_2_
  63.6 1.5 %multiply_reduce_fusion = f32[512]{0:T(512)S(1)} fusion(bf16[512,1152]{1,0:T(8,128)(2,1)} %collective-permute-done.7.refs_2_), kind=kLoop, calls=%fused_computation | loop fusion | flops 1572352 | bytes 1050624 | tf_op jit(solution)/shard_map/reduce_sum | solution.py:167
  65.1 0.1 fusion.1.refs_3_
  65.3 16.7 %all-to-all-done.1 = bf16[4,192,1024]{2,1,0:T(8,128)(2,1)S(1)} async-done(((bf16[4,192,1024]{2,1,0:T(8,128)(2,1)}), bf16[4,192,1024]{2,1,0:T(8,128)(2,1)S(1)}, u32[]{:S(2)}, u32[]{:S(2)}) %all-to-all-start.1) | async-done | bytes 1572896 | tf_op jit(solution)/shard_map/all_to_all | solution.py:22
  82.0 4.6 %score.1 = bf16[768,256]{1,0:T(8,128)(2,1)S(1)} custom-call(bf16[768,1024]{1,0:T(8,128)(2,1)S(1)} %bitcast.12, bf16[512,1152]{1,0:T(8,128)(2,1)S(1)} %constant_dynamic-update-slice_fusion.2.refs_1_, bf16[512,1152]{1,0:T(8,128)(2,1)} %collective-permute-done.7.refs_2_, f32[3,8,1024]{2,1,0:T(8,128)S(1)} %fusion.1.refs_3_), custom_call_target="tpu_custom_call" | custom-call | flops 1811939328 | bytes 4325376 | tf_op jit(solution)/shard_map/score/pallas_call | solution.py:93
  86.6 8.6 %all_to_all.20.parts_ref = bf16[4,192,256]{2,1,0:T(8,128)(2,1)S(1)} all-to-all(bf16[4,192,256]{2,1,0:T(8,128)(2,1)S(1)} %bitcast.13), channel_id=1, replica_groups=mesh['zl'=6,'x'=4,'zh'=2,'y'=8,'c'=2] {'x'}, dimensions={0} | all-to-all | bytes 786432 | tf_op jit(solution)/shard_map/all_to_all | solution.py:173
  95.2 0.4 merge.2
  95.6 20.8 %all_to_all.21.parts_ref = bf16[12,16,256]{2,1,0:T(8,128)(2,1)S(1)} all-to-all(bf16[12,16,256]{2,1,0:T(8,128)(2,1)S(1)} %bitcast.14), channel_id=1, replica_groups=mesh['zl'=6,'x'=4,'zh'=2,'y'=8,'c'=2] {'zl','zh'}, dimensions={0} | all-to-all | bytes 196608 | tf_op jit(solution)/shard_map/all_to_all | solution.py:175
  116.3 0.8 merge.3
  (15 shorter events, 0.2 us)
Async XLA Ops:
  1.7 37.8 %collective-permute-start = (bf16[64,1152]{1,0:T(8,128)(2,1)S(1)}, bf16[64,1152]{1,0:T(8,128)(2,1)S(1)}, u32[]{:S(2)}, u32[]{:S(2)}) collective-permute-start(bf16[64,1152]{1,0:T(8,128)(2,1)S(1)} %get-tuple-element.7), channel_id=1, source_target_pairs={{0,2},{2,4},{4,6},{6,8},{8,10},{10,12},{12,14},{14,0},{1,3},{3,5},... | collective-permute-start | bytes 442376 | tf_op jit(solution)/shard_map/ppermute | solution.py:30
  5.7 38.8 %collective-permute-start.1 = (bf16[64,1152]{1,0:T(8,128)(2,1)S(1)}, bf16[64,1152]{1,0:T(8,128)(2,1)S(1)}, u32[]{:S(2)}, u32[]{:S(2)}) collective-permute-start(bf16[64,1152]{1,0:T(8,128)(2,1)S(1)} %get-tuple-element.7), channel_id=1, source_target_pairs={{0,4},{2,6},{4,8},{6,10},{8,12},{10,14},{12,0},{14,2},{1,5},{3,7},... | collective-permute-start | bytes 442376 | tf_op jit(solution)/shard_map/ppermute | solution.py:30
  9.9 37.6 %collective-permute-start.2 = (bf16[64,1152]{1,0:T(8,128)(2,1)S(1)}, bf16[64,1152]{1,0:T(8,128)(2,1)S(1)}, u32[]{:S(2)}, u32[]{:S(2)}) collective-permute-start(bf16[64,1152]{1,0:T(8,128)(2,1)S(1)} %get-tuple-element.7), channel_id=1, source_target_pairs={{0,6},{2,8},{4,10},{6,12},{8,14},{10,0},{12,2},{14,4},{1,7},{3,9},... | collective-permute-start | bytes 442376 | tf_op jit(solution)/shard_map/ppermute | solution.py:30
  14.6 32.9 %collective-permute-start.3 = (bf16[64,1152]{1,0:T(8,128)(2,1)S(1)}, bf16[64,1152]{1,0:T(8,128)(2,1)S(1)}, u32[]{:S(2)}, u32[]{:S(2)}) collective-permute-start(bf16[64,1152]{1,0:T(8,128)(2,1)S(1)} %get-tuple-element.7), channel_id=1, source_target_pairs={{0,8},{2,10},{4,12},{6,14},{8,0},{10,2},{12,4},{14,6},{1,9},{3,11}... | collective-permute-start | bytes 442376 | tf_op jit(solution)/shard_map/ppermute | solution.py:30
  18.1 29.4 %collective-permute-start.4 = (bf16[64,1152]{1,0:T(8,128)(2,1)S(1)}, bf16[64,1152]{1,0:T(8,128)(2,1)S(1)}, u32[]{:S(2)}, u32[]{:S(2)}) collective-permute-start(bf16[64,1152]{1,0:T(8,128)(2,1)S(1)} %get-tuple-element.7), channel_id=1, source_target_pairs={{0,10},{2,12},{4,14},{6,0},{8,2},{10,4},{12,6},{14,8},{1,11},{3,13... | collective-permute-start | bytes 442376 | tf_op jit(solution)/shard_map/ppermute | solution.py:30
  24.5 33.2 %all-to-all-start = ((bf16[12,16,1024]{2,1,0:T(8,128)(2,1)}), bf16[12,16,1024]{2,1,0:T(8,128)(2,1)S(1)}, u32[]{:S(2)}, u32[]{:S(2)}) async-start(bf16[12,16,1024]{2,1,0:T(8,128)(2,1)} %broadcast_in_dim.31), calls=%async_computation | async-start | bytes 786432 | tf_op jit(solution)/shard_map/all_to_all | solution.py:22
  39.4 9.1 %collective-permute-start.5 = (bf16[64,1152]{1,0:T(8,128)(2,1)S(1)}, bf16[64,1152]{1,0:T(8,128)(2,1)S(1)}, u32[]{:S(2)}, u32[]{:S(2)}) collective-permute-start(bf16[64,1152]{1,0:T(8,128)(2,1)S(1)} %get-tuple-element.7), channel_id=1, source_target_pairs={{0,12},{2,14},{4,0},{6,2},{8,4},{10,6},{12,8},{14,10},{1,13},{3,15... | collective-permute-start | bytes 442376 | tf_op jit(solution)/shard_map/ppermute | solution.py:30
  44.5 8.9 %collective-permute-start.6 = (bf16[64,1152]{1,0:T(8,128)(2,1)S(1)}, bf16[64,1152]{1,0:T(8,128)(2,1)S(1)}, u32[]{:S(2)}, u32[]{:S(2)}) collective-permute-start(bf16[64,1152]{1,0:T(8,128)(2,1)S(1)} %get-tuple-element.7), channel_id=1, source_target_pairs={{0,14},{2,0},{4,2},{6,4},{8,6},{10,8},{12,10},{14,12},{1,15},{3,1}... | collective-permute-start | bytes 442376 | tf_op jit(solution)/shard_map/ppermute | solution.py:30
  53.4 10.2 %collective-permute-start.7 = (bf16[512,1152]{1,0:T(8,128)(2,1)S(1)}, bf16[512,1152]{1,0:T(8,128)(2,1)}, u32[]{:S(2)}, u32[]{:S(2)}) collective-permute-start(bf16[512,1152]{1,0:T(8,128)(2,1)S(1)} %constant_dynamic-update-slice_fusion.2.refs_1_), channel_id=1, source_target_pairs={{0,1},{1,0},{2,3},{3,2},{4,5},{5,4},{6,7},{7,6},{8,9},{9,8},{10,11... | collective-permute-start | bytes 3538952 | tf_op jit(solution)/shard_map/ppermute | solution.py:150
  59.1 22.9 %all-to-all-start.1 = ((bf16[4,192,1024]{2,1,0:T(8,128)(2,1)}), bf16[4,192,1024]{2,1,0:T(8,128)(2,1)S(1)}, u32[]{:S(2)}, u32[]{:S(2)}) async-start(bf16[4,192,1024]{2,1,0:T(8,128)(2,1)} %broadcast_in_dim.33), calls=%async_computation.1 | async-start | bytes 3145728 | tf_op jit(solution)/shard_map/all_to_all | solution.py:22

commit v3 on v2

--- a/solution.py
+++ b/solution.py
@@ -23,12 +23,29 @@
     return gathered.reshape((count * value.shape[0],) + value.shape[1:])
 
 
-def gather_by_permutes(value, axis, count):
-    blocks = [value]
-    for steps in range(1, count):
-        pairs = [(source, (source + steps) % count) for source in range(count)]
-        blocks.append(lax.ppermute(value, axis, pairs))
-    return jnp.concatenate(blocks, axis=0)
+def both_ways(value, steps):
+    pairs = [
+        (y * CORE + core, (y + (steps if core == 0 else -steps)) % Y * CORE + core)
+        for y in range(Y)
+        for core in range(CORE)
+    ]
+    return lax.ppermute(value, ("y", "c"), pairs)
+
+
+def swap_cores(value):
+    return lax.ppermute(value, "c", [(0, 1), (1, 0)])
+
+
+def tiles_held():
+    y, core = lax.axis_index("y"), lax.axis_index("c")
+    steps = jnp.array([0, 1, 1, 2, 2, 3, 3, 4], jnp.int32)
+    flip = jnp.array([0, 0, 1, 0, 1, 0, 1, 0], jnp.int32)
+
+    def of(core):
+        behind = jnp.where(core == 0, -steps, steps)
+        return (y + behind) % Y * CORE + (core ^ flip)
+
+    return jnp.concatenate([of(core), of(1 - core)])
 
 
 def split3(value):
@@ -144,20 +161,19 @@
     rows, width = queries.shape
     tile_lands, classes = labels.shape
     scale = 4.0 / math.sqrt(width)
+    mine = jnp.concatenate([landmarks, labels], axis=1)
+    pair = jnp.concatenate([mine, swap_cores(mine)], axis=0)
     gathered = gather_direct(queries, Z_AXES, Z)
-    packed = jnp.concatenate([landmarks, labels], axis=1)
-    own = gather_by_permutes(packed, "y", Y)
-    other = lax.ppermute(own, "c", [(0, 1), (1, 0)])
+    third, fourth, second = both_ways(pair, 3), both_ways(mine, 4), both_ways(pair, 2)
+    first = both_ways(pair, 1)
+    own = jnp.concatenate([mine, first, second, third, fourth], axis=0)
+    other = swap_cores(own)
     gathered = gather_direct(gathered, "x", X)
 
     place = lax.axis_index("zl") * X + lax.axis_index("x")
-    first = (place * ZH + lax.axis_index("zh")) * (Y * CORE)
-    steps = jnp.arange(Y, dtype=jnp.int32)
-    behind = (lax.axis_index("y") - steps) % Y
-    wanted = lax.axis_index("c") ^ jnp.arange(CORE, dtype=jnp.int32)
-    tiles = (behind[None, :] * CORE + wanted[:, None]).reshape(1, CORE * Y)
-    pick = tiles == lax.broadcasted_iota(jnp.int32, (Y * CORE, 1), 0)
-    listed = lax.dynamic_slice_in_dim(tile_mask, first, Y * CORE, 1).astype(jnp.float32)
+    start = (place * ZH + lax.axis_index("zh")) * (Y * CORE)
+    pick = tiles_held()[None, :] == lax.broadcasted_iota(jnp.int32, (Y * CORE, 1), 0)
+    listed = lax.dynamic_slice_in_dim(tile_mask, start, Y * CORE, 1).astype(jnp.float32)
     listed = listed.reshape(ZL, X, Y * CORE).transpose(1, 0, 2).reshape(X * ZL, Y * CORE)
     pick = jnp.repeat(pick.astype(jnp.float32), tile_lands, axis=1)
     listed = jnp.dot(listed, pick, preferred_element_type=jnp.float32) > 0.5

time: 119 us -> 119 us (level)
  the two profiles are of different devices: /device:TPU:1 before, /device:TPU:48 now
where the time goes in v3:
time: 119 us; the launch traced here: 118 us
  starting transfers between devices  37.7 us (32%)
  waiting for transfers between devices  36.2 us (30%)
  blocking collectives  30.4 us (26%)
  Pallas kernels  5.74 us (5%)
  local copies, waits for them, and re-layouts  4.93 us (4%)
  other arithmetic  2.72 us (2%)
    all_to_all x1, blocking collectives, local(): lax.all_to_all(parts.reshape(Z, rows, classes + LANES), Z_AXES, 0, 0, til...  20.1 us
    all_to_all x2, waiting for transfers between devices, gather_direct(): gathered = lax.all_to_all(copies, axes, 0, 0, tiled=True)  19.2 us
    all_to_all x2, starting transfers between devices, gather_direct(): gathered = lax.all_to_all(copies, axes, 0, 0, tiled=True)  16.9 us
    ppermute x4, starting transfers between devices, both_ways(): return lax.ppermute(value, ('y', 'c'), pairs)  16.9 us
    ppermute x4, waiting for transfers between devices, both_ways(): return lax.ppermute(value, ('y', 'c'), pairs)  15.7 us
    all_to_all x1, blocking collectives, local(): lax.all_to_all(parts.reshape(X, Z * rows, classes + LANES), 'x', 0, 0, ti...  10.3 us
    pallas_call x1, Pallas kernels, score(): pl.pallas_call(lambda *refs: score_kernel(*refs, width=width, tile_rows=t...  4.6 us
    ppermute x2, starting transfers between devices, swap_cores(): return lax.ppermute(value, 'c', [(0, 1), (1, 0)])  3.84 us
  transfers between devices with their start and end apart: 8, of which 3 were waited for; matrix products, arithmetic and copies ran while one was open for 5% of the time, Pallas kernels for 0%

profile of v3, /device:TPU:48, one launch (start us, length us, event | category | flops | bytes accessed | tf_op | source)
XLA Modules:
  0.0 118.0 jit_solution(10213172890938449457)
XLA Ops:
  0.0 0.9 constant_dynamic-update-slice_fusion.1
  0.9 0.7 constant_dynamic-update-slice_fusion
  1.7 1.9 %collective-permute-start = (bf16[64,1152]{1,0:T(8,128)(2,1)S(1)}, bf16[64,1152]{1,0:T(8,128)(2,1)S(1)}, u32[]{:S(2)}, u32[]{:S(2)}) collective-permute-start(bf16[64,1152]{1,0:T(8,128)(2,1)S(1)} %get-tuple-element.7), channel_id=1, source_target_pairs={{0,1},{1,0},{2,3},{3,2},{4,5},{5,4},{6,7},{7,6},{8,9},{9,8},{10,11... | collective-permute-start | bytes 442376 | tf_op jit(solution)/shard_map/ppermute | solution.py:36
  3.6 1.3 %collective-permute-done = bf16[64,1152]{1,0:T(8,128)(2,1)S(1)} collective-permute-done((bf16[64,1152]{1,0:T(8,128)(2,1)S(1)}, bf16[64,1152]{1,0:T(8,128)(2,1)S(1)}, u32[]{:S(2)}, u32[]{:S(2)}) %collective-permute-start) | collective-permute-done | bytes 147488 | tf_op jit(solution)/shard_map/ppermute | solution.py:36
  5.0 2.6 %collective-permute-start.1 = (bf16[128,1152]{1,0:T(8,128)(2,1)S(1)}, bf16[128,1152]{1,0:T(8,128)(2,1)S(1)}, u32[]{:S(2)}, u32[]{:S(2)}) collective-permute-start(bf16[128,1152]{1,0:T(8,128)(2,1)S(1)} %pad_maximum_fusion), channel_id=1, source_target_pairs={{0,2},{1,15},{2,4},{3,1},{4,6},{5,3},{6,8},{7,5},{8,10},{9,7},{10,... | collective-permute-start | bytes 884744 | tf_op jit(solution)/shard_map/ppermute | solution.py:32
  7.5 10.1 %collective-permute-start.2 = (bf16[128,1152]{1,0:T(8,128)(2,1)S(1)}, bf16[128,1152]{1,0:T(8,128)(2,1)S(1)}, u32[]{:S(2)}, u32[]{:S(2)}) collective-permute-start(bf16[128,1152]{1,0:T(8,128)(2,1)S(1)} %pad_maximum_fusion), channel_id=1, source_target_pairs={{0,4},{1,13},{2,6},{3,15},{4,8},{5,1},{6,10},{7,3},{8,12},{9,5},{1... | collective-permute-start | bytes 884744 | tf_op jit(solution)/shard_map/ppermute | solution.py:32
  17.7 1.9 %collective-permute-start.4 = (bf16[64,1152]{1,0:T(8,128)(2,1)S(1)}, bf16[64,1152]{1,0:T(8,128)(2,1)S(1)}, u32[]{:S(2)}, u32[]{:S(2)}) collective-permute-start(bf16[64,1152]{1,0:T(8,128)(2,1)S(1)} %get-tuple-element.7), channel_id=1, source_target_pairs={{0,8},{1,9},{2,10},{3,11},{4,12},{5,13},{6,14},{7,15},{8,0},{9,1},... | collective-permute-start | bytes 442376 | tf_op jit(solution)/shard_map/ppermute | solution.py:32
  19.6 1.5 %broadcast_in_dim.30 = bf16[12,16,1024]{2,1,0:T(8,128)(2,1)} broadcast(bf16[16,1024]{1,0:T(8,128)(2,1)} %param.6), dimensions={1,2} | broadcast | bytes 425984 | tf_op jit(solution)/shard_map/broadcast_in_dim | solution.py:21
  21.1 12.7 %all-to-all-start = ((bf16[12,16,1024]{2,1,0:T(8,128)(2,1)}), bf16[12,16,1024]{2,1,0:T(8,128)(2,1)S(1)}, u32[]{:S(2)}, u32[]{:S(2)}) async-start(bf16[12,16,1024]{2,1,0:T(8,128)(2,1)} %broadcast_in_dim.30), calls=%async_computation | async-start | bytes 786432 | tf_op jit(solution)/shard_map/all_to_all | solution.py:22
  33.8 0.0 copy-start
  33.8 0.0 copy-start.1
  33.8 0.0 copy-start.2
  33.8 2.3 %collective-permute-start.3 = (bf16[128,1152]{1,0:T(8,128)(2,1)S(1)}, bf16[128,1152]{1,0:T(8,128)(2,1)S(1)}, u32[]{:S(2)}, u32[]{:S(2)}) collective-permute-start(bf16[128,1152]{1,0:T(8,128)(2,1)S(1)} %pad_maximum_fusion), channel_id=1, source_target_pairs={{0,6},{1,11},{2,8},{3,13},{4,10},{5,15},{6,12},{7,1},{8,14},{9,3},... | collective-permute-start | bytes 884744 | tf_op jit(solution)/shard_map/ppermute | solution.py:32
  36.1 0.0 collective-permute-done.1
  36.2 0.0 collective-permute-done.2
  36.2 15.6 %collective-permute-done.3 = bf16[128,1152]{1,0:T(8,128)(2,1)S(1)} collective-permute-done((bf16[128,1152]{1,0:T(8,128)(2,1)S(1)}, bf16[128,1152]{1,0:T(8,128)(2,1)S(1)}, u32[]{:S(2)}, u32[]{:S(2)}) %collective-permute-start.3) | collective-permute-done | bytes 294944 | tf_op jit(solution)/shard_map/ppermute | solution.py:32
  51.9 0.0 collective-permute-done.4
  51.9 1.9 %collective-permute-start.5 = (bf16[512,1152]{1,0:T(8,128)(2,1)S(1)}, bf16[512,1152]{1,0:T(8,128)(2,1)}, u32[]{:S(2)}, u32[]{:S(2)}) collective-permute-start(bf16[512,1152]{1,0:T(8,128)(2,1)S(1)} %constant_dynamic-update-slice_fusion.2.refs_1_), channel_id=1, source_target_pairs={{0,1},{1,0},{2,3},{3,2},{4,5},{5,4},{6,7},{7,6},{8,9},{9,8},{10,11... | collective-permute-start | bytes 3538952 | tf_op jit(solution)/shard_map/ppermute | solution.py:36
  53.9 0.8 dynamic-slice_convert_fusion
  54.7 0.0 copy-done
  54.7 0.0 copy-done.1
  54.7 0.0 copy-done.2
  54.7 0.1 pad_add_fusion
  54.8 0.0 all-to-all-done
  54.8 1.4 %broadcast_in_dim.32 = bf16[4,192,1024]{2,1,0:T(8,128)(2,1)} broadcast(bf16[192,1024]{1,0:T(8,128)(2,1)S(1)} %bitcast.15), dimensions={1,2} | broadcast | bytes 1966080 | tf_op jit(solution)/shard_map/broadcast_in_dim | solution.py:21
  56.2 4.3 %all-to-all-start.1 = ((bf16[4,192,1024]{2,1,0:T(8,128)(2,1)}), bf16[4,192,1024]{2,1,0:T(8,128)(2,1)S(1)}, u32[]{:S(2)}, u32[]{:S(2)}) async-start(bf16[4,192,1024]{2,1,0:T(8,128)(2,1)} %broadcast_in_dim.32), calls=%async_computation.1 | async-start | bytes 3145728 | tf_op jit(solution)/shard_map/all_to_all | solution.py:22
  60.5 0.1 broadcast_in_dim.33
  60.6 0.1 reshape.41
  60.7 0.3 multiply_reduce_fusion.1
  61.0 0.0 collective-permute-done.5.refs_2_
  61.0 1.5 %multiply_reduce_fusion = f32[512]{0:T(512)S(1)} fusion(bf16[512,1152]{1,0:T(8,128)(2,1)} %collective-permute-done.5.refs_2_), kind=kLoop, calls=%fused_computation | loop fusion | flops 1572352 | bytes 1050624 | tf_op jit(solution)/shard_map/reduce_sum | solution.py:183
  62.5 0.1 fusion.1.refs_3_
  62.7 19.2 %all-to-all-done.1 = bf16[4,192,1024]{2,1,0:T(8,128)(2,1)S(1)} async-done(((bf16[4,192,1024]{2,1,0:T(8,128)(2,1)}), bf16[4,192,1024]{2,1,0:T(8,128)(2,1)S(1)}, u32[]{:S(2)}, u32[]{:S(2)}) %all-to-all-start.1) | async-done | bytes 1572896 | tf_op jit(solution)/shard_map/all_to_all | solution.py:22
  81.8 4.6 %score.1 = bf16[768,256]{1,0:T(8,128)(2,1)S(1)} custom-call(bf16[768,1024]{1,0:T(8,128)(2,1)S(1)} %bitcast.12, bf16[512,1152]{1,0:T(8,128)(2,1)S(1)} %constant_dynamic-update-slice_fusion.2.refs_1_, bf16[512,1152]{1,0:T(8,128)(2,1)} %collective-permute-done.5.refs_2_, f32[3,8,1024]{2,1,0:T(8,128)S(1)} %fusion.1.refs_3_), custom_call_target="tpu_custom_call" | custom-call | flops 1811939328 | bytes 4325376 | tf_op jit(solution)/shard_map/score/pallas_call | solution.py:110
  86.5 10.3 %all_to_all.20.parts_ref = bf16[4,192,256]{2,1,0:T(8,128)(2,1)S(1)} all-to-all(bf16[4,192,256]{2,1,0:T(8,128)(2,1)S(1)} %bitcast.13), channel_id=1, replica_groups=mesh['zl'=6,'x'=4,'zh'=2,'y'=8,'c'=2] {'x'}, dimensions={0} | all-to-all | bytes 786432 | tf_op jit(solution)/shard_map/all_to_all | solution.py:189
  96.7 0.4 merge.2
  97.1 20.1 %all_to_all.21.parts_ref = bf16[12,16,256]{2,1,0:T(8,128)(2,1)S(1)} all-to-all(bf16[12,16,256]{2,1,0:T(8,128)(2,1)S(1)} %bitcast.14), channel_id=1, replica_groups=mesh['zl'=6,'x'=4,'zh'=2,'y'=8,'c'=2] {'zl','zh'}, dimensions={0} | all-to-all | bytes 196608 | tf_op jit(solution)/shard_map/all_to_all | solution.py:191
  117.2 0.8 merge.3
  (12 shorter events, 0.2 us)
Async XLA Ops:
  1.7 3.3 %collective-permute-start = (bf16[64,1152]{1,0:T(8,128)(2,1)S(1)}, bf16[64,1152]{1,0:T(8,128)(2,1)S(1)}, u32[]{:S(2)}, u32[]{:S(2)}) collective-permute-start(bf16[64,1152]{1,0:T(8,128)(2,1)S(1)} %get-tuple-element.7), channel_id=1, source_target_pairs={{0,1},{1,0},{2,3},{3,2},{4,5},{5,4},{6,7},{7,6},{8,9},{9,8},{10,11... | collective-permute-start | bytes 442376 | tf_op jit(solution)/shard_map/ppermute | solution.py:36
  5.0 31.2 %collective-permute-start.1 = (bf16[128,1152]{1,0:T(8,128)(2,1)S(1)}, bf16[128,1152]{1,0:T(8,128)(2,1)S(1)}, u32[]{:S(2)}, u32[]{:S(2)}) collective-permute-start(bf16[128,1152]{1,0:T(8,128)(2,1)S(1)} %pad_maximum_fusion), channel_id=1, source_target_pairs={{0,2},{1,15},{2,4},{3,1},{4,6},{5,3},{6,8},{7,5},{8,10},{9,7},{10,... | collective-permute-start | bytes 884744 | tf_op jit(solution)/shard_map/ppermute | solution.py:32
  7.5 28.6 %collective-permute-start.2 = (bf16[128,1152]{1,0:T(8,128)(2,1)S(1)}, bf16[128,1152]{1,0:T(8,128)(2,1)S(1)}, u32[]{:S(2)}, u32[]{:S(2)}) collective-permute-start(bf16[128,1152]{1,0:T(8,128)(2,1)S(1)} %pad_maximum_fusion), channel_id=1, source_target_pairs={{0,4},{1,13},{2,6},{3,15},{4,8},{5,1},{6,10},{7,3},{8,12},{9,5},{1... | collective-permute-start | bytes 884744 | tf_op jit(solution)/shard_map/ppermute | solution.py:32
  17.7 34.2 %collective-permute-start.4 = (bf16[64,1152]{1,0:T(8,128)(2,1)S(1)}, bf16[64,1152]{1,0:T(8,128)(2,1)S(1)}, u32[]{:S(2)}, u32[]{:S(2)}) collective-permute-start(bf16[64,1152]{1,0:T(8,128)(2,1)S(1)} %get-tuple-element.7), channel_id=1, source_target_pairs={{0,8},{1,9},{2,10},{3,11},{4,12},{5,13},{6,14},{7,15},{8,0},{9,1},... | collective-permute-start | bytes 442376 | tf_op jit(solution)/shard_map/ppermute | solution.py:32
  21.1 33.7 %all-to-all-start = ((bf16[12,16,1024]{2,1,0:T(8,128)(2,1)}), bf16[12,16,1024]{2,1,0:T(8,128)(2,1)S(1)}, u32[]{:S(2)}, u32[]{:S(2)}) async-start(bf16[12,16,1024]{2,1,0:T(8,128)(2,1)} %broadcast_in_dim.30), calls=%async_computation | async-start | bytes 786432 | tf_op jit(solution)/shard_map/all_to_all | solution.py:22
  33.8 20.9 %copy-start = (s32[8]{0:T(128)S(1)}, s32[8]{0:T(128)}, u32[]{:S(2)}) copy-start(s32[8]{0:T(128)} %constant.72) | copy-start | bytes 100
  33.8 20.9 %copy-start.1 = (s32[8]{0:T(128)S(1)}, s32[8]{0:T(128)}, u32[]{:S(2)}) copy-start(s32[8]{0:T(128)} %constant.67.clone) | copy-start | bytes 100
  33.8 20.9 %copy-start.2 = (s32[8]{0:T(128)S(1)}, s32[8]{0:T(128)}, u32[]{:S(2)}) copy-start(s32[8]{0:T(128)} %constant.68.clone) | copy-start | bytes 100
  33.8 18.0 %collective-permute-start.3 = (bf16[128,1152]{1,0:T(8,128)(2,1)S(1)}, bf16[128,1152]{1,0:T(8,128)(2,1)S(1)}, u32[]{:S(2)}, u32[]{:S(2)}) collective-permute-start(bf16[128,1152]{1,0:T(8,128)(2,1)S(1)} %pad_maximum_fusion), channel_id=1, source_target_pairs={{0,6},{1,11},{2,8},{3,13},{4,10},{5,15},{6,12},{7,1},{8,14},{9,3},... | collective-permute-start | bytes 884744 | tf_op jit(solution)/shard_map/ppermute | solution.py:32
  51.9 9.1 %collective-permute-start.5 = (bf16[512,1152]{1,0:T(8,128)(2,1)S(1)}, bf16[512,1152]{1,0:T(8,128)(2,1)}, u32[]{:S(2)}, u32[]{:S(2)}) collective-permute-start(bf16[512,1152]{1,0:T(8,128)(2,1)S(1)} %constant_dynamic-update-slice_fusion.2.refs_1_), channel_id=1, source_target_pairs={{0,1},{1,0},{2,3},{3,2},{4,5},{5,4},{6,7},{7,6},{8,9},{9,8},{10,11... | collective-permute-start | bytes 3538952 | tf_op jit(solution)/shard_map/ppermute | solution.py:36
  56.2 25.7 %all-to-all-start.1 = ((bf16[4,192,1024]{2,1,0:T(8,128)(2,1)}), bf16[4,192,1024]{2,1,0:T(8,128)(2,1)S(1)}, u32[]{:S(2)}, u32[]{:S(2)}) async-start(bf16[4,192,1024]{2,1,0:T(8,128)(2,1)} %broadcast_in_dim.32), calls=%async_computation.1 | async-start | bytes 3145728 | tf_op jit(solution)/shard_map/all_to_all | solution.py:22

commit v4 on v3

--- a/solution.py
+++ b/solution.py
@@ -56,15 +56,17 @@
     return high, middle, low
 
 
-def pack_stats(row_max, weight_sum, rows):
-    lane = lax.broadcasted_iota(jnp.int32, (rows, LANES), 1)
-    stats = jnp.zeros((rows, LANES), jnp.float32)
+def stats_rows(row_max, weight_sum, dests, rows):
+    lane = lax.broadcasted_iota(jnp.int32, (dests * rows, LANES), 1)
+    row = lax.broadcasted_iota(jnp.int32, (dests * rows, LANES), 0) % rows
+    stats = jnp.zeros((dests * rows, LANES), jnp.float32)
     for place, piece in enumerate(split3(row_max) + split3(weight_sum)):
-        stats = jnp.where(lane == place, piece.astype(jnp.float32), stats)
-    return stats.astype(jnp.bfloat16)
-
-
-def score_kernel(queries_ref, own_ref, other_ref, bias_ref, out_ref, *, width, tile_rows, scale):
+        stats = jnp.where(lane // rows == place, piece.astype(jnp.float32), stats)
+    stats = jnp.where(lane % rows == row, stats, 0.0)
+    return jnp.sum(stats.reshape(dests, rows, LANES), axis=1, keepdims=True)
+
+
+def score_kernel(queries_ref, own_ref, other_ref, bias_ref, out_ref, *, width, tile_rows, part_rows, scale):
     rows = queries_ref.shape[0]
     lands = own_ref.shape[0]
     tiles = bias_ref.shape[1]
@@ -96,25 +98,31 @@
         ) + jnp.dot(
             other.astype(jnp.bfloat16), other_ref[:, width:], preferred_element_type=jnp.float32
         )
-        out_ref[pl.ds(start, chunk), :LANES] = (label_sum / weight_sum).astype(jnp.bfloat16)
-        out_ref[pl.ds(start, chunk), LANES:] = pack_stats(row_max, weight_sum, chunk)
+        dests = chunk // part_rows
+        place = pl.ds(pl.multiple_of(index * dests, dests), dests)
+        scores = (label_sum / weight_sum).astype(jnp.bfloat16)
+        out_ref[place, :part_rows, :] = scores.reshape(dests, part_rows, LANES)
+        stats = stats_rows(row_max, weight_sum, dests, part_rows)
+        out_ref[place, part_rows:, :] = jnp.broadcast_to(stats, (dests, 8, LANES)).astype(jnp.bfloat16)
 
     pl.loop(0, rows // chunk)(step)
 
 
-def score(queries, own, other, bias, width, tile_rows, scale):
+def score(queries, own, other, bias, width, tile_rows, part_rows, scale):
     rows = queries.shape[0]
     lands = own.shape[0] + other.shape[0]
     classes = own.shape[1] - width
     tiles = 8
     return pl.pallas_call(
-        lambda *refs: score_kernel(*refs, width=width, tile_rows=tile_rows, scale=scale),
-        out_shape=jax.ShapeDtypeStruct((rows, classes + LANES), jnp.bfloat16),
+        lambda *refs: score_kernel(
+            *refs, width=width, tile_rows=tile_rows, part_rows=part_rows, scale=scale
+        ),
+        out_shape=jax.ShapeDtypeStruct((rows // part_rows, part_rows + 8, classes), jnp.bfloat16),
         in_specs=[VMEM] * 4,
         out_specs=VMEM,
         cost_estimate=pl.CostEstimate(
             flops=2 * rows * lands * (width + classes),
-            bytes_accessed=2 * (rows * width + lands * (width + classes) + rows * 256),
+            bytes_accessed=2 * (rows * width + lands * (width + classes) + rows * 192),
             transcendentals=rows * lands,
         ),
         compiler_params=pltpu.CompilerParams(vmem_limit_bytes=24 << 20),
@@ -123,33 +131,29 @@
 
 
 def merge_kernel(parts_ref, out_ref):
-    sources, rows, _ = parts_ref.shape
-    piece = lax.broadcasted_iota(jnp.int32, (LANES, 2 * LANES), 0)
-    lane = lax.broadcasted_iota(jnp.int32, (LANES, 2 * LANES), 1)
-    first = jnp.where(lane < LANES, 0, 3)
-    spread = jnp.where((piece >= first) & (piece < first + 3), 1.0, 0.0).astype(jnp.bfloat16)
-    stats = [
-        jnp.dot(parts_ref[source, :, LANES:], spread, preferred_element_type=jnp.float32)
-        for source in range(sources)
-    ]
-    joint = stats[0][:, :LANES]
-    for stat in stats[1:]:
-        joint = jnp.maximum(joint, stat[:, :LANES])
-    total = jnp.zeros((rows, LANES), jnp.float32)
-    labels = jnp.zeros((rows, LANES), jnp.float32)
-    for source, stat in enumerate(stats):
-        weight = stat[:, LANES:] * jnp.exp(stat[:, :LANES] - joint)
-        total = total + weight
-        labels = labels + parts_ref[source, :, :LANES].astype(jnp.float32) * weight
-    out_ref[:, :LANES] = (labels / total).astype(jnp.bfloat16)
-    if out_ref.shape[1] > LANES:
-        out_ref[:, LANES:] = pack_stats(joint, total, rows)
-
-
-def merge(parts, width):
+    sources = parts_ref.shape[0]
+    rows = out_ref.shape[0]
+    lane = lax.broadcasted_iota(jnp.int32, (1, rows, LANES), 2)
+    row = lax.broadcasted_iota(jnp.int32, (1, rows, LANES), 1)
+    stats = parts_ref[:, rows:, :].astype(jnp.float32)
+    stats = jnp.concatenate([stats] * (rows // 8), axis=1)
+    stats = jnp.where(lane % rows == row, stats, 0.0).astype(jnp.bfloat16)
+    piece = lax.broadcasted_iota(jnp.int32, (LANES, 2 * LANES), 0) // rows
+    half = lax.broadcasted_iota(jnp.int32, (LANES, 2 * LANES), 1) // LANES
+    spread = jnp.where(piece // 3 == half, 1.0, 0.0).astype(jnp.bfloat16)
+    stats = jnp.dot(
+        stats.reshape(sources * rows, LANES), spread, preferred_element_type=jnp.float32
+    ).reshape(sources, rows, 2 * LANES)
+    row_max = stats[:, :, :LANES]
+    weight = stats[:, :, LANES:] * jnp.exp(row_max - jnp.max(row_max, axis=0, keepdims=True))
+    labels = jnp.sum(parts_ref[:, :rows, :].astype(jnp.float32) * weight, axis=0)
+    out_ref[...] = (labels / jnp.sum(weight, axis=0)).astype(jnp.bfloat16)
+
+
+def merge(parts, rows):
     return pl.pallas_call(
         merge_kernel,
-        out_shape=jax.ShapeDtypeStruct((parts.shape[1], width), jnp.bfloat16),
+        out_shape=jax.ShapeDtypeStruct((rows, parts.shape[2]), jnp.bfloat16),
         in_specs=[VMEM],
         out_specs=VMEM,
         compiler_params=pltpu.CompilerParams(vmem_limit_bytes=8 << 20),
@@ -159,14 +163,14 @@
 
 def local(queries, landmarks, labels, tile_mask):
     rows, width = queries.shape
-    tile_lands, classes = labels.shape
+    tile_lands, _ = labels.shape
     scale = 4.0 / math.sqrt(width)
     mine = jnp.concatenate([landmarks, labels], axis=1)
     pair = jnp.concatenate([mine, swap_cores(mine)], axis=0)
     gathered = gather_direct(queries, Z_AXES, Z)
-    third, fourth, second = both_ways(pair, 3), both_ways(mine, 4), both_ways(pair, 2)
-    first = both_ways(pair, 1)
-    own = jnp.concatenate([mine, first, second, third, fourth], axis=0)
+    second, first = both_ways(pair, 2), both_ways(pair, 1)
+    relayed = both_ways(jnp.concatenate([first, second[:tile_lands]], axis=0), 2)
+    own = jnp.concatenate([mine, first, second, relayed], axis=0)
     other = swap_cores(own)
     gathered = gather_direct(gathered, "x", X)
 
@@ -185,11 +189,9 @@
     norms = jnp.concatenate([half_norm(own), half_norm(other)])
     bias = jnp.where(listed, -scale * norms[None, :], jnp.float32(UNLISTED))
 
-    parts = score(gathered, own, other, bias, width, ZH * rows, scale)
-    parts = lax.all_to_all(parts.reshape(X, Z * rows, classes + LANES), "x", 0, 0, tiled=True)
-    parts = merge(parts, classes + LANES)
-    parts = lax.all_to_all(parts.reshape(Z, rows, classes + LANES), Z_AXES, 0, 0, tiled=True)
-    return merge(parts, classes)
+    parts = score(gathered, own, other, bias, width, ZH * rows, rows, scale)
+    parts = lax.all_to_all(parts, ("x",) + Z_AXES, 0, 0, tiled=True)
+    return merge(parts, rows)
 
 
 def solution(mesh):

time: 119 us -> 114 us (0.958)
  the two profiles are of different devices: /device:TPU:48 before, /device:TPU:2 now
where the time goes in v4:
time: 114 us
  waiting for transfers between devices  40.1 us (35%)
  starting transfers between devices  35.4 us (31%)
  blocking collectives  25.2 us (22%)
  Pallas kernels  5.67 us (5%)
  local copies, waits for them, and re-layouts  4.04 us (4%)
  other arithmetic  2.84 us (2%)
    all_to_all x2, waiting for transfers between devices, gather_direct(): gathered = lax.all_to_all(copies, axes, 0, 0, tiled=True)  29.6 us
    all_to_all x1, blocking collectives, local(): parts = lax.all_to_all(parts, ('x',) + Z_AXES, 0, 0, tiled=True)  25.2 us
    all_to_all x2, starting transfers between devices, gather_direct(): gathered = lax.all_to_all(copies, axes, 0, 0, tiled=True)  20.1 us
    ppermute x3, starting transfers between devices, both_ways(): return lax.ppermute(value, ('y', 'c'), pairs)  11.5 us
    ppermute x3, waiting for transfers between devices, both_ways(): return lax.ppermute(value, ('y', 'c'), pairs)  9.19 us
    pallas_call x1, Pallas kernels, score(): pl.pallas_call(lambda *refs: score_kernel(*refs, width=width, tile_rows=t...  4.67 us
    ppermute x2, starting transfers between devices, swap_cores(): return lax.ppermute(value, 'c', [(0, 1), (1, 0)])  3.83 us
  transfers between devices with their start and end apart: 7, of which 5 were waited for; matrix products, arithmetic and copies ran while one was open for 5% of the time, Pallas kernels for 0%

profile of v4, /device:TPU:2, one launch (start us, length us, event | category | flops | bytes accessed | tf_op | source)
XLA Modules:
  0.0 113.7 jit_solution(17840386785883338974)
XLA Ops:
  0.0 0.0 copy-start
  0.0 0.9 constant_dynamic-update-slice_fusion.1
  0.9 0.7 constant_dynamic-update-slice_fusion
  1.7 1.9 %collective-permute-start = (bf16[64,1152]{1,0:T(8,128)(2,1)S(1)}, bf16[64,1152]{1,0:T(8,128)(2,1)S(1)}, u32[]{:S(2)}, u32[]{:S(2)}) collective-permute-start(bf16[64,1152]{1,0:T(8,128)(2,1)S(1)} %constant_dynamic-update-slice_fusion), channel_id=1, source_target_pairs={{0,1},{1,0},{2,3},{3,2},{4,5},{5,4},{6,7},{7,6},{8,9},{9,8},{10,11... | collective-permute-start | bytes 442376 | tf_op jit(solution)/shard_map/ppermute | solution.py:36
  3.6 1.3 %collective-permute-done = bf16[64,1152]{1,0:T(8,128)(2,1)S(1)} collective-permute-done((bf16[64,1152]{1,0:T(8,128)(2,1)S(1)}, bf16[64,1152]{1,0:T(8,128)(2,1)S(1)}, u32[]{:S(2)}, u32[]{:S(2)}) %collective-permute-start) | collective-permute-done | bytes 147488 | tf_op jit(solution)/shard_map/ppermute | solution.py:36
  4.9 4.5 %collective-permute-start.2 = (bf16[128,1152]{1,0:T(8,128)(2,1)S(1)}, bf16[128,1152]{1,0:T(8,128)(2,1)S(1)}, u32[]{:S(2)}, u32[]{:S(2)}) collective-permute-start(bf16[128,1152]{1,0:T(8,128)(2,1)S(1)} %pad_maximum_fusion.2), channel_id=1, source_target_pairs={{0,4},{1,13},{2,6},{3,15},{4,8},{5,1},{6,10},{7,3},{8,12},{9,5},{1... | collective-permute-start | bytes 884744 | tf_op jit(solution)/shard_map/ppermute | solution.py:32
  9.4 3.5 %collective-permute-start.1 = (bf16[128,1152]{1,0:T(8,128)(2,1)S(1)}, bf16[128,1152]{1,0:T(8,128)(2,1)S(1)}, u32[]{:S(2)}, u32[]{:S(2)}) collective-permute-start(bf16[128,1152]{1,0:T(8,128)(2,1)S(1)} %pad_maximum_fusion.2), channel_id=1, source_target_pairs={{0,2},{1,15},{2,4},{3,1},{4,6},{5,3},{6,8},{7,5},{8,10},{9,7},{10,... | collective-permute-start | bytes 884744 | tf_op jit(solution)/shard_map/ppermute | solution.py:32
  12.9 3.8 %collective-permute-done.2 = bf16[128,1152]{1,0:T(8,128)(2,1)S(1)} collective-permute-done((bf16[128,1152]{1,0:T(8,128)(2,1)S(1)}, bf16[128,1152]{1,0:T(8,128)(2,1)S(1)}, u32[]{:S(2)}, u32[]{:S(2)}) %collective-permute-start.2) | collective-permute-done | bytes 294944 | tf_op jit(solution)/shard_map/ppermute | solution.py:32
  16.7 5.4 %collective-permute-done.1 = bf16[128,1152]{1,0:T(8,128)(2,1)S(1)} collective-permute-done((bf16[128,1152]{1,0:T(8,128)(2,1)S(1)}, bf16[128,1152]{1,0:T(8,128)(2,1)S(1)}, u32[]{:S(2)}, u32[]{:S(2)}) %collective-permute-start.1) | collective-permute-done | bytes 294944 | tf_op jit(solution)/shard_map/ppermute | solution.py:32
  22.2 3.5 %collective-permute-start.3 = (bf16[192,1152]{1,0:T(8,128)(2,1)S(1)}, bf16[192,1152]{1,0:T(8,128)(2,1)S(1)}, u32[]{:S(2)}, u32[]{:S(2)}) collective-permute-start(bf16[192,1152]{1,0:T(8,128)(2,1)S(1)} %pad_maximum_fusion.1), channel_id=1, source_target_pairs={{0,4},{1,13},{2,6},{3,15},{4,8},{5,1},{6,10},{7,3},{8,12},{9,5},{1... | collective-permute-start | bytes 1327112 | tf_op jit(solution)/shard_map/ppermute | solution.py:32
  25.7 0.0 copy-done
  25.7 0.8 broadcast_in_dim.30
  26.5 0.0 copy-start.1
  26.5 0.0 copy-start.2
  26.5 0.0 copy-start.3
  26.5 15.3 %all-to-all-start = ((bf16[12,16,1024]{2,1,0:T(8,128)(2,1)}), bf16[12,16,1024]{2,1,0:T(8,128)(2,1)S(1)}, u32[]{:S(2)}, u32[]{:S(2)}) async-start(bf16[12,16,1024]{2,1,0:T(8,128)(2,1)} %broadcast_in_dim.30), calls=%async_computation | async-start | bytes 786432 | tf_op jit(solution)/shard_map/all_to_all | solution.py:22
  41.8 0.0 collective-permute-done.3
  41.8 0.1 pad_maximum_fusion.refs_1_
  41.9 1.9 %collective-permute-start.4 = (bf16[512,1152]{1,0:T(8,128)(2,1)S(1)}, bf16[512,1152]{1,0:T(8,128)(2,1)}, u32[]{:S(2)}, u32[]{:S(2)}) collective-permute-start(bf16[512,1152]{1,0:T(8,128)(2,1)S(1)} %pad_maximum_fusion.refs_1_), channel_id=1, source_target_pairs={{0,1},{1,0},{2,3},{3,2},{4,5},{5,4},{6,7},{7,6},{8,9},{9,8},{10,11... | collective-permute-start | bytes 3538952 | tf_op jit(solution)/shard_map/ppermute | solution.py:36
  43.9 0.8 dynamic-slice_convert_fusion
  44.7 0.0 copy-done.1
  44.7 0.0 copy-done.2
  44.7 0.0 copy-done.3
  44.7 0.1 pad_add_fusion
  44.8 14.6 %all-to-all-done = bf16[12,16,1024]{2,1,0:T(8,128)(2,1)S(1)} async-done(((bf16[12,16,1024]{2,1,0:T(8,128)(2,1)}), bf16[12,16,1024]{2,1,0:T(8,128)(2,1)S(1)}, u32[]{:S(2)}, u32[]{:S(2)}) %all-to-all-start) | async-done | bytes 393248 | tf_op jit(solution)/shard_map/all_to_all | solution.py:22
  59.4 1.3 %broadcast_in_dim.32 = bf16[4,192,1024]{2,1,0:T(8,128)(2,1)} broadcast(bf16[192,1024]{1,0:T(8,128)(2,1)S(1)} %bitcast.11), dimensions={1,2} | broadcast | bytes 1966080 | tf_op jit(solution)/shard_map/broadcast_in_dim | solution.py:21
  60.8 4.8 %all-to-all-start.1 = ((bf16[4,192,1024]{2,1,0:T(8,128)(2,1)}), bf16[4,192,1024]{2,1,0:T(8,128)(2,1)S(1)}, u32[]{:S(2)}, u32[]{:S(2)}) async-start(bf16[4,192,1024]{2,1,0:T(8,128)(2,1)} %broadcast_in_dim.32), calls=%async_computation.1 | async-start | bytes 3145728 | tf_op jit(solution)/shard_map/all_to_all | solution.py:22
  65.6 0.1 broadcast_in_dim.33
  65.7 0.1 reshape.35
  65.8 0.3 multiply_reduce_fusion.1
  66.1 0.0 collective-permute-done.4.refs_2_
  66.1 1.5 %multiply_reduce_fusion = f32[512]{0:T(512)S(1)} fusion(bf16[512,1152]{1,0:T(8,128)(2,1)} %collective-permute-done.4.refs_2_), kind=kLoop, calls=%fused_computation | loop fusion | flops 1572352 | bytes 1050624 | tf_op jit(solution)/shard_map/reduce_sum | solution.py:187
  67.7 0.1 fusion.1.refs_3_
  67.8 15.0 %all-to-all-done.1 = bf16[4,192,1024]{2,1,0:T(8,128)(2,1)S(1)} async-done(((bf16[4,192,1024]{2,1,0:T(8,128)(2,1)}), bf16[4,192,1024]{2,1,0:T(8,128)(2,1)S(1)}, u32[]{:S(2)}, u32[]{:S(2)}) %all-to-all-start.1) | async-done | bytes 1572896 | tf_op jit(solution)/shard_map/all_to_all | solution.py:22
  82.8 4.7 %score.1 = bf16[48,24,128]{2,1,0:T(8,128)(2,1)S(1)} custom-call(bf16[768,1024]{1,0:T(8,128)(2,1)S(1)} %bitcast.10, bf16[512,1152]{1,0:T(8,128)(2,1)S(1)} %pad_maximum_fusion.refs_1_, bf16[512,1152]{1,0:T(8,128)(2,1)} %collective-permute-done.4.refs_2_, f32[3,8,1024]{2,1,0:T(8,128)S(1)} %fusion.1.refs_3_), custom_call_target="tpu_custom_call" | custom-call | flops 1811939328 | bytes 4227072 | tf_op jit(solution)/shard_map/score/pallas_call | solution.py:116
  87.4 25.2 %all_to_all.15.parts_ref = bf16[48,24,128]{2,1,0:T(8,128)(2,1)S(1)} all-to-all(bf16[48,24,128]{2,1,0:T(8,128)(2,1)S(1)} %score.1), channel_id=1, replica_groups=mesh['zl'=6,'x'=4,'zh'=2,'y'=8,'c'=2] {'x','zl','zh'}, dimensions={0} | all-to-all | bytes 589824 | tf_op jit(solution)/shard_map/all_to_all | solution.py:193
  112.7 1.0 merge.1
  (10 shorter events, 0.1 us)
Async XLA Ops:
  0.0 25.7 %copy-start = (bf16[16,1024]{1,0:T(8,128)(2,1)S(1)}, bf16[16,1024]{1,0:T(8,128)(2,1)}, u32[]{:S(2)}) copy-start(bf16[16,1024]{1,0:T(8,128)(2,1)} %param.6) | copy-start | bytes 98308
  1.7 3.3 %collective-permute-start = (bf16[64,1152]{1,0:T(8,128)(2,1)S(1)}, bf16[64,1152]{1,0:T(8,128)(2,1)S(1)}, u32[]{:S(2)}, u32[]{:S(2)}) collective-permute-start(bf16[64,1152]{1,0:T(8,128)(2,1)S(1)} %constant_dynamic-update-slice_fusion), channel_id=1, source_target_pairs={{0,1},{1,0},{2,3},{3,2},{4,5},{5,4},{6,7},{7,6},{8,9},{9,8},{10,11... | collective-permute-start | bytes 442376 | tf_op jit(solution)/shard_map/ppermute | solution.py:36
  4.9 11.8 %collective-permute-start.2 = (bf16[128,1152]{1,0:T(8,128)(2,1)S(1)}, bf16[128,1152]{1,0:T(8,128)(2,1)S(1)}, u32[]{:S(2)}, u32[]{:S(2)}) collective-permute-start(bf16[128,1152]{1,0:T(8,128)(2,1)S(1)} %pad_maximum_fusion.2), channel_id=1, source_target_pairs={{0,4},{1,13},{2,6},{3,15},{4,8},{5,1},{6,10},{7,3},{8,12},{9,5},{1... | collective-permute-start | bytes 884744 | tf_op jit(solution)/shard_map/ppermute | solution.py:32
  9.4 12.7 %collective-permute-start.1 = (bf16[128,1152]{1,0:T(8,128)(2,1)S(1)}, bf16[128,1152]{1,0:T(8,128)(2,1)S(1)}, u32[]{:S(2)}, u32[]{:S(2)}) collective-permute-start(bf16[128,1152]{1,0:T(8,128)(2,1)S(1)} %pad_maximum_fusion.2), channel_id=1, source_target_pairs={{0,2},{1,15},{2,4},{3,1},{4,6},{5,3},{6,8},{7,5},{8,10},{9,7},{10,... | collective-permute-start | bytes 884744 | tf_op jit(solution)/shard_map/ppermute | solution.py:32
  22.2 19.6 %collective-permute-start.3 = (bf16[192,1152]{1,0:T(8,128)(2,1)S(1)}, bf16[192,1152]{1,0:T(8,128)(2,1)S(1)}, u32[]{:S(2)}, u32[]{:S(2)}) collective-permute-start(bf16[192,1152]{1,0:T(8,128)(2,1)S(1)} %pad_maximum_fusion.1), channel_id=1, source_target_pairs={{0,4},{1,13},{2,6},{3,15},{4,8},{5,1},{6,10},{7,3},{8,12},{9,5},{1... | collective-permute-start | bytes 1327112 | tf_op jit(solution)/shard_map/ppermute | solution.py:32
  26.5 18.2 %copy-start.1 = (s32[8]{0:T(128)S(1)}, s32[8]{0:T(128)}, u32[]{:S(2)}) copy-start(s32[8]{0:T(128)} %constant.72) | copy-start | bytes 100
  26.5 18.2 %copy-start.2 = (s32[8]{0:T(128)S(1)}, s32[8]{0:T(128)}, u32[]{:S(2)}) copy-start(s32[8]{0:T(128)} %constant.67.clone) | copy-start | bytes 100
  26.5 18.2 %copy-start.3 = (s32[8]{0:T(128)S(1)}, s32[8]{0:T(128)}, u32[]{:S(2)}) copy-start(s32[8]{0:T(128)} %constant.68.clone) | copy-start | bytes 100
  26.5 32.9 %all-to-all-start = ((bf16[12,16,1024]{2,1,0:T(8,128)(2,1)}), bf16[12,16,1024]{2,1,0:T(8,128)(2,1)S(1)}, u32[]{:S(2)}, u32[]{:S(2)}) async-start(bf16[12,16,1024]{2,1,0:T(8,128)(2,1)} %broadcast_in_dim.30), calls=%async_computation | async-start | bytes 786432 | tf_op jit(solution)/shard_map/all_to_all | solution.py:22
  41.9 24.2 %collective-permute-start.4 = (bf16[512,1152]{1,0:T(8,128)(2,1)S(1)}, bf16[512,1152]{1,0:T(8,128)(2,1)}, u32[]{:S(2)}, u32[]{:S(2)}) collective-permute-start(bf16[512,1152]{1,0:T(8,128)(2,1)S(1)} %pad_maximum_fusion.refs_1_), channel_id=1, source_target_pairs={{0,1},{1,0},{2,3},{3,2},{4,5},{5,4},{6,7},{7,6},{8,9},{9,8},{10,11... | collective-permute-start | bytes 3538952 | tf_op jit(solution)/shard_map/ppermute | solution.py:36
  60.8 22.0 %all-to-all-start.1 = ((bf16[4,192,1024]{2,1,0:T(8,128)(2,1)}), bf16[4,192,1024]{2,1,0:T(8,128)(2,1)S(1)}, u32[]{:S(2)}, u32[]{:S(2)}) async-start(bf16[4,192,1024]{2,1,0:T(8,128)(2,1)} %broadcast_in_dim.32), calls=%async_computation.1 | async-start | bytes 3145728 | tf_op jit(solution)/shard_map/all_to_all | solution.py:22

commit v5 on v4

v5 whole, which is shorter than its diff:
```python
import math

import jax
import jax.numpy as jnp
from jax import lax
from jax.experimental import pallas as pl
from jax.experimental.pallas import tpu as pltpu
from jax.sharding import Mesh, PartitionSpec as P


ZL, X, ZH, Y, CORE = 6, 4, 2, 8, 2
NAMES = ("zl", "x", "zh", "y", "c")
Z = ZL * ZH
UNLISTED = -1e30
LANES = 128
VMEM = pl.BlockSpec(memory_space=pltpu.VMEM)


def gather_direct(value, axes, count):
    copies = jnp.broadcast_to(value[None], (count,) + value.shape)
    gathered = lax.all_to_all(copies, axes, 0, 0, tiled=True)
    return gathered.reshape((count * value.shape[0],) + value.shape[1:])


def pass_on(tile):
    pairs = []
    for z in range(Z):
        for core in range(CORE):
            to = (z + (1 if core == 0 else -1)) % Z
            pairs.append(tuple((at % ZL * ZH + at // ZL) * CORE + core for at in (z, to)))
    return lax.ppermute(tile, ("zl", "zh", "c"), pairs)


def swap_cores(value):
    return lax.ppermute(value, "c", [(0, 1), (1, 0)])


def tiles_held():
    core = lax.axis_index("c")
    place = lax.broadcasted_iota(jnp.int32, (Z,), 0)
    steps = (place + 1) // 2
    flip = jnp.where(place == 0, 0, 1 - place % 2)
    z = lax.axis_index("zh") * ZL + lax.axis_index("zl")
    z = (z + jnp.where(core == 0, Z - steps, steps)) % Z
    loop = z % ZL * X + lax.axis_index("x")
    return ((loop * ZH + z // ZL) * Y + lax.axis_index("y")) * CORE + (core ^ flip)


def split3(value):
    high = value.astype(jnp.bfloat16)
    rest = value - high.astype(jnp.float32)
    middle = rest.astype(jnp.bfloat16)
    low = (rest - middle.astype(jnp.float32)).astype(jnp.bfloat16)
    return high, middle, low


def stats_rows(row_max, weight_sum, dests, rows):
    lane = lax.broadcasted_iota(jnp.int32, (dests * rows, LANES), 1)
    row = lax.broadcasted_iota(jnp.int32, (dests * rows, LANES), 0) % rows
    stats = jnp.zeros((dests * rows, LANES), jnp.float32)
    for place, piece in enumerate(split3(row_max) + split3(weight_sum)):
        stats = jnp.where(lane // rows == place, piece.astype(jnp.float32), stats)
    stats = jnp.where(lane % rows == row, stats, 0.0)
    return jnp.sum(stats.reshape(dests, rows, LANES), axis=1, keepdims=True)


def score_kernel(
    queries_ref, own_ref, other_ref, own_bias_ref, other_bias_ref, out_ref, *, width, part_rows, scale
):
    tiles = own_bias_ref.shape[0]
    chunk = queries_ref.shape[0] // tiles
    dests = chunk // part_rows

    for tile in range(tiles):
        queries = queries_ref[tile * chunk : (tile + 1) * chunk, :]

        def logits_of(land_ref, bias_ref):
            logits = lax.dot_general(
                queries,
                land_ref[:, :width],
                (((1,), (1,)), ((), ())),
                preferred_element_type=jnp.float32,
            )
            return logits * scale + bias_ref[tile : tile + 1, :]

        own = logits_of(own_ref, own_bias_ref)
        other = logits_of(other_ref, other_bias_ref)
        row_max = jnp.max(jnp.maximum(own, other), axis=1, keepdims=True)
        own = jnp.exp(own - row_max)
        other = jnp.exp(other - row_max)
        weight_sum = jnp.sum(own + other, axis=1, keepdims=True)
        label_sum = jnp.dot(
            own.astype(jnp.bfloat16), own_ref[:, width:], preferred_element_type=jnp.float32
        ) + jnp.dot(
            other.astype(jnp.bfloat16), other_ref[:, width:], preferred_element_type=jnp.float32
        )
        place = slice(tile * dests, (tile + 1) * dests)
        scores = (label_sum / weight_sum).astype(jnp.bfloat16)
        out_ref[place, :part_rows, :] = scores.reshape(dests, part_rows, LANES)
        stats = stats_rows(row_max, weight_sum, dests, part_rows)
        out_ref[place, part_rows:, :] = jnp.broadcast_to(stats, (dests, 8, LANES)).astype(jnp.bfloat16)


def score(queries, own, other, own_bias, other_bias, width, part_rows, scale):
    rows = queries.shape[0]
    lands = own.shape[0] + other.shape[0]
    classes = own.shape[1] - width
    return pl.pallas_call(
        lambda *refs: score_kernel(*refs, width=width, part_rows=part_rows, scale=scale),
        out_shape=jax.ShapeDtypeStruct((rows // part_rows, part_rows + 8, classes), jnp.bfloat16),
        in_specs=[VMEM] * 5,
        out_specs=VMEM,
        cost_estimate=pl.CostEstimate(
            flops=2 * rows * lands * (width + classes),
            bytes_accessed=2 * (rows * width + lands * (width + classes) + rows * 192),
            transcendentals=rows * lands,
        ),
        compiler_params=pltpu.CompilerParams(vmem_limit_bytes=24 << 20),
        name="score",
    )(queries, own, other, own_bias, other_bias)


def merge_kernel(parts_ref, out_ref):
    sources = parts_ref.shape[0]
    rows = out_ref.shape[0]
    lane = lax.broadcasted_iota(jnp.int32, (1, rows, LANES), 2)
    row = lax.broadcasted_iota(jnp.int32, (1, rows, LANES), 1)
    stats = parts_ref[:, rows:, :].astype(jnp.float32)
    stats = jnp.concatenate([stats] * (rows // 8), axis=1)
    stats = jnp.where(lane % rows == row, stats, 0.0).astype(jnp.bfloat16)
    piece = lax.broadcasted_iota(jnp.int32, (LANES, 2 * LANES), 0) // rows
    half = lax.broadcasted_iota(jnp.int32, (LANES, 2 * LANES), 1) // LANES
    spread = jnp.where(piece // 3 == half, 1.0, 0.0).astype(jnp.bfloat16)
    stats = jnp.dot(
        stats.reshape(sources * rows, LANES), spread, preferred_element_type=jnp.float32
    ).reshape(sources, rows, 2 * LANES)
    row_max = stats[:, :, :LANES]
    weight = stats[:, :, LANES:] * jnp.exp(row_max - jnp.max(row_max, axis=0, keepdims=True))
    labels = jnp.sum(parts_ref[:, :rows, :].astype(jnp.float32) * weight, axis=0)
    out_ref[...] = (labels / jnp.sum(weight, axis=0)).astype(jnp.bfloat16)


def merge(parts, rows):
    return pl.pallas_call(
        merge_kernel,
        out_shape=jax.ShapeDtypeStruct((rows, parts.shape[2]), jnp.bfloat16),
        in_specs=[VMEM],
        out_specs=VMEM,
        compiler_params=pltpu.CompilerParams(vmem_limit_bytes=8 << 20),
        name="merge",
    )(parts)


def local(queries, landmarks, labels, tile_mask):
    rows, width = queries.shape
    tile_lands, classes = labels.shape
    scale = 4.0 / math.sqrt(width)
    mine = jnp.concatenate([landmarks, labels], axis=1)
    gathered = gather_direct(queries, ("x", "y"), X * Y)

    own = jnp.zeros((Z * tile_lands, width + classes), jnp.bfloat16)
    own = lax.dynamic_update_slice_in_dim(own, mine, 0, 0)
    chains = [mine, swap_cores(mine)]
    for place in range(1, Z):
        chain = (place + 1) % 2
        chains[chain] = pass_on(chains[chain])
        own = lax.dynamic_update_slice_in_dim(own, chains[chain], place * tile_lands, 0)
    other = swap_cores(own)

    wanted = lax.dynamic_slice_in_dim(tile_mask, lax.axis_index("zl") * X, X, 0)
    pick = lax.broadcasted_iota(jnp.int32, (tile_mask.shape[1], 1), 0) == tiles_held()[None, :]
    listed = jnp.dot(
        wanted.astype(jnp.float32), pick.astype(jnp.float32), preferred_element_type=jnp.float32
    )
    listed = jnp.broadcast_to(listed[:, :, None] > 0.5, (X, Z, tile_lands)).reshape(X, Z * tile_lands)
    own_f = own[:, :width].astype(jnp.float32)
    half_norm = 0.5 * jnp.sum(own_f * own_f, axis=1)
    own_bias = jnp.where(listed, -scale * half_norm[None, :], jnp.float32(UNLISTED))
    other_bias = swap_cores(own_bias)

    parts = score(gathered, own, other, own_bias, other_bias, width, rows, scale)
    parts = lax.all_to_all(parts, ("x", "y"), 0, 0, tiled=True)
    return merge(parts, rows)


def solution(mesh):
    physical = Mesh(mesh.devices.reshape(ZL, X, ZH, Y, CORE), NAMES)
    split = P(NAMES, None)

    return jax.shard_map(
        local, mesh=physical, in_specs=(split, split, split, P()), out_specs=split, check_vma=False
    )
```

time: 114 us -> 107 us (0.939)
  the two profiles are of different devices: /device:TPU:2 before, /device:TPU:1 now
where the time goes in v5:
time: 107 us; the launch traced here: 105 us
  starting transfers between devices  65.3 us (61%)
  blocking collectives  18.7 us (17%)
  Pallas kernels  7.91 us (7%)
  waiting for transfers between devices  7.16 us (7%)
  local copies, waits for them, and re-layouts  4.01 us (4%)
    ppermute x11, starting transfers between devices, pass_on(): return lax.ppermute(tile, ('zl', 'zh', 'c'), pairs)  36.3 us
    ppermute x3, starting transfers between devices, swap_cores(): return lax.ppermute(value, 'c', [(0, 1), (1, 0)])  19.4 us
    all_to_all x1, blocking collectives, local(): parts = lax.all_to_all(parts, ('x', 'y'), 0, 0, tiled=True)  18.7 us
    all_to_all x1, starting transfers between devices, gather_direct(): gathered = lax.all_to_all(copies, axes, 0, 0, tiled=True)  9.67 us
    pallas_call x1, Pallas kernels, score(): pl.pallas_call(lambda *refs: score_kernel(*refs, width=width, part_rows=p...  7 us
    ppermute x11, waiting for transfers between devices, pass_on(): return lax.ppermute(tile, ('zl', 'zh', 'c'), pairs)  6.01 us
  transfers between devices with their start and end apart: 15, of which 4 were waited for; matrix products, arithmetic and copies ran while one was open for 4% of the time, Pallas kernels for 0%

profile of v5, /device:TPU:1, one launch (start us, length us, event | category | flops | bytes accessed | tf_op | source)
XLA Modules:
  0.0 104.8 jit_solution(10625266169522742693)
XLA Ops:
  0.0 0.9 constant_dynamic-update-slice_fusion.1
  0.9 0.7 constant_dynamic-update-slice_fusion
  1.6 12.4 %collective-permute-start.1 = (bf16[64,1152]{1,0:T(8,128)(2,1)S(1)}, bf16[64,1152]{1,0:T(8,128)(2,1)S(1)}, u32[]{:S(2)}, u32[]{:S(2)}) collective-permute-start(bf16[64,1152]{1,0:T(8,128)(2,1)S(1)} %constant_dynamic-update-slice_fusion), channel_id=1, source_target_pairs={{0,1},{1,0},{2,3},{3,2},{4,5},{5,4},{6,7},{7,6},{8,9},{9,8},{10,11... | collective-permute-start | bytes 442376 | tf_op jit(solution)/shard_map/ppermute | solution.py:35
  14.0 5.3 %collective-permute-start = (bf16[64,1152]{1,0:T(8,128)(2,1)S(1)}, bf16[64,1152]{1,0:T(8,128)(2,1)S(1)}, u32[]{:S(2)}, u32[]{:S(2)}) collective-permute-start(bf16[64,1152]{1,0:T(8,128)(2,1)S(1)} %constant_dynamic-update-slice_fusion), channel_id=1, source_target_pairs={{0,128},{1,657},{128,256},{129,1},{256,384},{257,129},{384,512},{3... | collective-permute-start | bytes 442376 | tf_op jit(solution)/shard_map/ppermute | solution.py:31
  19.4 1.9 %broadcast_in_dim.14 = bf16[32,16,1024]{2,1,0:T(8,128)(2,1)} broadcast(bf16[16,1024]{1,0:T(8,128)(2,1)} %param.4), dimensions={1,2} | broadcast | bytes 1081344 | tf_op jit(solution)/shard_map/broadcast_in_dim | solution.py:20
  21.2 9.7 %all-to-all-start = ((bf16[32,16,1024]{2,1,0:T(8,128)(2,1)}), bf16[32,16,1024]{2,1,0:T(8,128)(2,1)S(1)}, u32[]{:S(2)}, u32[]{:S(2)}) async-start(bf16[32,16,1024]{2,1,0:T(8,128)(2,1)} %broadcast_in_dim.14), calls=%async_computation | async-start | bytes 2097152 | tf_op jit(solution)/shard_map/all_to_all | solution.py:21
  30.9 0.1 dynamic_update_slice.36
  31.0 0.0 collective-permute-done.1
  31.0 2.2 %collective-permute-start.2 = (bf16[64,1152]{1,0:T(8,128)(2,1)S(1)}, bf16[64,1152]{1,0:T(8,128)(2,1)S(1)}, u32[]{:S(2)}, u32[]{:S(2)}) collective-permute-start(bf16[64,1152]{1,0:T(8,128)(2,1)S(1)} %collective-permute-done.1), channel_id=1, source_target_pairs={{0,128},{1,657},{128,256},{129,1},{256,384},{257,129},{384,512},{3... | collective-permute-start | bytes 442376 | tf_op jit(solution)/shard_map/ppermute | solution.py:31
  33.2 0.0 collective-permute-done
  33.2 2.2 %collective-permute-start.3 = (bf16[64,1152]{1,0:T(8,128)(2,1)S(1)}, bf16[64,1152]{1,0:T(8,128)(2,1)S(1)}, u32[]{:S(2)}, u32[]{:S(2)}) collective-permute-start(bf16[64,1152]{1,0:T(8,128)(2,1)S(1)} %collective-permute-done), channel_id=1, source_target_pairs={{0,128},{1,657},{128,256},{129,1},{256,384},{257,129},{384,512},{3... | collective-permute-start | bytes 442376 | tf_op jit(solution)/shard_map/ppermute | solution.py:31
  35.5 1.8 %collective-permute-done.2 = bf16[64,1152]{1,0:T(8,128)(2,1)S(1)} collective-permute-done((bf16[64,1152]{1,0:T(8,128)(2,1)S(1)}, bf16[64,1152]{1,0:T(8,128)(2,1)S(1)}, u32[]{:S(2)}, u32[]{:S(2)}) %collective-permute-start.2) | collective-permute-done | bytes 147488 | tf_op jit(solution)/shard_map/ppermute | solution.py:31
  37.2 3.1 %collective-permute-start.4 = (bf16[64,1152]{1,0:T(8,128)(2,1)S(1)}, bf16[64,1152]{1,0:T(8,128)(2,1)S(1)}, u32[]{:S(2)}, u32[]{:S(2)}) collective-permute-start(bf16[64,1152]{1,0:T(8,128)(2,1)S(1)} %collective-permute-done.2), channel_id=1, source_target_pairs={{0,128},{1,657},{128,256},{129,1},{256,384},{257,129},{384,512},{3... | collective-permute-start | bytes 442376 | tf_op jit(solution)/shard_map/ppermute | solution.py:31
  40.3 0.0 collective-permute-done.3
  40.4 2.5 %collective-permute-start.5 = (bf16[64,1152]{1,0:T(8,128)(2,1)S(1)}, bf16[64,1152]{1,0:T(8,128)(2,1)S(1)}, u32[]{:S(2)}, u32[]{:S(2)}) collective-permute-start(bf16[64,1152]{1,0:T(8,128)(2,1)S(1)} %collective-permute-done.3), channel_id=1, source_target_pairs={{0,128},{1,657},{128,256},{129,1},{256,384},{257,129},{384,512},{3... | collective-permute-start | bytes 442376 | tf_op jit(solution)/shard_map/ppermute | solution.py:31
  42.8 0.6 collective-permute-done.4
  43.4 4.3 %collective-permute-start.6 = (bf16[64,1152]{1,0:T(8,128)(2,1)S(1)}, bf16[64,1152]{1,0:T(8,128)(2,1)S(1)}, u32[]{:S(2)}, u32[]{:S(2)}) collective-permute-start(bf16[64,1152]{1,0:T(8,128)(2,1)S(1)} %collective-permute-done.4), channel_id=1, source_target_pairs={{0,128},{1,657},{128,256},{129,1},{256,384},{257,129},{384,512},{3... | collective-permute-start | bytes 442376 | tf_op jit(solution)/shard_map/ppermute | solution.py:31
  47.7 0.0 collective-permute-done.5
  47.7 2.5 %collective-permute-start.7 = (bf16[64,1152]{1,0:T(8,128)(2,1)S(1)}, bf16[64,1152]{1,0:T(8,128)(2,1)S(1)}, u32[]{:S(2)}, u32[]{:S(2)}) collective-permute-start(bf16[64,1152]{1,0:T(8,128)(2,1)S(1)} %collective-permute-done.5), channel_id=1, source_target_pairs={{0,128},{1,657},{128,256},{129,1},{256,384},{257,129},{384,512},{3... | collective-permute-start | bytes 442376 | tf_op jit(solution)/shard_map/ppermute | solution.py:31
  50.2 0.0 collective-permute-done.6
  50.2 4.8 %collective-permute-start.8 = (bf16[64,1152]{1,0:T(8,128)(2,1)S(1)}, bf16[64,1152]{1,0:T(8,128)(2,1)S(1)}, u32[]{:S(2)}, u32[]{:S(2)}) collective-permute-start(bf16[64,1152]{1,0:T(8,128)(2,1)S(1)} %collective-permute-done.6), channel_id=1, source_target_pairs={{0,128},{1,657},{128,256},{129,1},{256,384},{257,129},{384,512},{3... | collective-permute-start | bytes 442376 | tf_op jit(solution)/shard_map/ppermute | solution.py:31
  55.1 0.0 collective-permute-done.7
  55.1 2.5 %collective-permute-start.9 = (bf16[64,1152]{1,0:T(8,128)(2,1)S(1)}, bf16[64,1152]{1,0:T(8,128)(2,1)S(1)}, u32[]{:S(2)}, u32[]{:S(2)}) collective-permute-start(bf16[64,1152]{1,0:T(8,128)(2,1)S(1)} %collective-permute-done.7), channel_id=1, source_target_pairs={{0,128},{1,657},{128,256},{129,1},{256,384},{257,129},{384,512},{3... | collective-permute-start | bytes 442376 | tf_op jit(solution)/shard_map/ppermute | solution.py:31
  57.6 0.0 collective-permute-done.8
  57.6 4.5 %collective-permute-start.10 = (bf16[64,1152]{1,0:T(8,128)(2,1)S(1)}, bf16[64,1152]{1,0:T(8,128)(2,1)S(1)}, u32[]{:S(2)}, u32[]{:S(2)}) collective-permute-start(bf16[64,1152]{1,0:T(8,128)(2,1)S(1)} %collective-permute-done.8), channel_id=1, source_target_pairs={{0,128},{1,657},{128,256},{129,1},{256,384},{257,129},{384,512},{3... | collective-permute-start | bytes 442376 | tf_op jit(solution)/shard_map/ppermute | solution.py:31
  62.2 0.0 collective-permute-done.9
  62.2 2.5 %collective-permute-start.11 = (bf16[64,1152]{1,0:T(8,128)(2,1)S(1)}, bf16[64,1152]{1,0:T(8,128)(2,1)S(1)}, u32[]{:S(2)}, u32[]{:S(2)}) collective-permute-start(bf16[64,1152]{1,0:T(8,128)(2,1)S(1)} %collective-permute-done.9), channel_id=1, source_target_pairs={{0,128},{1,657},{128,256},{129,1},{256,384},{257,129},{384,512},{3... | collective-permute-start | bytes 442376 | tf_op jit(solution)/shard_map/ppermute | solution.py:31
  64.7 0.0 collective-permute-done.10
  64.7 3.7 %collective-permute-done.11 = bf16[64,1152]{1,0:T(8,128)(2,1)S(1)} collective-permute-done((bf16[64,1152]{1,0:T(8,128)(2,1)S(1)}, bf16[64,1152]{1,0:T(8,128)(2,1)S(1)}, u32[]{:S(2)}, u32[]{:S(2)}) %collective-permute-start.11) | collective-permute-done | bytes 147488 | tf_op jit(solution)/shard_map/ppermute | solution.py:31
  68.4 5.1 %collective-permute-start.12 = (bf16[768,1152]{1,0:T(8,128)(2,1)S(1)}, bf16[768,1152]{1,0:T(8,128)(2,1)}, u32[]{:S(2)}, u32[]{:S(2)}) collective-permute-start(bf16[768,1152]{1,0:T(8,128)(2,1)S(1)} %constant_dynamic-update-slice_fusion.2.refs_1_), channel_id=1, source_target_pairs={{0,1},{1,0},{2,3},{3,2},{4,5},{5,4},{6,7},{7,6},{8,9},{9,8},{10,11... | collective-permute-start | bytes 5308424 | tf_op jit(solution)/shard_map/ppermute | solution.py:35
  73.6 0.9 convolution_compare_fusion
  74.5 0.1 broadcast_in_dim.15
  74.6 0.1 reshape.74
  74.7 0.4 multiply_reduce_fusion
  75.1 1.9 %collective-permute-start.13 = (f32[4,768]{1,0:T(4,128)S(1)}, f32[4,768]{1,0:T(4,128)S(1)}, u32[]{:S(2)}, u32[]{:S(2)}) collective-permute-start(f32[4,768]{1,0:T(4,128)S(1)} %broadcast_select_fusion.refs_3_), channel_id=1, source_target_pairs={{0,1},{1,0},{2,3},{3,2},{4,5},{5,4},{6,7},{7,6},{8,9},{9,8},{10,11... | collective-permute-start | bytes 36872 | tf_op jit(solution)/shard_map/ppermute | solution.py:35
  77.0 1.1 %collective-permute-done.13.refs_4_ = f32[4,768]{1,0:T(4,128)S(1)} collective-permute-done((f32[4,768]{1,0:T(4,128)S(1)}, f32[4,768]{1,0:T(4,128)S(1)}, u32[]{:S(2)}, u32[]{:S(2)}) %collective-permute-start.13) | collective-permute-done | bytes 12320 | tf_op jit(solution)/shard_map/ppermute | solution.py:35
  78.1 0.0 all-to-all-done
  78.1 0.0 collective-permute-done.12.refs_2_
  78.2 7.0 %score.1 = bf16[32,24,128]{2,1,0:T(8,128)(2,1)S(1)} custom-call(bf16[512,1024]{1,0:T(8,128)(2,1)S(1)} %bitcast.1, bf16[768,1152]{1,0:T(8,128)(2,1)S(1)} %constant_dynamic-update-slice_fusion.2.refs_1_, bf16[768,1152]{1,0:T(8,128)(2,1)} %collective-permute-done.12.refs_2_, f32[4,768]{1,0:T(4,128)S(1)} %broadcast_select_fusion.refs_3_, ...), custom_call_target="tpu_custom_call" | custom-call | flops 1811939328 | bytes 4784128 | tf_op jit(solution)/shard_map/score/pallas_call | solution.py:108
  85.2 18.7 %all_to_all.10.parts_ref = bf16[32,24,128]{2,1,0:T(8,128)(2,1)S(1)} all-to-all(bf16[32,24,128]{2,1,0:T(8,128)(2,1)S(1)} %score.1), channel_id=1, replica_groups=mesh['zl'=6,'x'=4,'zh'=2,'y'=8,'c'=2] {'x','y'}, dimensions={0} | all-to-all | bytes 393216 | tf_op jit(solution)/shard_map/all_to_all | solution.py:182
  103.9 0.9 merge.1
  (14 shorter events, 0.3 us)
Async XLA Ops:
  1.6 29.4 %collective-permute-start.1 = (bf16[64,1152]{1,0:T(8,128)(2,1)S(1)}, bf16[64,1152]{1,0:T(8,128)(2,1)S(1)}, u32[]{:S(2)}, u32[]{:S(2)}) collective-permute-start(bf16[64,1152]{1,0:T(8,128)(2,1)S(1)} %constant_dynamic-update-slice_fusion), channel_id=1, source_target_pairs={{0,1},{1,0},{2,3},{3,2},{4,5},{5,4},{6,7},{7,6},{8,9},{9,8},{10,11... | collective-permute-start | bytes 442376 | tf_op jit(solution)/shard_map/ppermute | solution.py:35
  14.0 19.2 %collective-permute-start = (bf16[64,1152]{1,0:T(8,128)(2,1)S(1)}, bf16[64,1152]{1,0:T(8,128)(2,1)S(1)}, u32[]{:S(2)}, u32[]{:S(2)}) collective-permute-start(bf16[64,1152]{1,0:T(8,128)(2,1)S(1)} %constant_dynamic-update-slice_fusion), channel_id=1, source_target_pairs={{0,128},{1,657},{128,256},{129,1},{256,384},{257,129},{384,512},{3... | collective-permute-start | bytes 442376 | tf_op jit(solution)/shard_map/ppermute | solution.py:31
  21.2 56.9 %all-to-all-start = ((bf16[32,16,1024]{2,1,0:T(8,128)(2,1)}), bf16[32,16,1024]{2,1,0:T(8,128)(2,1)S(1)}, u32[]{:S(2)}, u32[]{:S(2)}) async-start(bf16[32,16,1024]{2,1,0:T(8,128)(2,1)} %broadcast_in_dim.14), calls=%async_computation | async-start | bytes 2097152 | tf_op jit(solution)/shard_map/all_to_all | solution.py:21
  31.0 6.2 %collective-permute-start.2 = (bf16[64,1152]{1,0:T(8,128)(2,1)S(1)}, bf16[64,1152]{1,0:T(8,128)(2,1)S(1)}, u32[]{:S(2)}, u32[]{:S(2)}) collective-permute-start(bf16[64,1152]{1,0:T(8,128)(2,1)S(1)} %collective-permute-done.1), channel_id=1, source_target_pairs={{0,128},{1,657},{128,256},{129,1},{256,384},{257,129},{384,512},{3... | collective-permute-start | bytes 442376 | tf_op jit(solution)/shard_map/ppermute | solution.py:31
  33.2 7.1 %collective-permute-start.3 = (bf16[64,1152]{1,0:T(8,128)(2,1)S(1)}, bf16[64,1152]{1,0:T(8,128)(2,1)S(1)}, u32[]{:S(2)}, u32[]{:S(2)}) collective-permute-start(bf16[64,1152]{1,0:T(8,128)(2,1)S(1)} %collective-permute-done), channel_id=1, source_target_pairs={{0,128},{1,657},{128,256},{129,1},{256,384},{257,129},{384,512},{3... | collective-permute-start | bytes 442376 | tf_op jit(solution)/shard_map/ppermute | solution.py:31
  37.2 6.2 %collective-permute-start.4 = (bf16[64,1152]{1,0:T(8,128)(2,1)S(1)}, bf16[64,1152]{1,0:T(8,128)(2,1)S(1)}, u32[]{:S(2)}, u32[]{:S(2)}) collective-permute-start(bf16[64,1152]{1,0:T(8,128)(2,1)S(1)} %collective-permute-done.2), channel_id=1, source_target_pairs={{0,128},{1,657},{128,256},{129,1},{256,384},{257,129},{384,512},{3... | collective-permute-start | bytes 442376 | tf_op jit(solution)/shard_map/ppermute | solution.py:31
  40.4 7.4 %collective-permute-start.5 = (bf16[64,1152]{1,0:T(8,128)(2,1)S(1)}, bf16[64,1152]{1,0:T(8,128)(2,1)S(1)}, u32[]{:S(2)}, u32[]{:S(2)}) collective-permute-start(bf16[64,1152]{1,0:T(8,128)(2,1)S(1)} %collective-permute-done.3), channel_id=1, source_target_pairs={{0,128},{1,657},{128,256},{129,1},{256,384},{257,129},{384,512},{3... | collective-permute-start | bytes 442376 | tf_op jit(solution)/shard_map/ppermute | solution.py:31
  43.4 6.8 %collective-permute-start.6 = (bf16[64,1152]{1,0:T(8,128)(2,1)S(1)}, bf16[64,1152]{1,0:T(8,128)(2,1)S(1)}, u32[]{:S(2)}, u32[]{:S(2)}) collective-permute-start(bf16[64,1152]{1,0:T(8,128)(2,1)S(1)} %collective-permute-done.4), channel_id=1, source_target_pairs={{0,128},{1,657},{128,256},{129,1},{256,384},{257,129},{384,512},{3... | collective-permute-start | bytes 442376 | tf_op jit(solution)/shard_map/ppermute | solution.py:31
  47.7 7.4 %collective-permute-start.7 = (bf16[64,1152]{1,0:T(8,128)(2,1)S(1)}, bf16[64,1152]{1,0:T(8,128)(2,1)S(1)}, u32[]{:S(2)}, u32[]{:S(2)}) collective-permute-start(bf16[64,1152]{1,0:T(8,128)(2,1)S(1)} %collective-permute-done.5), channel_id=1, source_target_pairs={{0,128},{1,657},{128,256},{129,1},{256,384},{257,129},{384,512},{3... | collective-permute-start | bytes 442376 | tf_op jit(solution)/shard_map/ppermute | solution.py:31
  50.2 7.4 %collective-permute-start.8 = (bf16[64,1152]{1,0:T(8,128)(2,1)S(1)}, bf16[64,1152]{1,0:T(8,128)(2,1)S(1)}, u32[]{:S(2)}, u32[]{:S(2)}) collective-permute-start(bf16[64,1152]{1,0:T(8,128)(2,1)S(1)} %collective-permute-done.6), channel_id=1, source_target_pairs={{0,128},{1,657},{128,256},{129,1},{256,384},{257,129},{384,512},{3... | collective-permute-start | bytes 442376 | tf_op jit(solution)/shard_map/ppermute | solution.py:31
  55.1 7.1 %collective-permute-start.9 = (bf16[64,1152]{1,0:T(8,128)(2,1)S(1)}, bf16[64,1152]{1,0:T(8,128)(2,1)S(1)}, u32[]{:S(2)}, u32[]{:S(2)}) collective-permute-start(bf16[64,1152]{1,0:T(8,128)(2,1)S(1)} %collective-permute-done.7), channel_id=1, source_target_pairs={{0,128},{1,657},{128,256},{129,1},{256,384},{257,129},{384,512},{3... | collective-permute-start | bytes 442376 | tf_op jit(solution)/shard_map/ppermute | solution.py:31
  57.6 7.1 %collective-permute-start.10 = (bf16[64,1152]{1,0:T(8,128)(2,1)S(1)}, bf16[64,1152]{1,0:T(8,128)(2,1)S(1)}, u32[]{:S(2)}, u32[]{:S(2)}) collective-permute-start(bf16[64,1152]{1,0:T(8,128)(2,1)S(1)} %collective-permute-done.8), channel_id=1, source_target_pairs={{0,128},{1,657},{128,256},{129,1},{256,384},{257,129},{384,512},{3... | collective-permute-start | bytes 442376 | tf_op jit(solution)/shard_map/ppermute | solution.py:31
  62.2 6.2 %collective-permute-start.11 = (bf16[64,1152]{1,0:T(8,128)(2,1)S(1)}, bf16[64,1152]{1,0:T(8,128)(2,1)S(1)}, u32[]{:S(2)}, u32[]{:S(2)}) collective-permute-start(bf16[64,1152]{1,0:T(8,128)(2,1)S(1)} %collective-permute-done.9), channel_id=1, source_target_pairs={{0,128},{1,657},{128,256},{129,1},{256,384},{257,129},{384,512},{3... | collective-permute-start | bytes 442376 | tf_op jit(solution)/shard_map/ppermute | solution.py:31
  68.4 9.7 %collective-permute-start.12 = (bf16[768,1152]{1,0:T(8,128)(2,1)S(1)}, bf16[768,1152]{1,0:T(8,128)(2,1)}, u32[]{:S(2)}, u32[]{:S(2)}) collective-permute-start(bf16[768,1152]{1,0:T(8,128)(2,1)S(1)} %constant_dynamic-update-slice_fusion.2.refs_1_), channel_id=1, source_target_pairs={{0,1},{1,0},{2,3},{3,2},{4,5},{5,4},{6,7},{7,6},{8,9},{9,8},{10,11... | collective-permute-start | bytes 5308424 | tf_op jit(solution)/shard_map/ppermute | solution.py:35
  75.1 3.1 %collective-permute-start.13 = (f32[4,768]{1,0:T(4,128)S(1)}, f32[4,768]{1,0:T(4,128)S(1)}, u32[]{:S(2)}, u32[]{:S(2)}) collective-permute-start(f32[4,768]{1,0:T(4,128)S(1)} %broadcast_select_fusion.refs_3_), channel_id=1, source_target_pairs={{0,1},{1,0},{2,3},{3,2},{4,5},{5,4},{6,7},{7,6},{8,9},{9,8},{10,11... | collective-permute-start | bytes 36872 | tf_op jit(solution)/shard_map/ppermute | solution.py:35

commit v6 on v4

--- a/solution.py
+++ b/solution.py
@@ -23,13 +23,13 @@
     return gathered.reshape((count * value.shape[0],) + value.shape[1:])
 
 
-def both_ways(value, steps):
-    pairs = [
-        (y * CORE + core, (y + (steps if core == 0 else -steps)) % Y * CORE + core)
-        for y in range(Y)
-        for core in range(CORE)
-    ]
-    return lax.ppermute(value, ("y", "c"), pairs)
+def pass_on(tiles):
+    pairs = []
+    for y in range(Y):
+        for core in range(CORE):
+            to = (y + (1 if core == 0 else -1)) % Y
+            pairs.append((y * CORE + core, to * CORE + core))
+    return lax.ppermute(tiles, ("y", "c"), pairs)
 
 
 def swap_cores(value):
@@ -37,15 +37,12 @@
 
 
 def tiles_held():
-    y, core = lax.axis_index("y"), lax.axis_index("c")
-    steps = jnp.array([0, 1, 1, 2, 2, 3, 3, 4], jnp.int32)
-    flip = jnp.array([0, 0, 1, 0, 1, 0, 1, 0], jnp.int32)
-
-    def of(core):
-        behind = jnp.where(core == 0, -steps, steps)
-        return (y + behind) % Y * CORE + (core ^ flip)
-
-    return jnp.concatenate([of(core), of(1 - core)])
+    core = lax.axis_index("c")
+    place = lax.broadcasted_iota(jnp.int32, (Y,), 0)
+    steps = (place + 1) // 2
+    flip = jnp.where(place == 0, 0, 1 - place % 2)
+    y = (lax.axis_index("y") + jnp.where(core == 0, Y - steps, steps)) % Y
+    return y * CORE + (core ^ flip)
 
 
 def split3(value):
@@ -66,18 +63,19 @@
     return jnp.sum(stats.reshape(dests, rows, LANES), axis=1, keepdims=True)
 
 
-def score_kernel(queries_ref, own_ref, other_ref, bias_ref, out_ref, *, width, tile_rows, part_rows, scale):
+def score_kernel(
+    queries_ref, own_ref, other_ref, own_bias_ref, other_bias_ref, out_ref, *, width, tile_rows, part_rows, scale
+):
     rows = queries_ref.shape[0]
     lands = own_ref.shape[0]
-    tiles = bias_ref.shape[1]
+    tiles = own_bias_ref.shape[1]
     chunk = tiles * tile_rows
 
     def step(index):
         start = pl.multiple_of(index * chunk, chunk)
         queries = queries_ref[pl.ds(start, chunk), :]
-        bias = bias_ref[index]
-
-        def logits_of(land_ref, first):
+
+        def logits_of(land_ref, bias_ref):
             logits = lax.dot_general(
                 queries,
                 land_ref[:, :width],
@@ -85,10 +83,10 @@
                 preferred_element_type=jnp.float32,
             )
             logits = (logits * scale).reshape(tiles, tile_rows, lands)
-            return (logits + bias[:, None, first : first + lands]).reshape(chunk, lands)
-
-        own = logits_of(own_ref, 0)
-        other = logits_of(other_ref, lands)
+            return (logits + bias_ref[index][:, None, :]).reshape(chunk, lands)
+
+        own = logits_of(own_ref, own_bias_ref)
+        other = logits_of(other_ref, other_bias_ref)
         row_max = jnp.max(jnp.maximum(own, other), axis=1, keepdims=True)
         own = jnp.exp(own - row_max)
         other = jnp.exp(other - row_max)
@@ -108,17 +106,16 @@
     pl.loop(0, rows // chunk)(step)
 
 
-def score(queries, own, other, bias, width, tile_rows, part_rows, scale):
+def score(queries, own, other, own_bias, other_bias, width, tile_rows, part_rows, scale):
     rows = queries.shape[0]
     lands = own.shape[0] + other.shape[0]
     classes = own.shape[1] - width
-    tiles = 8
     return pl.pallas_call(
         lambda *refs: score_kernel(
             *refs, width=width, tile_rows=tile_rows, part_rows=part_rows, scale=scale
         ),
         out_shape=jax.ShapeDtypeStruct((rows // part_rows, part_rows + 8, classes), jnp.bfloat16),
-        in_specs=[VMEM] * 4,
+        in_specs=[VMEM] * 5,
         out_specs=VMEM,
         cost_estimate=pl.CostEstimate(
             flops=2 * rows * lands * (width + classes),
@@ -127,7 +124,7 @@
         ),
         compiler_params=pltpu.CompilerParams(vmem_limit_bytes=24 << 20),
         name="score",
-    )(queries, own, other, bias.reshape(rows // (tiles * tile_rows), tiles, lands))
+    )(queries, own, other, own_bias, other_bias)
 
 
 def merge_kernel(parts_ref, out_ref):
@@ -163,33 +160,38 @@
 
 def local(queries, landmarks, labels, tile_mask):
     rows, width = queries.shape
-    tile_lands, _ = labels.shape
+    tile_lands, classes = labels.shape
     scale = 4.0 / math.sqrt(width)
     mine = jnp.concatenate([landmarks, labels], axis=1)
-    pair = jnp.concatenate([mine, swap_cores(mine)], axis=0)
     gathered = gather_direct(queries, Z_AXES, Z)
-    second, first = both_ways(pair, 2), both_ways(pair, 1)
-    relayed = both_ways(jnp.concatenate([first, second[:tile_lands]], axis=0), 2)
-    own = jnp.concatenate([mine, first, second, relayed], axis=0)
-    other = swap_cores(own)
-    gathered = gather_direct(gathered, "x", X)
-
     place = lax.axis_index("zl") * X + lax.axis_index("x")
     start = (place * ZH + lax.axis_index("zh")) * (Y * CORE)
     pick = tiles_held()[None, :] == lax.broadcasted_iota(jnp.int32, (Y * CORE, 1), 0)
     listed = lax.dynamic_slice_in_dim(tile_mask, start, Y * CORE, 1).astype(jnp.float32)
     listed = listed.reshape(ZL, X, Y * CORE).transpose(1, 0, 2).reshape(X * ZL, Y * CORE)
     pick = jnp.repeat(pick.astype(jnp.float32), tile_lands, axis=1)
-    listed = jnp.dot(listed, pick, preferred_element_type=jnp.float32) > 0.5
-
-    def half_norm(land):
-        land_f = land[:, :width].astype(jnp.float32)
-        return 0.5 * jnp.sum(land_f * land_f, axis=1)
-
-    norms = jnp.concatenate([half_norm(own), half_norm(other)])
-    bias = jnp.where(listed, -scale * norms[None, :], jnp.float32(UNLISTED))
-
-    parts = score(gathered, own, other, bias, width, ZH * rows, rows, scale)
+    listed = jnp.dot(listed, pick, preferred_element_type=jnp.float32)
+
+    passing = jnp.concatenate([mine, swap_cores(mine)], axis=0)
+    own = jnp.zeros((Y * tile_lands, width + classes), jnp.bfloat16)
+    own = lax.dynamic_update_slice_in_dim(own, mine, 0, 0)
+    for hop in range(1, Y // 2 + 1):
+        if hop == 2:
+            passing, listed = lax.optimization_barrier((passing, listed))
+        if hop == Y // 2:
+            passing = passing[:tile_lands]
+        passing = pass_on(passing)
+        own = lax.dynamic_update_slice_in_dim(own, passing, (2 * hop - 1) * tile_lands, 0)
+    other = swap_cores(own)
+    gathered = gather_direct(gathered, "x", X)
+
+    own_f = own[:, :width].astype(jnp.float32)
+    half_norm = 0.5 * jnp.sum(own_f * own_f, axis=1)
+    listed = listed.reshape(X * ZL // 8, 8, Y * tile_lands) > 0.5
+    own_bias = jnp.where(listed, -scale * half_norm[None, None, :], jnp.float32(UNLISTED))
+    other_bias = swap_cores(own_bias)
+
+    parts = score(gathered, own, other, own_bias, other_bias, width, ZH * rows, rows, scale)
     parts = lax.all_to_all(parts, ("x",) + Z_AXES, 0, 0, tiled=True)
     return merge(parts, rows)
 

time: 114 us -> 111 us (0.974)
  waiting for transfers between devices: 40.1 us -> 36.9 us
  blocking collectives: 25.2 us -> 27.4 us
  other arithmetic: 2.84 us -> 1.13 us
    all_to_all x2, waiting for transfers between devices: 29.6 us -> 13.7 us  [gather_direct(): gathered = lax.all_to_all(copies, axes, 0, 0, tiled=True)]
    ppermute x3 -> x4, waiting for transfers between devices: 9.19 us -> 21.1 us  [pass_on(): return lax.ppermute(tiles, ('y', 'c'), pairs)]
    ppermute x2 -> x3, starting transfers between devices: 3.83 us -> 6.25 us  [swap_cores(): return lax.ppermute(value, 'c', [(0, 1), (1, 0)])]
    all_to_all x1, blocking collectives: 25.2 us -> 27.4 us  [local(): parts = lax.all_to_all(parts, ('x',) + Z_AXES, 0, 0, tiled=True)]
    ppermute x3 -> x4, starting transfers between devices: 11.5 us -> 9.33 us  [pass_on(): return lax.ppermute(tiles, ('y', 'c'), pairs)]
    reduce_sum x2 -> x1, other arithmetic: 1.78 us -> 0.28 us  [local(): half_norm = 0.5 * jnp.sum(own_f * own_f, axis=1)]
  transfers between devices with their start and end apart: 7 -> 9, of which waited for: 5 -> 7; matrix products, arithmetic and copies ran while one was open for 5% -> 3% of each run, Pallas kernels for 0% -> 0%
where the time goes in v6:
time: 111 us; the launch traced here: 110 us
  waiting for transfers between devices  36.9 us (33%)
  starting transfers between devices  35.6 us (32%)
  blocking collectives  27.4 us (25%)
  Pallas kernels  5.68 us (5%)
  local copies, waits for them, and re-layouts  3.38 us (3%)
  other arithmetic  1.13 us (1%)
    all_to_all x1, blocking collectives, local(): parts = lax.all_to_all(parts, ('x',) + Z_AXES, 0, 0, tiled=True)  27.4 us
    ppermute x4, waiting for transfers between devices, pass_on(): return lax.ppermute(tiles, ('y', 'c'), pairs)  21.1 us
    all_to_all x2, starting transfers between devices, gather_direct(): gathered = lax.all_to_all(copies, axes, 0, 0, tiled=True)  20 us
    all_to_all x2, waiting for transfers between devices, gather_direct(): gathered = lax.all_to_all(copies, axes, 0, 0, tiled=True)  13.7 us
    ppermute x4, starting transfers between devices, pass_on(): return lax.ppermute(tiles, ('y', 'c'), pairs)  9.33 us
    ppermute x3, starting transfers between devices, swap_cores(): return lax.ppermute(value, 'c', [(0, 1), (1, 0)])  6.25 us
    pallas_call x1, Pallas kernels, score(): pl.pallas_call(lambda *refs: score_kernel(*refs, width=width, tile_rows=t...  4.68 us
    broadcast_in_dim x2, local copies, waits for them, and re-layouts, gather_direct(): copies = jnp.broadcast_to(value[None], (count,) + value.shape)  2.93 us
  transfers between devices with their start and end apart: 9, of which 7 were waited for; matrix products, arithmetic and copies ran while one was open for 3% of the time, Pallas kernels for 0%

profile of v6, /device:TPU:2, one launch (start us, length us, event | category | flops | bytes accessed | tf_op | source)
XLA Modules:
  0.0 110.4 jit_solution(8134950415877294702)
XLA Ops:
  0.0 0.0 copy-start
  0.0 0.0 copy-start.1
  0.0 1.6 %broadcast_in_dim.33 = bf16[12,16,1024]{2,1,0:T(8,128)(2,1)} broadcast(bf16[16,1024]{1,0:T(8,128)(2,1)} %param.4), dimensions={1,2} | broadcast | bytes 425984 | tf_op jit(solution)/shard_map/broadcast_in_dim | solution.py:21
  1.6 15.2 %all-to-all-start = ((bf16[12,16,1024]{2,1,0:T(8,128)(2,1)}), bf16[12,16,1024]{2,1,0:T(8,128)(2,1)S(1)}, u32[]{:S(2)}, u32[]{:S(2)}) async-start(bf16[12,16,1024]{2,1,0:T(8,128)(2,1)} %broadcast_in_dim.33), calls=%async_computation | async-start | bytes 786432 | tf_op jit(solution)/shard_map/all_to_all | solution.py:22
  16.8 0.0 copy-done
  16.8 0.0 copy-done.1
  16.8 1.9 %collective-permute-start = (bf16[64,1152]{1,0:T(8,128)(2,1)S(1)}, bf16[64,1152]{1,0:T(8,128)(2,1)S(1)}, u32[]{:S(2)}, u32[]{:S(2)}) collective-permute-start(bf16[64,1152]{1,0:T(8,128)(2,1)S(1)} %constant_dynamic-update-slice_fusion), channel_id=1, source_target_pairs={{0,1},{1,0},{2,3},{3,2},{4,5},{5,4},{6,7},{7,6},{8,9},{9,8},{10,11... | collective-permute-start | bytes 442376 | tf_op jit(solution)/shard_map/ppermute | solution.py:36
  18.8 1.3 %collective-permute-done = bf16[64,1152]{1,0:T(8,128)(2,1)S(1)} collective-permute-done((bf16[64,1152]{1,0:T(8,128)(2,1)S(1)}, bf16[64,1152]{1,0:T(8,128)(2,1)S(1)}, u32[]{:S(2)}, u32[]{:S(2)}) %collective-permute-start) | collective-permute-done | bytes 147488 | tf_op jit(solution)/shard_map/ppermute | solution.py:36
  20.1 3.5 %collective-permute-start.1 = (bf16[128,1152]{1,0:T(8,128)(2,1)S(1)}, bf16[128,1152]{1,0:T(8,128)(2,1)S(1)}, u32[]{:S(2)}, u32[]{:S(2)}) collective-permute-start(bf16[128,1152]{1,0:T(8,128)(2,1)S(1)} %pad_maximum_fusion), channel_id=1, source_target_pairs={{0,2},{1,15},{2,4},{3,1},{4,6},{5,3},{6,8},{7,5},{8,10},{9,7},{10,... | collective-permute-start | bytes 884744 | tf_op jit(solution)/shard_map/ppermute | solution.py:32
  23.6 0.8 dynamic-slice_convert_fusion
  24.4 0.1 broadcast_in_dim.36
  24.5 0.1 reshape.71
  24.6 0.1 fusion.7
  24.7 5.4 %collective-permute-done.1 = bf16[128,1152]{1,0:T(8,128)(2,1)S(1)} collective-permute-done((bf16[128,1152]{1,0:T(8,128)(2,1)S(1)}, bf16[128,1152]{1,0:T(8,128)(2,1)S(1)}, u32[]{:S(2)}, u32[]{:S(2)}) %collective-permute-start.1) | collective-permute-done | bytes 294944 | tf_op jit(solution)/shard_map/ppermute | solution.py:32
  30.2 2.0 %collective-permute-start.2 = (bf16[128,1152]{1,0:T(8,128)(2,1)S(1)}, bf16[128,1152]{1,0:T(8,128)(2,1)S(1)}, u32[]{:S(2)}, u32[]{:S(2)}) collective-permute-start(bf16[128,1152]{1,0:T(8,128)(2,1)S(1)} %collective-permute-done.1), channel_id=1, source_target_pairs={{0,2},{1,15},{2,4},{3,1},{4,6},{5,3},{6,8},{7,5},{8,10},{9,7},{10,... | collective-permute-start | bytes 884744 | tf_op jit(solution)/shard_map/ppermute | solution.py:32
  32.2 0.1 dynamic_update_slice.15
  32.3 7.7 %collective-permute-done.2 = bf16[128,1152]{1,0:T(8,128)(2,1)S(1)} collective-permute-done((bf16[128,1152]{1,0:T(8,128)(2,1)S(1)}, bf16[128,1152]{1,0:T(8,128)(2,1)S(1)}, u32[]{:S(2)}, u32[]{:S(2)}) %collective-permute-start.2) | collective-permute-done | bytes 294944 | tf_op jit(solution)/shard_map/ppermute | solution.py:32
  40.0 1.9 %collective-permute-start.3 = (bf16[128,1152]{1,0:T(8,128)(2,1)S(1)}, bf16[128,1152]{1,0:T(8,128)(2,1)S(1)}, u32[]{:S(2)}, u32[]{:S(2)}) collective-permute-start(bf16[128,1152]{1,0:T(8,128)(2,1)S(1)} %collective-permute-done.2), channel_id=1, source_target_pairs={{0,2},{1,15},{2,4},{3,1},{4,6},{5,3},{6,8},{7,5},{8,10},{9,7},{10,... | collective-permute-start | bytes 884744 | tf_op jit(solution)/shard_map/ppermute | solution.py:32
  42.0 7.8 %collective-permute-done.3 = bf16[128,1152]{1,0:T(8,128)(2,1)S(1)} collective-permute-done((bf16[128,1152]{1,0:T(8,128)(2,1)S(1)}, bf16[128,1152]{1,0:T(8,128)(2,1)S(1)}, u32[]{:S(2)}, u32[]{:S(2)}) %collective-permute-start.3) | collective-permute-done | bytes 294944 | tf_op jit(solution)/shard_map/ppermute | solution.py:32
  49.8 1.9 %collective-permute-start.4 = (bf16[64,1152]{1,0:T(8,128)(2,1)S(1)}, bf16[64,1152]{1,0:T(8,128)(2,1)S(1)}, u32[]{:S(2)}, u32[]{:S(2)}) collective-permute-start(bf16[64,1152]{1,0:T(8,128)(2,1)S(1)} %slice.8), channel_id=1, source_target_pairs={{0,2},{1,15},{2,4},{3,1},{4,6},{5,3},{6,8},{7,5},{8,10},{9,7},{10,... | collective-permute-start | bytes 442376 | tf_op jit(solution)/shard_map/ppermute | solution.py:32
  51.8 0.0 all-to-all-done
  51.8 1.4 %broadcast_in_dim.35 = bf16[4,192,1024]{2,1,0:T(8,128)(2,1)} broadcast(bf16[192,1024]{1,0:T(8,128)(2,1)S(1)} %bitcast.11), dimensions={1,2} | broadcast | bytes 1966080 | tf_op jit(solution)/shard_map/broadcast_in_dim | solution.py:21
  53.1 4.8 %all-to-all-start.1 = ((bf16[4,192,1024]{2,1,0:T(8,128)(2,1)}), bf16[4,192,1024]{2,1,0:T(8,128)(2,1)S(1)}, u32[]{:S(2)}, u32[]{:S(2)}) async-start(bf16[4,192,1024]{2,1,0:T(8,128)(2,1)} %broadcast_in_dim.35), calls=%async_computation.1 | async-start | bytes 3145728 | tf_op jit(solution)/shard_map/all_to_all | solution.py:22
  58.0 0.1 collective-permute-done.4
  58.1 1.9 %collective-permute-start.5 = (bf16[512,1152]{1,0:T(8,128)(2,1)S(1)}, bf16[512,1152]{1,0:T(8,128)(2,1)}, u32[]{:S(2)}, u32[]{:S(2)}) collective-permute-start(bf16[512,1152]{1,0:T(8,128)(2,1)S(1)} %constant_dynamic-update-slice_fusion.2.refs_1_), channel_id=1, source_target_pairs={{0,1},{1,0},{2,3},{3,2},{4,5},{5,4},{6,7},{7,6},{8,9},{9,8},{10,11... | collective-permute-start | bytes 3538952 | tf_op jit(solution)/shard_map/ppermute | solution.py:36
  60.0 0.3 multiply_reduce_fusion
  60.3 2.4 %collective-permute-start.6 = (f32[3,8,512]{2,1,0:T(8,128)S(1)}, f32[3,8,512]{2,1,0:T(8,128)S(1)}, u32[]{:S(2)}, u32[]{:S(2)}) collective-permute-start(f32[3,8,512]{2,1,0:T(8,128)S(1)} %bitcast_select_fusion.refs_3_), channel_id=1, source_target_pairs={{0,1},{1,0},{2,3},{3,2},{4,5},{5,4},{6,7},{7,6},{8,9},{9,8},{10,11... | collective-permute-start | bytes 147464 | tf_op jit(solution)/shard_map/ppermute | solution.py:36
  62.7 0.9 collective-permute-done.6.refs_4_
  63.6 13.7 %all-to-all-done.1 = bf16[4,192,1024]{2,1,0:T(8,128)(2,1)S(1)} async-done(((bf16[4,192,1024]{2,1,0:T(8,128)(2,1)}), bf16[4,192,1024]{2,1,0:T(8,128)(2,1)S(1)}, u32[]{:S(2)}, u32[]{:S(2)}) %all-to-all-start.1) | async-done | bytes 1572896 | tf_op jit(solution)/shard_map/all_to_all | solution.py:22
  77.3 0.0 collective-permute-done.5.refs_2_
  77.3 4.7 %score.1 = bf16[48,24,128]{2,1,0:T(8,128)(2,1)S(1)} custom-call(bf16[768,1024]{1,0:T(8,128)(2,1)S(1)} %bitcast.10, bf16[512,1152]{1,0:T(8,128)(2,1)S(1)} %constant_dynamic-update-slice_fusion.2.refs_1_, bf16[512,1152]{1,0:T(8,128)(2,1)} %collective-permute-done.5.refs_2_, f32[3,8,512]{2,1,0:T(8,128)S(1)} %bitcast_select_fusion.refs_3_, ...), custom_call_target="tpu_custom_call" | custom-call | flops 1811939328 | bytes 4227072 | tf_op jit(solution)/shard_map/score/pallas_call | solution.py:113
  82.0 27.4 %all_to_all.15.parts_ref = bf16[48,24,128]{2,1,0:T(8,128)(2,1)S(1)} all-to-all(bf16[48,24,128]{2,1,0:T(8,128)(2,1)S(1)} %score.1), channel_id=1, replica_groups=mesh['zl'=6,'x'=4,'zh'=2,'y'=8,'c'=2] {'x','zl','zh'}, dimensions={0} | all-to-all | bytes 589824 | tf_op jit(solution)/shard_map/all_to_all | solution.py:195
  109.4 1.0 merge.1
  (14 shorter events, 0.2 us)
Async XLA Ops:
  0.0 16.8 %copy-start = (bf16[64,1024]{1,0:T(8,128)(2,1)S(1)}, bf16[64,1024]{1,0:T(8,128)(2,1)}, u32[]{:S(2)}) copy-start(bf16[64,1024]{1,0:T(8,128)(2,1)} %param.5) | copy-start | bytes 393220
  0.0 16.8 %copy-start.1 = (bf16[64,128]{1,0:T(8,128)(2,1)S(1)}, bf16[64,128]{1,0:T(8,128)(2,1)}, u32[]{:S(2)}) copy-start(bf16[64,128]{1,0:T(8,128)(2,1)} %param.6) | copy-start | bytes 49156
  1.6 50.2 %all-to-all-start = ((bf16[12,16,1024]{2,1,0:T(8,128)(2,1)}), bf16[12,16,1024]{2,1,0:T(8,128)(2,1)S(1)}, u32[]{:S(2)}, u32[]{:S(2)}) async-start(bf16[12,16,1024]{2,1,0:T(8,128)(2,1)} %broadcast_in_dim.33), calls=%async_computation | async-start | bytes 786432 | tf_op jit(solution)/shard_map/all_to_all | solution.py:22
  16.8 3.3 %collective-permute-start = (bf16[64,1152]{1,0:T(8,128)(2,1)S(1)}, bf16[64,1152]{1,0:T(8,128)(2,1)S(1)}, u32[]{:S(2)}, u32[]{:S(2)}) collective-permute-start(bf16[64,1152]{1,0:T(8,128)(2,1)S(1)} %constant_dynamic-update-slice_fusion), channel_id=1, source_target_pairs={{0,1},{1,0},{2,3},{3,2},{4,5},{5,4},{6,7},{7,6},{8,9},{9,8},{10,11... | collective-permute-start | bytes 442376 | tf_op jit(solution)/shard_map/ppermute | solution.py:36
  20.1 10.1 %collective-permute-start.1 = (bf16[128,1152]{1,0:T(8,128)(2,1)S(1)}, bf16[128,1152]{1,0:T(8,128)(2,1)S(1)}, u32[]{:S(2)}, u32[]{:S(2)}) collective-permute-start(bf16[128,1152]{1,0:T(8,128)(2,1)S(1)} %pad_maximum_fusion), channel_id=1, source_target_pairs={{0,2},{1,15},{2,4},{3,1},{4,6},{5,3},{6,8},{7,5},{8,10},{9,7},{10,... | collective-permute-start | bytes 884744 | tf_op jit(solution)/shard_map/ppermute | solution.py:32
  30.2 9.8 %collective-permute-start.2 = (bf16[128,1152]{1,0:T(8,128)(2,1)S(1)}, bf16[128,1152]{1,0:T(8,128)(2,1)S(1)}, u32[]{:S(2)}, u32[]{:S(2)}) collective-permute-start(bf16[128,1152]{1,0:T(8,128)(2,1)S(1)} %collective-permute-done.1), channel_id=1, source_target_pairs={{0,2},{1,15},{2,4},{3,1},{4,6},{5,3},{6,8},{7,5},{8,10},{9,7},{10,... | collective-permute-start | bytes 884744 | tf_op jit(solution)/shard_map/ppermute | solution.py:32
  40.0 9.8 %collective-permute-start.3 = (bf16[128,1152]{1,0:T(8,128)(2,1)S(1)}, bf16[128,1152]{1,0:T(8,128)(2,1)S(1)}, u32[]{:S(2)}, u32[]{:S(2)}) collective-permute-start(bf16[128,1152]{1,0:T(8,128)(2,1)S(1)} %collective-permute-done.2), channel_id=1, source_target_pairs={{0,2},{1,15},{2,4},{3,1},{4,6},{5,3},{6,8},{7,5},{8,10},{9,7},{10,... | collective-permute-start | bytes 884744 | tf_op jit(solution)/shard_map/ppermute | solution.py:32
  49.8 8.2 %collective-permute-start.4 = (bf16[64,1152]{1,0:T(8,128)(2,1)S(1)}, bf16[64,1152]{1,0:T(8,128)(2,1)S(1)}, u32[]{:S(2)}, u32[]{:S(2)}) collective-permute-start(bf16[64,1152]{1,0:T(8,128)(2,1)S(1)} %slice.8), channel_id=1, source_target_pairs={{0,2},{1,15},{2,4},{3,1},{4,6},{5,3},{6,8},{7,5},{8,10},{9,7},{10,... | collective-permute-start | bytes 442376 | tf_op jit(solution)/shard_map/ppermute | solution.py:32
  53.1 24.2 %all-to-all-start.1 = ((bf16[4,192,1024]{2,1,0:T(8,128)(2,1)}), bf16[4,192,1024]{2,1,0:T(8,128)(2,1)S(1)}, u32[]{:S(2)}, u32[]{:S(2)}) async-start(bf16[4,192,1024]{2,1,0:T(8,128)(2,1)} %broadcast_in_dim.35), calls=%async_computation.1 | async-start | bytes 3145728 | tf_op jit(solution)/shard_map/all_to_all | solution.py:22
  58.1 19.2 %collective-permute-start.5 = (bf16[512,1152]{1,0:T(8,128)(2,1)S(1)}, bf16[512,1152]{1,0:T(8,128)(2,1)}, u32[]{:S(2)}, u32[]{:S(2)}) collective-permute-start(bf16[512,1152]{1,0:T(8,128)(2,1)S(1)} %constant_dynamic-update-slice_fusion.2.refs_1_), channel_id=1, source_target_pairs={{0,1},{1,0},{2,3},{3,2},{4,5},{5,4},{6,7},{7,6},{8,9},{9,8},{10,11... | collective-permute-start | bytes 3538952 | tf_op jit(solution)/shard_map/ppermute | solution.py:36
  60.3 3.3 %collective-permute-start.6 = (f32[3,8,512]{2,1,0:T(8,128)S(1)}, f32[3,8,512]{2,1,0:T(8,128)S(1)}, u32[]{:S(2)}, u32[]{:S(2)}) collective-permute-start(f32[3,8,512]{2,1,0:T(8,128)S(1)} %bitcast_select_fusion.refs_3_), channel_id=1, source_target_pairs={{0,1},{1,0},{2,3},{3,2},{4,5},{5,4},{6,7},{7,6},{8,9},{9,8},{10,11... | collective-permute-start | bytes 147464 | tf_op jit(solution)/shard_map/ppermute | solution.py:36

commit v7 on v6

--- a/solution.py
+++ b/solution.py
@@ -23,11 +23,11 @@
     return gathered.reshape((count * value.shape[0],) + value.shape[1:])
 
 
-def pass_on(tiles):
+def send_on(tiles, chips):
     pairs = []
     for y in range(Y):
         for core in range(CORE):
-            to = (y + (1 if core == 0 else -1)) % Y
+            to = (y + (chips if core == 0 else -chips)) % Y
             pairs.append((y * CORE + core, to * CORE + core))
     return lax.ppermute(tiles, ("y", "c"), pairs)
 
@@ -172,16 +172,15 @@
     pick = jnp.repeat(pick.astype(jnp.float32), tile_lands, axis=1)
     listed = jnp.dot(listed, pick, preferred_element_type=jnp.float32)
 
-    passing = jnp.concatenate([mine, swap_cores(mine)], axis=0)
+    pair = jnp.concatenate([mine, swap_cores(mine)], axis=0)
+    first = send_on(pair, 1)
+    third = send_on(pair, 3)
+    fourth = send_on(mine, 4)
+    first, listed = lax.optimization_barrier((first, listed))
+    second = send_on(first, 1)
     own = jnp.zeros((Y * tile_lands, width + classes), jnp.bfloat16)
-    own = lax.dynamic_update_slice_in_dim(own, mine, 0, 0)
-    for hop in range(1, Y // 2 + 1):
-        if hop == 2:
-            passing, listed = lax.optimization_barrier((passing, listed))
-        if hop == Y // 2:
-            passing = passing[:tile_lands]
-        passing = pass_on(passing)
-        own = lax.dynamic_update_slice_in_dim(own, passing, (2 * hop - 1) * tile_lands, 0)
+    for place, tiles in ((0, mine), (1, first), (3, second), (5, third), (7, fourth)):
+        own = lax.dynamic_update_slice_in_dim(own, tiles, place * tile_lands, 0)
     other = swap_cores(own)
     gathered = gather_direct(gathered, "x", X)
 

time: 111 us -> 122 us (1.099)
  the two profiles are of different devices: /device:TPU:2 before, /device:TPU:8 now
where the time goes in v7:
time: 122 us; the launch traced here: 121 us
  starting transfers between devices  41.1 us (34%)
  waiting for transfers between devices  39.2 us (32%)
  blocking collectives  28.5 us (23%)
  Pallas kernels  5.68 us (5%)
  local copies, waits for them, and re-layouts  4.94 us (4%)
    all_to_all x1, blocking collectives, local(): parts = lax.all_to_all(parts, ('x',) + Z_AXES, 0, 0, tiled=True)  28.5 us
    ppermute x4, waiting for transfers between devices, send_on(): return lax.ppermute(tiles, ('y', 'c'), pairs)  20.3 us
    all_to_all x2, starting transfers between devices, gather_direct(): gathered = lax.all_to_all(copies, axes, 0, 0, tiled=True)  19.4 us
    all_to_all x2, waiting for transfers between devices, gather_direct(): gathered = lax.all_to_all(copies, axes, 0, 0, tiled=True)  17.9 us
    ppermute x4, starting transfers between devices, send_on(): return lax.ppermute(tiles, ('y', 'c'), pairs)  15.7 us
    ppermute x3, starting transfers between devices, swap_cores(): return lax.ppermute(value, 'c', [(0, 1), (1, 0)])  5.96 us
    pallas_call x1, Pallas kernels, score(): pl.pallas_call(lambda *refs: score_kernel(*refs, width=width, tile_rows=t...  4.68 us
    broadcast_in_dim x2, local copies, waits for them, and re-layouts, gather_direct(): copies = jnp.broadcast_to(value[None], (count,) + value.shape)  2.89 us
  transfers between devices with their start and end apart: 9, of which 4 were waited for; matrix products, arithmetic and copies ran while one was open for 4% of the time, Pallas kernels for 0%

profile of v7, /device:TPU:8, one launch (start us, length us, event | category | flops | bytes accessed | tf_op | source)
XLA Modules:
  0.0 120.9 jit_solution(12436934376466071858)
XLA Ops:
  0.0 0.9 constant_dynamic-update-slice_fusion.1
  0.9 0.7 constant_dynamic-update-slice_fusion
  1.6 1.9 %collective-permute-start = (bf16[64,1152]{1,0:T(8,128)(2,1)S(1)}, bf16[64,1152]{1,0:T(8,128)(2,1)S(1)}, u32[]{:S(2)}, u32[]{:S(2)}) collective-permute-start(bf16[64,1152]{1,0:T(8,128)(2,1)S(1)} %constant_dynamic-update-slice_fusion), channel_id=1, source_target_pairs={{0,1},{1,0},{2,3},{3,2},{4,5},{5,4},{6,7},{7,6},{8,9},{9,8},{10,11... | collective-permute-start | bytes 442376 | tf_op jit(solution)/shard_map/ppermute | solution.py:36
  3.6 1.5 %broadcast_in_dim.33 = bf16[12,16,1024]{2,1,0:T(8,128)(2,1)} broadcast(bf16[16,1024]{1,0:T(8,128)(2,1)} %param.4), dimensions={1,2} | broadcast | bytes 425984 | tf_op jit(solution)/shard_map/broadcast_in_dim | solution.py:21
  5.1 15.2 %all-to-all-start = ((bf16[12,16,1024]{2,1,0:T(8,128)(2,1)}), bf16[12,16,1024]{2,1,0:T(8,128)(2,1)S(1)}, u32[]{:S(2)}, u32[]{:S(2)}) async-start(bf16[12,16,1024]{2,1,0:T(8,128)(2,1)} %broadcast_in_dim.33), calls=%async_computation | async-start | bytes 786432 | tf_op jit(solution)/shard_map/all_to_all | solution.py:22
  20.3 0.0 collective-permute-done
  20.4 3.5 %collective-permute-start.1 = (bf16[128,1152]{1,0:T(8,128)(2,1)S(1)}, bf16[128,1152]{1,0:T(8,128)(2,1)S(1)}, u32[]{:S(2)}, u32[]{:S(2)}) collective-permute-start(bf16[128,1152]{1,0:T(8,128)(2,1)S(1)} %pad_maximum_fusion), channel_id=1, source_target_pairs={{0,2},{1,15},{2,4},{3,1},{4,6},{5,3},{6,8},{7,5},{8,10},{9,7},{10,... | collective-permute-start | bytes 884744 | tf_op jit(solution)/shard_map/ppermute | solution.py:32
  23.9 0.8 dynamic-slice_convert_fusion
  24.7 0.1 broadcast_in_dim.36
  24.8 0.1 reshape.71
  24.9 0.1 fusion.7
  25.0 4.0 %collective-permute-done.1 = bf16[128,1152]{1,0:T(8,128)(2,1)S(1)} collective-permute-done((bf16[128,1152]{1,0:T(8,128)(2,1)S(1)}, bf16[128,1152]{1,0:T(8,128)(2,1)S(1)}, u32[]{:S(2)}, u32[]{:S(2)}) %collective-permute-start.1) | collective-permute-done | bytes 294944 | tf_op jit(solution)/shard_map/ppermute | solution.py:32
  29.0 3.5 %collective-permute-start.2 = (bf16[128,1152]{1,0:T(8,128)(2,1)S(1)}, bf16[128,1152]{1,0:T(8,128)(2,1)S(1)}, u32[]{:S(2)}, u32[]{:S(2)}) collective-permute-start(bf16[128,1152]{1,0:T(8,128)(2,1)S(1)} %collective-permute-done.1), channel_id=1, source_target_pairs={{0,2},{1,15},{2,4},{3,1},{4,6},{5,3},{6,8},{7,5},{8,10},{9,7},{10,... | collective-permute-start | bytes 884744 | tf_op jit(solution)/shard_map/ppermute | solution.py:32
  32.5 5.9 %collective-permute-start.4 = (bf16[64,1152]{1,0:T(8,128)(2,1)S(1)}, bf16[64,1152]{1,0:T(8,128)(2,1)S(1)}, u32[]{:S(2)}, u32[]{:S(2)}) collective-permute-start(bf16[64,1152]{1,0:T(8,128)(2,1)S(1)} %constant_dynamic-update-slice_fusion), channel_id=1, source_target_pairs={{0,8},{1,9},{2,10},{3,11},{4,12},{5,13},{6,14},{7,15},{8,0},{9,1},... | collective-permute-start | bytes 442376 | tf_op jit(solution)/shard_map/ppermute | solution.py:32
  38.4 0.1 dynamic_update_slice.15
  38.5 2.8 %collective-permute-start.3 = (bf16[128,1152]{1,0:T(8,128)(2,1)S(1)}, bf16[128,1152]{1,0:T(8,128)(2,1)S(1)}, u32[]{:S(2)}, u32[]{:S(2)}) collective-permute-start(bf16[128,1152]{1,0:T(8,128)(2,1)S(1)} %pad_maximum_fusion), channel_id=1, source_target_pairs={{0,6},{1,11},{2,8},{3,13},{4,10},{5,15},{6,12},{7,1},{8,14},{9,3},... | collective-permute-start | bytes 884744 | tf_op jit(solution)/shard_map/ppermute | solution.py:32
  41.3 0.0 collective-permute-done.2
  41.4 16.3 %collective-permute-done.3 = bf16[128,1152]{1,0:T(8,128)(2,1)S(1)} collective-permute-done((bf16[128,1152]{1,0:T(8,128)(2,1)S(1)}, bf16[128,1152]{1,0:T(8,128)(2,1)S(1)}, u32[]{:S(2)}, u32[]{:S(2)}) %collective-permute-start.3) | collective-permute-done | bytes 294944 | tf_op jit(solution)/shard_map/ppermute | solution.py:32
  57.7 0.0 collective-permute-done.4
  57.8 1.9 %collective-permute-start.5 = (bf16[512,1152]{1,0:T(8,128)(2,1)S(1)}, bf16[512,1152]{1,0:T(8,128)(2,1)}, u32[]{:S(2)}, u32[]{:S(2)}) collective-permute-start(bf16[512,1152]{1,0:T(8,128)(2,1)S(1)} %constant_dynamic-update-slice_fusion.2.refs_1_), channel_id=1, source_target_pairs={{0,1},{1,0},{2,3},{3,2},{4,5},{5,4},{6,7},{7,6},{8,9},{9,8},{10,11... | collective-permute-start | bytes 3538952 | tf_op jit(solution)/shard_map/ppermute | solution.py:36
  59.7 0.0 all-to-all-done
  59.7 1.3 %broadcast_in_dim.35 = bf16[4,192,1024]{2,1,0:T(8,128)(2,1)} broadcast(bf16[192,1024]{1,0:T(8,128)(2,1)S(1)} %bitcast.11), dimensions={1,2} | broadcast | bytes 1966080 | tf_op jit(solution)/shard_map/broadcast_in_dim | solution.py:21
  61.0 4.3 %all-to-all-start.1 = ((bf16[4,192,1024]{2,1,0:T(8,128)(2,1)}), bf16[4,192,1024]{2,1,0:T(8,128)(2,1)S(1)}, u32[]{:S(2)}, u32[]{:S(2)}) async-start(bf16[4,192,1024]{2,1,0:T(8,128)(2,1)} %broadcast_in_dim.35), calls=%async_computation.1 | async-start | bytes 3145728 | tf_op jit(solution)/shard_map/all_to_all | solution.py:22
  65.3 0.3 multiply_reduce_fusion
  65.6 2.1 %collective-permute-start.6 = (f32[3,8,512]{2,1,0:T(8,128)S(1)}, f32[3,8,512]{2,1,0:T(8,128)S(1)}, u32[]{:S(2)}, u32[]{:S(2)}) collective-permute-start(f32[3,8,512]{2,1,0:T(8,128)S(1)} %bitcast_select_fusion.refs_3_), channel_id=1, source_target_pairs={{0,1},{1,0},{2,3},{3,2},{4,5},{5,4},{6,7},{7,6},{8,9},{9,8},{10,11... | collective-permute-start | bytes 147464 | tf_op jit(solution)/shard_map/ppermute | solution.py:36
  67.8 1.0 collective-permute-done.6.refs_4_
  68.8 0.0 collective-permute-done.5.refs_2_
  68.8 17.9 %all-to-all-done.1 = bf16[4,192,1024]{2,1,0:T(8,128)(2,1)S(1)} async-done(((bf16[4,192,1024]{2,1,0:T(8,128)(2,1)}), bf16[4,192,1024]{2,1,0:T(8,128)(2,1)S(1)}, u32[]{:S(2)}, u32[]{:S(2)}) %all-to-all-start.1) | async-done | bytes 1572896 | tf_op jit(solution)/shard_map/all_to_all | solution.py:22
  86.7 4.7 %score.1 = bf16[48,24,128]{2,1,0:T(8,128)(2,1)S(1)} custom-call(bf16[768,1024]{1,0:T(8,128)(2,1)S(1)} %bitcast.10, bf16[512,1152]{1,0:T(8,128)(2,1)S(1)} %constant_dynamic-update-slice_fusion.2.refs_1_, bf16[512,1152]{1,0:T(8,128)(2,1)} %collective-permute-done.5.refs_2_, f32[3,8,512]{2,1,0:T(8,128)S(1)} %bitcast_select_fusion.refs_3_, ...), custom_call_target="tpu_custom_call" | custom-call | flops 1811939328 | bytes 4227072 | tf_op jit(solution)/shard_map/score/pallas_call | solution.py:113
  91.4 28.5 %all_to_all.15.parts_ref = bf16[48,24,128]{2,1,0:T(8,128)(2,1)S(1)} all-to-all(bf16[48,24,128]{2,1,0:T(8,128)(2,1)S(1)} %score.1), channel_id=1, replica_groups=mesh['zl'=6,'x'=4,'zh'=2,'y'=8,'c'=2] {'x','zl','zh'}, dimensions={0} | all-to-all | bytes 589824 | tf_op jit(solution)/shard_map/all_to_all | solution.py:194
  119.9 1.0 merge.1
  (11 shorter events, 0.2 us)
Async XLA Ops:
  1.6 18.7 %collective-permute-start = (bf16[64,1152]{1,0:T(8,128)(2,1)S(1)}, bf16[64,1152]{1,0:T(8,128)(2,1)S(1)}, u32[]{:S(2)}, u32[]{:S(2)}) collective-permute-start(bf16[64,1152]{1,0:T(8,128)(2,1)S(1)} %constant_dynamic-update-slice_fusion), channel_id=1, source_target_pairs={{0,1},{1,0},{2,3},{3,2},{4,5},{5,4},{6,7},{7,6},{8,9},{9,8},{10,11... | collective-permute-start | bytes 442376 | tf_op jit(solution)/shard_map/ppermute | solution.py:36
  5.1 54.6 %all-to-all-start = ((bf16[12,16,1024]{2,1,0:T(8,128)(2,1)}), bf16[12,16,1024]{2,1,0:T(8,128)(2,1)S(1)}, u32[]{:S(2)}, u32[]{:S(2)}) async-start(bf16[12,16,1024]{2,1,0:T(8,128)(2,1)} %broadcast_in_dim.33), calls=%async_computation | async-start | bytes 786432 | tf_op jit(solution)/shard_map/all_to_all | solution.py:22
  20.4 8.6 %collective-permute-start.1 = (bf16[128,1152]{1,0:T(8,128)(2,1)S(1)}, bf16[128,1152]{1,0:T(8,128)(2,1)S(1)}, u32[]{:S(2)}, u32[]{:S(2)}) collective-permute-start(bf16[128,1152]{1,0:T(8,128)(2,1)S(1)} %pad_maximum_fusion), channel_id=1, source_target_pairs={{0,2},{1,15},{2,4},{3,1},{4,6},{5,3},{6,8},{7,5},{8,10},{9,7},{10,... | collective-permute-start | bytes 884744 | tf_op jit(solution)/shard_map/ppermute | solution.py:32
  29.0 12.4 %collective-permute-start.2 = (bf16[128,1152]{1,0:T(8,128)(2,1)S(1)}, bf16[128,1152]{1,0:T(8,128)(2,1)S(1)}, u32[]{:S(2)}, u32[]{:S(2)}) collective-permute-start(bf16[128,1152]{1,0:T(8,128)(2,1)S(1)} %collective-permute-done.1), channel_id=1, source_target_pairs={{0,2},{1,15},{2,4},{3,1},{4,6},{5,3},{6,8},{7,5},{8,10},{9,7},{10,... | collective-permute-start | bytes 884744 | tf_op jit(solution)/shard_map/ppermute | solution.py:32
  32.5 25.3 %collective-permute-start.4 = (bf16[64,1152]{1,0:T(8,128)(2,1)S(1)}, bf16[64,1152]{1,0:T(8,128)(2,1)S(1)}, u32[]{:S(2)}, u32[]{:S(2)}) collective-permute-start(bf16[64,1152]{1,0:T(8,128)(2,1)S(1)} %constant_dynamic-update-slice_fusion), channel_id=1, source_target_pairs={{0,8},{1,9},{2,10},{3,11},{4,12},{5,13},{6,14},{7,15},{8,0},{9,1},... | collective-permute-start | bytes 442376 | tf_op jit(solution)/shard_map/ppermute | solution.py:32
  38.5 19.2 %collective-permute-start.3 = (bf16[128,1152]{1,0:T(8,128)(2,1)S(1)}, bf16[128,1152]{1,0:T(8,128)(2,1)S(1)}, u32[]{:S(2)}, u32[]{:S(2)}) collective-permute-start(bf16[128,1152]{1,0:T(8,128)(2,1)S(1)} %pad_maximum_fusion), channel_id=1, source_target_pairs={{0,6},{1,11},{2,8},{3,13},{4,10},{5,15},{6,12},{7,1},{8,14},{9,3},... | collective-permute-start | bytes 884744 | tf_op jit(solution)/shard_map/ppermute | solution.py:32
  57.8 11.0 %collective-permute-start.5 = (bf16[512,1152]{1,0:T(8,128)(2,1)S(1)}, bf16[512,1152]{1,0:T(8,128)(2,1)}, u32[]{:S(2)}, u32[]{:S(2)}) collective-permute-start(bf16[512,1152]{1,0:T(8,128)(2,1)S(1)} %constant_dynamic-update-slice_fusion.2.refs_1_), channel_id=1, source_target_pairs={{0,1},{1,0},{2,3},{3,2},{4,5},{5,4},{6,7},{7,6},{8,9},{9,8},{10,11... | collective-permute-start | bytes 3538952 | tf_op jit(solution)/shard_map/ppermute | solution.py:36
  61.0 25.7 %all-to-all-start.1 = ((bf16[4,192,1024]{2,1,0:T(8,128)(2,1)}), bf16[4,192,1024]{2,1,0:T(8,128)(2,1)S(1)}, u32[]{:S(2)}, u32[]{:S(2)}) async-start(bf16[4,192,1024]{2,1,0:T(8,128)(2,1)} %broadcast_in_dim.35), calls=%async_computation.1 | async-start | bytes 3145728 | tf_op jit(solution)/shard_map/all_to_all | solution.py:22
  65.6 3.1 %collective-permute-start.6 = (f32[3,8,512]{2,1,0:T(8,128)S(1)}, f32[3,8,512]{2,1,0:T(8,128)S(1)}, u32[]{:S(2)}, u32[]{:S(2)}) collective-permute-start(f32[3,8,512]{2,1,0:T(8,128)S(1)} %bitcast_select_fusion.refs_3_), channel_id=1, source_target_pairs={{0,1},{1,0},{2,3},{3,2},{4,5},{5,4},{6,7},{7,6},{8,9},{9,8},{10,11... | collective-permute-start | bytes 147464 | tf_op jit(solution)/shard_map/ppermute | solution.py:36

commit v8 on v7

--- a/solution.py
+++ b/solution.py
@@ -40,6 +40,7 @@
     core = lax.axis_index("c")
     place = lax.broadcasted_iota(jnp.int32, (Y,), 0)
     steps = (place + 1) // 2
+    steps = jnp.where(steps == 3, Y - 3, steps)
     flip = jnp.where(place == 0, 0, 1 - place % 2)
     y = (lax.axis_index("y") + jnp.where(core == 0, Y - steps, steps)) % Y
     return y * CORE + (core ^ flip)
@@ -173,13 +174,13 @@
     listed = jnp.dot(listed, pick, preferred_element_type=jnp.float32)
 
     pair = jnp.concatenate([mine, swap_cores(mine)], axis=0)
+    third = send_on(pair, -3)
     first = send_on(pair, 1)
-    third = send_on(pair, 3)
+    second = send_on(pair, 2)
     fourth = send_on(mine, 4)
-    first, listed = lax.optimization_barrier((first, listed))
-    second = send_on(first, 1)
+    fourth, listed = lax.optimization_barrier((fourth, listed))
     own = jnp.zeros((Y * tile_lands, width + classes), jnp.bfloat16)
-    for place, tiles in ((0, mine), (1, first), (3, second), (5, third), (7, fourth)):
+    for place, tiles in ((0, mine), (5, third), (1, first), (3, second), (7, fourth)):
         own = lax.dynamic_update_slice_in_dim(own, tiles, place * tile_lands, 0)
     other = swap_cores(own)
     gathered = gather_direct(gathered, "x", X)

time: 122 us -> 116 us (0.951)
  waiting for transfers between devices: 39.2 us -> 32.2 us
  starting transfers between devices: 41.1 us -> 43.6 us
    ppermute x4, waiting for transfers between devices: 20.3 us -> 13.2 us  [send_on(): return lax.ppermute(tiles, ('y', 'c'), pairs)]
    ppermute x4, starting transfers between devices: 15.7 us -> 18.1 us  [send_on(): return lax.ppermute(tiles, ('y', 'c'), pairs)]
where the time goes in v8:
time: 116 us
  starting transfers between devices  43.6 us (38%)
  waiting for transfers between devices  32.2 us (28%)
  blocking collectives  28 us (24%)
  Pallas kernels  5.68 us (5%)
  local copies, waits for them, and re-layouts  4.94 us (4%)
    all_to_all x1, blocking collectives, local(): parts = lax.all_to_all(parts, ('x',) + Z_AXES, 0, 0, tiled=True)  28 us
    all_to_all x2, starting transfers between devices, gather_direct(): gathered = lax.all_to_all(copies, axes, 0, 0, tiled=True)  19.4 us
    ppermute x4, starting transfers between devices, send_on(): return lax.ppermute(tiles, ('y', 'c'), pairs)  18.1 us
    all_to_all x2, waiting for transfers between devices, gather_direct(): gathered = lax.all_to_all(copies, axes, 0, 0, tiled=True)  17.9 us
    ppermute x4, waiting for transfers between devices, send_on(): return lax.ppermute(tiles, ('y', 'c'), pairs)  13.2 us
    ppermute x3, starting transfers between devices, swap_cores(): return lax.ppermute(value, 'c', [(0, 1), (1, 0)])  5.97 us
    pallas_call x1, Pallas kernels, score(): pl.pallas_call(lambda *refs: score_kernel(*refs, width=width, tile_rows=t...  4.68 us
    broadcast_in_dim x2, local copies, waits for them, and re-layouts, gather_direct(): copies = jnp.broadcast_to(value[None], (count,) + value.shape)  2.89 us
  transfers between devices with their start and end apart: 9, of which 4 were waited for; matrix products, arithmetic and copies ran while one was open for 4% of the time, Pallas kernels for 0%

profile of v8, /device:TPU:8, one launch (start us, length us, event | category | flops | bytes accessed | tf_op | source)
XLA Modules:
  0.0 115.7 jit_solution(1702751745381923689)
XLA Ops:
  0.0 0.9 constant_dynamic-update-slice_fusion.1
  0.9 0.7 constant_dynamic-update-slice_fusion
  1.6 6.8 %collective-permute-start.4 = (bf16[64,1152]{1,0:T(8,128)(2,1)S(1)}, bf16[64,1152]{1,0:T(8,128)(2,1)S(1)}, u32[]{:S(2)}, u32[]{:S(2)}) collective-permute-start(bf16[64,1152]{1,0:T(8,128)(2,1)S(1)} %constant_dynamic-update-slice_fusion), channel_id=1, source_target_pairs={{0,8},{1,9},{2,10},{3,11},{4,12},{5,13},{6,14},{7,15},{8,0},{9,1},... | collective-permute-start | bytes 442376 | tf_op jit(solution)/shard_map/ppermute | solution.py:32
  8.5 1.9 %collective-permute-start = (bf16[64,1152]{1,0:T(8,128)(2,1)S(1)}, bf16[64,1152]{1,0:T(8,128)(2,1)S(1)}, u32[]{:S(2)}, u32[]{:S(2)}) collective-permute-start(bf16[64,1152]{1,0:T(8,128)(2,1)S(1)} %constant_dynamic-update-slice_fusion), channel_id=1, source_target_pairs={{0,1},{1,0},{2,3},{3,2},{4,5},{5,4},{6,7},{7,6},{8,9},{9,8},{10,11... | collective-permute-start | bytes 442376 | tf_op jit(solution)/shard_map/ppermute | solution.py:36
  10.4 1.5 %broadcast_in_dim.36 = bf16[12,16,1024]{2,1,0:T(8,128)(2,1)} broadcast(bf16[16,1024]{1,0:T(8,128)(2,1)} %param.4), dimensions={1,2} | broadcast | bytes 425984 | tf_op jit(solution)/shard_map/broadcast_in_dim | solution.py:21
  11.9 15.2 %all-to-all-start = ((bf16[12,16,1024]{2,1,0:T(8,128)(2,1)}), bf16[12,16,1024]{2,1,0:T(8,128)(2,1)S(1)}, u32[]{:S(2)}, u32[]{:S(2)}) async-start(bf16[12,16,1024]{2,1,0:T(8,128)(2,1)} %broadcast_in_dim.36), calls=%async_computation | async-start | bytes 786432 | tf_op jit(solution)/shard_map/all_to_all | solution.py:22
  27.2 0.0 collective-permute-done
  27.2 3.0 %collective-permute-start.1 = (bf16[128,1152]{1,0:T(8,128)(2,1)S(1)}, bf16[128,1152]{1,0:T(8,128)(2,1)S(1)}, u32[]{:S(2)}, u32[]{:S(2)}) collective-permute-start(bf16[128,1152]{1,0:T(8,128)(2,1)S(1)} %pad_maximum_fusion), channel_id=1, source_target_pairs={{0,10},{1,7},{2,12},{3,9},{4,14},{5,11},{6,0},{7,13},{8,2},{9,15},... | collective-permute-start | bytes 884744 | tf_op jit(solution)/shard_map/ppermute | solution.py:32
  30.2 0.8 dynamic-slice_convert_fusion
  31.1 0.1 broadcast_in_dim.40
  31.1 0.1 reshape.73
  31.2 3.5 %collective-permute-start.2 = (bf16[128,1152]{1,0:T(8,128)(2,1)S(1)}, bf16[128,1152]{1,0:T(8,128)(2,1)S(1)}, u32[]{:S(2)}, u32[]{:S(2)}) collective-permute-start(bf16[128,1152]{1,0:T(8,128)(2,1)S(1)} %pad_maximum_fusion), channel_id=1, source_target_pairs={{0,2},{1,15},{2,4},{3,1},{4,6},{5,3},{6,8},{7,5},{8,10},{9,7},{10,... | collective-permute-start | bytes 884744 | tf_op jit(solution)/shard_map/ppermute | solution.py:32
  34.7 0.1 fusion.7
  34.9 0.1 dynamic_update_slice.15
  35.0 4.8 %collective-permute-start.3 = (bf16[128,1152]{1,0:T(8,128)(2,1)S(1)}, bf16[128,1152]{1,0:T(8,128)(2,1)S(1)}, u32[]{:S(2)}, u32[]{:S(2)}) collective-permute-start(bf16[128,1152]{1,0:T(8,128)(2,1)S(1)} %pad_maximum_fusion), channel_id=1, source_target_pairs={{0,4},{1,13},{2,6},{3,15},{4,8},{5,1},{6,10},{7,3},{8,12},{9,5},{1... | collective-permute-start | bytes 884744 | tf_op jit(solution)/shard_map/ppermute | solution.py:32
  39.8 0.0 collective-permute-done.4
  39.8 10.1 %collective-permute-done.1 = bf16[128,1152]{1,0:T(8,128)(2,1)S(1)} collective-permute-done((bf16[128,1152]{1,0:T(8,128)(2,1)S(1)}, bf16[128,1152]{1,0:T(8,128)(2,1)S(1)}, u32[]{:S(2)}, u32[]{:S(2)}) %collective-permute-start.1) | collective-permute-done | bytes 294944 | tf_op jit(solution)/shard_map/ppermute | solution.py:32
  49.9 0.0 collective-permute-done.2
  49.9 3.1 %collective-permute-done.3 = bf16[128,1152]{1,0:T(8,128)(2,1)S(1)} collective-permute-done((bf16[128,1152]{1,0:T(8,128)(2,1)S(1)}, bf16[128,1152]{1,0:T(8,128)(2,1)S(1)}, u32[]{:S(2)}, u32[]{:S(2)}) %collective-permute-start.3) | collective-permute-done | bytes 294944 | tf_op jit(solution)/shard_map/ppermute | solution.py:32
  53.2 1.9 %collective-permute-start.5 = (bf16[512,1152]{1,0:T(8,128)(2,1)S(1)}, bf16[512,1152]{1,0:T(8,128)(2,1)}, u32[]{:S(2)}, u32[]{:S(2)}) collective-permute-start(bf16[512,1152]{1,0:T(8,128)(2,1)S(1)} %constant_dynamic-update-slice_fusion.2.refs_1_), channel_id=1, source_target_pairs={{0,1},{1,0},{2,3},{3,2},{4,5},{5,4},{6,7},{7,6},{8,9},{9,8},{10,11... | collective-permute-start | bytes 3538952 | tf_op jit(solution)/shard_map/ppermute | solution.py:36
  55.1 0.0 all-to-all-done
  55.1 1.3 %broadcast_in_dim.38 = bf16[4,192,1024]{2,1,0:T(8,128)(2,1)} broadcast(bf16[192,1024]{1,0:T(8,128)(2,1)S(1)} %bitcast.11), dimensions={1,2} | broadcast | bytes 1966080 | tf_op jit(solution)/shard_map/broadcast_in_dim | solution.py:21
  56.4 4.3 %all-to-all-start.1 = ((bf16[4,192,1024]{2,1,0:T(8,128)(2,1)}), bf16[4,192,1024]{2,1,0:T(8,128)(2,1)S(1)}, u32[]{:S(2)}, u32[]{:S(2)}) async-start(bf16[4,192,1024]{2,1,0:T(8,128)(2,1)} %broadcast_in_dim.38), calls=%async_computation.1 | async-start | bytes 3145728 | tf_op jit(solution)/shard_map/all_to_all | solution.py:22
  60.7 0.3 multiply_reduce_fusion
  61.0 2.1 %collective-permute-start.6 = (f32[3,8,512]{2,1,0:T(8,128)S(1)}, f32[3,8,512]{2,1,0:T(8,128)S(1)}, u32[]{:S(2)}, u32[]{:S(2)}) collective-permute-start(f32[3,8,512]{2,1,0:T(8,128)S(1)} %bitcast_select_fusion.refs_3_), channel_id=1, source_target_pairs={{0,1},{1,0},{2,3},{3,2},{4,5},{5,4},{6,7},{7,6},{8,9},{9,8},{10,11... | collective-permute-start | bytes 147464 | tf_op jit(solution)/shard_map/ppermute | solution.py:36
  63.2 1.0 collective-permute-done.6.refs_4_
  64.2 0.0 collective-permute-done.5.refs_2_
  64.2 17.9 %all-to-all-done.1 = bf16[4,192,1024]{2,1,0:T(8,128)(2,1)S(1)} async-done(((bf16[4,192,1024]{2,1,0:T(8,128)(2,1)}), bf16[4,192,1024]{2,1,0:T(8,128)(2,1)S(1)}, u32[]{:S(2)}, u32[]{:S(2)}) %all-to-all-start.1) | async-done | bytes 1572896 | tf_op jit(solution)/shard_map/all_to_all | solution.py:22
  82.1 4.7 %score.1 = bf16[48,24,128]{2,1,0:T(8,128)(2,1)S(1)} custom-call(bf16[768,1024]{1,0:T(8,128)(2,1)S(1)} %bitcast.10, bf16[512,1152]{1,0:T(8,128)(2,1)S(1)} %constant_dynamic-update-slice_fusion.2.refs_1_, bf16[512,1152]{1,0:T(8,128)(2,1)} %collective-permute-done.5.refs_2_, f32[3,8,512]{2,1,0:T(8,128)S(1)} %bitcast_select_fusion.refs_3_, ...), custom_call_target="tpu_custom_call" | custom-call | flops 1811939328 | bytes 4227072 | tf_op jit(solution)/shard_map/score/pallas_call | solution.py:114
  86.8 28.0 %all_to_all.15.parts_ref = bf16[48,24,128]{2,1,0:T(8,128)(2,1)S(1)} all-to-all(bf16[48,24,128]{2,1,0:T(8,128)(2,1)S(1)} %score.1), channel_id=1, replica_groups=mesh['zl'=6,'x'=4,'zh'=2,'y'=8,'c'=2] {'x','zl','zh'}, dimensions={0} | all-to-all | bytes 589824 | tf_op jit(solution)/shard_map/all_to_all | solution.py:195
  114.7 1.0 merge.1
  (11 shorter events, 0.2 us)
Async XLA Ops:
  1.6 38.1 %collective-permute-start.4 = (bf16[64,1152]{1,0:T(8,128)(2,1)S(1)}, bf16[64,1152]{1,0:T(8,128)(2,1)S(1)}, u32[]{:S(2)}, u32[]{:S(2)}) collective-permute-start(bf16[64,1152]{1,0:T(8,128)(2,1)S(1)} %constant_dynamic-update-slice_fusion), channel_id=1, source_target_pairs={{0,8},{1,9},{2,10},{3,11},{4,12},{5,13},{6,14},{7,15},{8,0},{9,1},... | collective-permute-start | bytes 442376 | tf_op jit(solution)/shard_map/ppermute | solution.py:32
  8.5 18.7 %collective-permute-start = (bf16[64,1152]{1,0:T(8,128)(2,1)S(1)}, bf16[64,1152]{1,0:T(8,128)(2,1)S(1)}, u32[]{:S(2)}, u32[]{:S(2)}) collective-permute-start(bf16[64,1152]{1,0:T(8,128)(2,1)S(1)} %constant_dynamic-update-slice_fusion), channel_id=1, source_target_pairs={{0,1},{1,0},{2,3},{3,2},{4,5},{5,4},{6,7},{7,6},{8,9},{9,8},{10,11... | collective-permute-start | bytes 442376 | tf_op jit(solution)/shard_map/ppermute | solution.py:36
  11.9 43.1 %all-to-all-start = ((bf16[12,16,1024]{2,1,0:T(8,128)(2,1)}), bf16[12,16,1024]{2,1,0:T(8,128)(2,1)S(1)}, u32[]{:S(2)}, u32[]{:S(2)}) async-start(bf16[12,16,1024]{2,1,0:T(8,128)(2,1)} %broadcast_in_dim.36), calls=%async_computation | async-start | bytes 786432 | tf_op jit(solution)/shard_map/all_to_all | solution.py:22
  27.2 22.7 %collective-permute-start.1 = (bf16[128,1152]{1,0:T(8,128)(2,1)S(1)}, bf16[128,1152]{1,0:T(8,128)(2,1)S(1)}, u32[]{:S(2)}, u32[]{:S(2)}) collective-permute-start(bf16[128,1152]{1,0:T(8,128)(2,1)S(1)} %pad_maximum_fusion), channel_id=1, source_target_pairs={{0,10},{1,7},{2,12},{3,9},{4,14},{5,11},{6,0},{7,13},{8,2},{9,15},... | collective-permute-start | bytes 884744 | tf_op jit(solution)/shard_map/ppermute | solution.py:32
  31.2 18.6 %collective-permute-start.2 = (bf16[128,1152]{1,0:T(8,128)(2,1)S(1)}, bf16[128,1152]{1,0:T(8,128)(2,1)S(1)}, u32[]{:S(2)}, u32[]{:S(2)}) collective-permute-start(bf16[128,1152]{1,0:T(8,128)(2,1)S(1)} %pad_maximum_fusion), channel_id=1, source_target_pairs={{0,2},{1,15},{2,4},{3,1},{4,6},{5,3},{6,8},{7,5},{8,10},{9,7},{10,... | collective-permute-start | bytes 884744 | tf_op jit(solution)/shard_map/ppermute | solution.py:32
  35.0 18.1 %collective-permute-start.3 = (bf16[128,1152]{1,0:T(8,128)(2,1)S(1)}, bf16[128,1152]{1,0:T(8,128)(2,1)S(1)}, u32[]{:S(2)}, u32[]{:S(2)}) collective-permute-start(bf16[128,1152]{1,0:T(8,128)(2,1)S(1)} %pad_maximum_fusion), channel_id=1, source_target_pairs={{0,4},{1,13},{2,6},{3,15},{4,8},{5,1},{6,10},{7,3},{8,12},{9,5},{1... | collective-permute-start | bytes 884744 | tf_op jit(solution)/shard_map/ppermute | solution.py:32
  53.2 11.0 %collective-permute-start.5 = (bf16[512,1152]{1,0:T(8,128)(2,1)S(1)}, bf16[512,1152]{1,0:T(8,128)(2,1)}, u32[]{:S(2)}, u32[]{:S(2)}) collective-permute-start(bf16[512,1152]{1,0:T(8,128)(2,1)S(1)} %constant_dynamic-update-slice_fusion.2.refs_1_), channel_id=1, source_target_pairs={{0,1},{1,0},{2,3},{3,2},{4,5},{5,4},{6,7},{7,6},{8,9},{9,8},{10,11... | collective-permute-start | bytes 3538952 | tf_op jit(solution)/shard_map/ppermute | solution.py:36
  56.4 25.7 %all-to-all-start.1 = ((bf16[4,192,1024]{2,1,0:T(8,128)(2,1)}), bf16[4,192,1024]{2,1,0:T(8,128)(2,1)S(1)}, u32[]{:S(2)}, u32[]{:S(2)}) async-start(bf16[4,192,1024]{2,1,0:T(8,128)(2,1)} %broadcast_in_dim.38), calls=%async_computation.1 | async-start | bytes 3145728 | tf_op jit(solution)/shard_map/all_to_all | solution.py:22
  61.0 3.1 %collective-permute-start.6 = (f32[3,8,512]{2,1,0:T(8,128)S(1)}, f32[3,8,512]{2,1,0:T(8,128)S(1)}, u32[]{:S(2)}, u32[]{:S(2)}) collective-permute-start(f32[3,8,512]{2,1,0:T(8,128)S(1)} %bitcast_select_fusion.refs_3_), channel_id=1, source_target_pairs={{0,1},{1,0},{2,3},{3,2},{4,5},{5,4},{6,7},{7,6},{8,9},{9,8},{10,11... | collective-permute-start | bytes 147464 | tf_op jit(solution)/shard_map/ppermute | solution.py:36

commit v9 on v7

--- a/solution.py
+++ b/solution.py
@@ -37,12 +37,16 @@
 
 
 def tiles_held():
-    core = lax.axis_index("c")
+    y, core = lax.axis_index("y"), lax.axis_index("c")
     place = lax.broadcasted_iota(jnp.int32, (Y,), 0)
-    steps = (place + 1) // 2
+    pair = (place + 1) // 2
+    steps = jnp.where(pair == 1, 2, jnp.where(pair == 2, Y - 3, jnp.where(pair == 3, 1, pair)))
     flip = jnp.where(place == 0, 0, 1 - place % 2)
-    y = (lax.axis_index("y") + jnp.where(core == 0, Y - steps, steps)) % Y
-    return y * CORE + (core ^ flip)
+
+    def of(core):
+        return (y + jnp.where(core == 0, Y - steps, steps)) % Y * CORE + (core ^ flip)
+
+    return jnp.concatenate([of(core), of(1 - core)])
 
 
 def split3(value):
@@ -63,60 +67,54 @@
     return jnp.sum(stats.reshape(dests, rows, LANES), axis=1, keepdims=True)
 
 
-def score_kernel(
-    queries_ref, own_ref, other_ref, own_bias_ref, other_bias_ref, out_ref, *, width, tile_rows, part_rows, scale
-):
-    rows = queries_ref.shape[0]
-    lands = own_ref.shape[0]
-    tiles = own_bias_ref.shape[1]
+def score_kernel(queries_ref, *refs, width, tile_rows, part_rows, scale):
+    *piece_refs, bias_ref, out_ref, land_ref = refs
+    lands = land_ref.shape[0]
+    tiles = bias_ref.shape[1]
     chunk = tiles * tile_rows
+    dests = chunk // part_rows
+    first = 0
+    for piece_ref in piece_refs:
+        land_ref[first : first + piece_ref.shape[0], :] = piece_ref[...]
+        first += piece_ref.shape[0]
 
     def step(index):
         start = pl.multiple_of(index * chunk, chunk)
-        queries = queries_ref[pl.ds(start, chunk), :]
-
-        def logits_of(land_ref, bias_ref):
-            logits = lax.dot_general(
-                queries,
-                land_ref[:, :width],
-                (((1,), (1,)), ((), ())),
-                preferred_element_type=jnp.float32,
-            )
-            logits = (logits * scale).reshape(tiles, tile_rows, lands)
-            return (logits + bias_ref[index][:, None, :]).reshape(chunk, lands)
-
-        own = logits_of(own_ref, own_bias_ref)
-        other = logits_of(other_ref, other_bias_ref)
-        row_max = jnp.max(jnp.maximum(own, other), axis=1, keepdims=True)
-        own = jnp.exp(own - row_max)
-        other = jnp.exp(other - row_max)
-        weight_sum = jnp.sum(own + other, axis=1, keepdims=True)
+        logits = lax.dot_general(
+            queries_ref[pl.ds(start, chunk), :],
+            land_ref[:, :width],
+            (((1,), (1,)), ((), ())),
+            preferred_element_type=jnp.float32,
+        )
+        logits = (logits * scale).reshape(tiles, tile_rows, lands) + bias_ref[index][:, None, :]
+        logits = logits.reshape(chunk, lands)
+        row_max = jnp.max(logits, axis=1, keepdims=True)
+        kernel = jnp.exp(logits - row_max)
+        weight_sum = jnp.sum(kernel, axis=1, keepdims=True)
         label_sum = jnp.dot(
-            own.astype(jnp.bfloat16), own_ref[:, width:], preferred_element_type=jnp.float32
-        ) + jnp.dot(
-            other.astype(jnp.bfloat16), other_ref[:, width:], preferred_element_type=jnp.float32
+            kernel.astype(jnp.bfloat16), land_ref[:, width:], preferred_element_type=jnp.float32
         )
-        dests = chunk // part_rows
         place = pl.ds(pl.multiple_of(index * dests, dests), dests)
         scores = (label_sum / weight_sum).astype(jnp.bfloat16)
         out_ref[place, :part_rows, :] = scores.reshape(dests, part_rows, LANES)
         stats = stats_rows(row_max, weight_sum, dests, part_rows)
         out_ref[place, part_rows:, :] = jnp.broadcast_to(stats, (dests, 8, LANES)).astype(jnp.bfloat16)
 
-    pl.loop(0, rows // chunk)(step)
-
-
-def score(queries, own, other, own_bias, other_bias, width, tile_rows, part_rows, scale):
+    pl.loop(0, queries_ref.shape[0] // chunk)(step)
+
+
+def score(queries, pieces, bias, width, tile_rows, part_rows, scale):
     rows = queries.shape[0]
-    lands = own.shape[0] + other.shape[0]
-    classes = own.shape[1] - width
+    lands = bias.shape[2]
+    classes = pieces[0].shape[1] - width
     return pl.pallas_call(
         lambda *refs: score_kernel(
             *refs, width=width, tile_rows=tile_rows, part_rows=part_rows, scale=scale
         ),
         out_shape=jax.ShapeDtypeStruct((rows // part_rows, part_rows + 8, classes), jnp.bfloat16),
-        in_specs=[VMEM] * 5,
+        in_specs=[VMEM] * (len(pieces) + 2),
         out_specs=VMEM,
+        scratch_shapes=[pltpu.VMEM((lands, width + classes), jnp.bfloat16)],
         cost_estimate=pl.CostEstimate(
             flops=2 * rows * lands * (width + classes),
             bytes_accessed=2 * (rows * width + lands * (width + classes) + rows * 192),
@@ -124,7 +122,7 @@
         ),
         compiler_params=pltpu.CompilerParams(vmem_limit_bytes=24 << 20),
         name="score",
-    )(queries, own, other, own_bias, other_bias)
+    )(queries, *pieces, bias)
 
 
 def merge_kernel(parts_ref, out_ref):
@@ -160,7 +158,7 @@
 
 def local(queries, landmarks, labels, tile_mask):
     rows, width = queries.shape
-    tile_lands, classes = labels.shape
+    tile_lands, _ = labels.shape
     scale = 4.0 / math.sqrt(width)
     mine = jnp.concatenate([landmarks, labels], axis=1)
     gathered = gather_direct(queries, Z_AXES, Z)
@@ -173,24 +171,27 @@
     listed = jnp.dot(listed, pick, preferred_element_type=jnp.float32)
 
     pair = jnp.concatenate([mine, swap_cores(mine)], axis=0)
+    second = send_on(pair, 2)
+    third = send_on(pair, -3)
+    fourth = send_on(second[:tile_lands], 2)
     first = send_on(pair, 1)
-    third = send_on(pair, 3)
-    fourth = send_on(mine, 4)
     first, listed = lax.optimization_barrier((first, listed))
-    second = send_on(first, 1)
-    own = jnp.zeros((Y * tile_lands, width + classes), jnp.bfloat16)
-    for place, tiles in ((0, mine), (1, first), (3, second), (5, third), (7, fourth)):
-        own = lax.dynamic_update_slice_in_dim(own, tiles, place * tile_lands, 0)
-    other = swap_cores(own)
+    early = jnp.concatenate([mine, second, third], axis=0)
+    late = jnp.concatenate([first, fourth], axis=0)
+    other_early = swap_cores(early)
+    other_late = swap_cores(late)
     gathered = gather_direct(gathered, "x", X)
 
-    own_f = own[:, :width].astype(jnp.float32)
-    half_norm = 0.5 * jnp.sum(own_f * own_f, axis=1)
-    listed = listed.reshape(X * ZL // 8, 8, Y * tile_lands) > 0.5
-    own_bias = jnp.where(listed, -scale * half_norm[None, None, :], jnp.float32(UNLISTED))
-    other_bias = swap_cores(own_bias)
-
-    parts = score(gathered, own, other, own_bias, other_bias, width, ZH * rows, rows, scale)
+    def half_norm(land):
+        land_f = land[:, :width].astype(jnp.float32)
+        return 0.5 * jnp.sum(land_f * land_f, axis=1)
+
+    pieces = (early, late, other_early, other_late)
+    norms = jnp.concatenate([half_norm(piece) for piece in pieces])
+    listed = listed.reshape(X * ZL // 8, 8, CORE * Y * tile_lands) > 0.5
+    bias = jnp.where(listed, -scale * norms[None, None, :], jnp.float32(UNLISTED))
+
+    parts = score(gathered, pieces, bias, width, ZH * rows, rows, scale)
     parts = lax.all_to_all(parts, ("x",) + Z_AXES, 0, 0, tiled=True)
     return merge(parts, rows)
 

time: 122 us -> 122 us (level)
  waiting for transfers between devices: 39.2 us -> 34.2 us
  other arithmetic: 1.13 us -> 4.38 us
  starting transfers between devices: 41.1 us -> 42.9 us
    ppermute x4, waiting for transfers between devices: 20.3 us -> 14.6 us  [send_on(): return lax.ppermute(tiles, ('y', 'c'), pairs)]
    ppermute x3, starting transfers between devices: 5.96 us -> 7.86 us  [swap_cores(): return lax.ppermute(value, 'c', [(0, 1), (1, 0)])]
    select_n x1, other arithmetic: 0.01 us -> 1.54 us  [local(): jnp.where(listed, -scale * norms[None, None, :], jnp.float32(UNLISTED))]
    reduce_sum x1 -> x4, other arithmetic: 0.28 us -> 1.77 us  [half_norm(): return 0.5 * jnp.sum(land_f * land_f, axis=1)]
  transfers between devices with their start and end apart: 9 -> 9, of which waited for: 4 -> 4; matrix products, arithmetic and copies ran while one was open for 4% -> 6% of each run, Pallas kernels for 0% -> 0%
where the time goes in v9:
time: 122 us; the launch traced here: 121 us
  starting transfers between devices  42.9 us (35%)
  waiting for transfers between devices  34.2 us (28%)
  blocking collectives  28.3 us (23%)
  Pallas kernels  5.58 us (5%)
  local copies, waits for them, and re-layouts  5.06 us (4%)
  other arithmetic  4.38 us (4%)
    all_to_all x1, blocking collectives, local(): parts = lax.all_to_all(parts, ('x',) + Z_AXES, 0, 0, tiled=True)  28.3 us
    all_to_all x2, starting transfers between devices, gather_direct(): gathered = lax.all_to_all(copies, axes, 0, 0, tiled=True)  19.4 us
    all_to_all x2, waiting for transfers between devices, gather_direct(): gathered = lax.all_to_all(copies, axes, 0, 0, tiled=True)  18.3 us
    ppermute x4, starting transfers between devices, send_on(): return lax.ppermute(tiles, ('y', 'c'), pairs)  15.5 us
    ppermute x4, waiting for transfers between devices, send_on(): return lax.ppermute(tiles, ('y', 'c'), pairs)  14.6 us
    ppermute x3, starting transfers between devices, swap_cores(): return lax.ppermute(value, 'c', [(0, 1), (1, 0)])  7.86 us
    pallas_call x1, Pallas kernels, score(): pl.pallas_call(lambda *refs: score_kernel(*refs, width=width, tile_rows=t...  4.59 us
    broadcast_in_dim x2, local copies, waits for them, and re-layouts, gather_direct(): copies = jnp.broadcast_to(value[None], (count,) + value.shape)  2.94 us
  transfers between devices with their start and end apart: 9, of which 4 were waited for; matrix products, arithmetic and copies ran while one was open for 6% of the time, Pallas kernels for 0%

profile of v9, /device:TPU:8, one launch (start us, length us, event | category | flops | bytes accessed | tf_op | source)
XLA Modules:
  0.0 121.3 jit_solution(6191482859733770000)
XLA Ops:
  0.0 0.0 copy-start.1
  0.0 1.6 %broadcast_in_dim.37 = bf16[12,16,1024]{2,1,0:T(8,128)(2,1)} broadcast(bf16[16,1024]{1,0:T(8,128)(2,1)} %param.4), dimensions={1,2} | broadcast | bytes 425984 | tf_op jit(solution)/shard_map/broadcast_in_dim | solution.py:21
  1.6 15.2 %all-to-all-start = ((bf16[12,16,1024]{2,1,0:T(8,128)(2,1)}), bf16[12,16,1024]{2,1,0:T(8,128)(2,1)S(1)}, u32[]{:S(2)}, u32[]{:S(2)}) async-start(bf16[12,16,1024]{2,1,0:T(8,128)(2,1)} %broadcast_in_dim.37), calls=%async_computation | async-start | bytes 786432 | tf_op jit(solution)/shard_map/all_to_all | solution.py:22
  16.7 0.9 constant_dynamic-update-slice_fusion.1
  17.7 0.0 copy-done.1
  17.7 1.9 %collective-permute-start = (bf16[64,1152]{1,0:T(8,128)(2,1)S(1)}, bf16[64,1152]{1,0:T(8,128)(2,1)S(1)}, u32[]{:S(2)}, u32[]{:S(2)}) collective-permute-start(bf16[64,1152]{1,0:T(8,128)(2,1)S(1)} %constant_dynamic-update-slice_fusion), channel_id=1, source_target_pairs={{0,1},{1,0},{2,3},{3,2},{4,5},{5,4},{6,7},{7,6},{8,9},{9,8},{10,11... | collective-permute-start | bytes 442376 | tf_op jit(solution)/shard_map/ppermute | solution.py:36
  19.7 0.1 pad_add_fusion
  19.7 1.2 collective-permute-done
  21.0 6.0 %collective-permute-start.2 = (bf16[128,1152]{1,0:T(8,128)(2,1)S(1)}, bf16[128,1152]{1,0:T(8,128)(2,1)S(1)}, u32[]{:S(2)}, u32[]{:S(2)}) collective-permute-start(bf16[128,1152]{1,0:T(8,128)(2,1)S(1)} %pad_maximum_fusion.1), channel_id=1, source_target_pairs={{0,10},{1,7},{2,12},{3,9},{4,14},{5,11},{6,0},{7,13},{8,2},{9,15},... | collective-permute-start | bytes 884744 | tf_op jit(solution)/shard_map/ppermute | solution.py:32
  27.0 1.9 %collective-permute-start.1 = (bf16[128,1152]{1,0:T(8,128)(2,1)S(1)}, bf16[128,1152]{1,0:T(8,128)(2,1)S(1)}, u32[]{:S(2)}, u32[]{:S(2)}) collective-permute-start(bf16[128,1152]{1,0:T(8,128)(2,1)S(1)} %pad_maximum_fusion.1), channel_id=1, source_target_pairs={{0,4},{1,13},{2,6},{3,15},{4,8},{5,1},{6,10},{7,3},{8,12},{9,5},{1... | collective-permute-start | bytes 884744 | tf_op jit(solution)/shard_map/ppermute | solution.py:32
  29.0 3.4 %collective-permute-start.3 = (bf16[128,1152]{1,0:T(8,128)(2,1)S(1)}, bf16[128,1152]{1,0:T(8,128)(2,1)S(1)}, u32[]{:S(2)}, u32[]{:S(2)}) collective-permute-start(bf16[128,1152]{1,0:T(8,128)(2,1)S(1)} %pad_maximum_fusion.1), channel_id=1, source_target_pairs={{0,2},{1,15},{2,4},{3,1},{4,6},{5,3},{6,8},{7,5},{8,10},{9,7},{10,... | collective-permute-start | bytes 884744 | tf_op jit(solution)/shard_map/ppermute | solution.py:32
  32.3 0.8 dynamic-slice_convert_fusion
  33.1 0.1 broadcast_in_dim.41
  33.2 0.1 reshape.47
  33.4 0.8 fusion.10
  34.1 12.5 %collective-permute-done.3 = bf16[128,1152]{1,0:T(8,128)(2,1)S(1)} collective-permute-done((bf16[128,1152]{1,0:T(8,128)(2,1)S(1)}, bf16[128,1152]{1,0:T(8,128)(2,1)S(1)}, u32[]{:S(2)}, u32[]{:S(2)}) %collective-permute-start.3) | collective-permute-done | bytes 294944 | tf_op jit(solution)/shard_map/ppermute | solution.py:32
  46.6 0.0 collective-permute-done.1
  46.7 4.2 %collective-permute-start.4 = (bf16[64,1152]{1,0:T(8,128)(2,1)S(1)}, bf16[64,1152]{1,0:T(8,128)(2,1)S(1)}, u32[]{:S(2)}, u32[]{:S(2)}) collective-permute-start(bf16[64,1152]{1,0:T(8,128)(2,1)S(1)} %slice.20), channel_id=1, source_target_pairs={{0,4},{1,13},{2,6},{3,15},{4,8},{5,1},{6,10},{7,3},{8,12},{9,5},{1... | collective-permute-start | bytes 442376 | tf_op jit(solution)/shard_map/ppermute | solution.py:32
  50.9 0.0 collective-permute-done.2
  50.9 0.1 pad_maximum_fusion.refs_1_
  51.0 4.0 %collective-permute-start.5 = (bf16[320,1152]{1,0:T(8,128)(2,1)S(1)}, bf16[320,1152]{1,0:T(8,128)(2,1)S(1)}, u32[]{:S(2)}, u32[]{:S(2)}) collective-permute-start(bf16[320,1152]{1,0:T(8,128)(2,1)S(1)} %pad_maximum_fusion.refs_1_), channel_id=1, source_target_pairs={{0,1},{1,0},{2,3},{3,2},{4,5},{5,4},{6,7},{7,6},{8,9},{9,8},{10,11... | collective-permute-start | bytes 2211848 | tf_op jit(solution)/shard_map/ppermute | solution.py:36
  55.0 0.2 multiply_reduce_fusion.1
  55.3 2.1 %collective-permute-done.4 = bf16[64,1152]{1,0:T(8,128)(2,1)S(1)} collective-permute-done((bf16[64,1152]{1,0:T(8,128)(2,1)S(1)}, bf16[64,1152]{1,0:T(8,128)(2,1)S(1)}, u32[]{:S(2)}, u32[]{:S(2)}) %collective-permute-start.4) | collective-permute-done | bytes 147488 | tf_op jit(solution)/shard_map/ppermute | solution.py:32
  57.4 1.9 %collective-permute-start.6 = (bf16[192,1152]{1,0:T(8,128)(2,1)S(1)}, bf16[192,1152]{1,0:T(8,128)(2,1)}, u32[]{:S(2)}, u32[]{:S(2)}) collective-permute-start(bf16[192,1152]{1,0:T(8,128)(2,1)S(1)} %constant_dynamic-update-slice_fusion.2.refs_2_), channel_id=1, source_target_pairs={{0,1},{1,0},{2,3},{3,2},{4,5},{5,4},{6,7},{7,6},{8,9},{9,8},{10,11... | collective-permute-start | bytes 1327112 | tf_op jit(solution)/shard_map/ppermute | solution.py:36
  59.3 0.2 multiply_reduce_fusion.3
  59.5 0.0 all-to-all-done
  59.5 1.4 %broadcast_in_dim.39 = bf16[4,192,1024]{2,1,0:T(8,128)(2,1)} broadcast(bf16[192,1024]{1,0:T(8,128)(2,1)S(1)} %bitcast.11), dimensions={1,2} | broadcast | bytes 1966080 | tf_op jit(solution)/shard_map/broadcast_in_dim | solution.py:21
  60.9 4.3 %all-to-all-start.1 = ((bf16[4,192,1024]{2,1,0:T(8,128)(2,1)}), bf16[4,192,1024]{2,1,0:T(8,128)(2,1)S(1)}, u32[]{:S(2)}, u32[]{:S(2)}) async-start(bf16[4,192,1024]{2,1,0:T(8,128)(2,1)} %broadcast_in_dim.39), calls=%async_computation.1 | async-start | bytes 3145728 | tf_op jit(solution)/shard_map/all_to_all | solution.py:22
  65.2 0.0 collective-permute-done.6.refs_4_
  65.2 1.2 multiply_reduce_fusion.2
  66.3 0.0 collective-permute-done.5.refs_3_
  66.4 0.2 multiply_reduce_fusion
  66.6 0.1 maximum_multiply_fusion
  66.7 1.5 %bitcast_select_fusion.refs_5_ = f32[3,8,1024]{2,1,0:T(8,128)} fusion(f32[24,1024]{1,0:T(8,128)} %fusion.10, f32[1024]{0:T(1024)S(1)} %maximum_multiply_fusion), kind=kLoop, calls=%fused_computation.6 | loop fusion | flops 49152 | bytes 200704 | tf_op jit(solution)/shard_map/jit(_where)/select_n | solution.py:192
  68.2 18.3 %all-to-all-done.1 = bf16[4,192,1024]{2,1,0:T(8,128)(2,1)S(1)} async-done(((bf16[4,192,1024]{2,1,0:T(8,128)(2,1)}), bf16[4,192,1024]{2,1,0:T(8,128)(2,1)S(1)}, u32[]{:S(2)}, u32[]{:S(2)}) %all-to-all-start.1) | async-done | bytes 1572896 | tf_op jit(solution)/shard_map/all_to_all | solution.py:22
  86.5 0.0 copy-start
  86.5 0.9 copy-done
  87.4 4.6 %score.1 = bf16[48,24,128]{2,1,0:T(8,128)(2,1)S(1)} custom-call(bf16[768,1024]{1,0:T(8,128)(2,1)S(1)} %bitcast.10, bf16[320,1152]{1,0:T(8,128)(2,1)S(1)} %pad_maximum_fusion.refs_1_, bf16[192,1152]{1,0:T(8,128)(2,1)S(1)} %constant_dynamic-update-slice_fusion.2.refs_2_, bf16[320,1152]{1,0:T(8,128)(2,1)S(1)} %collective-permute-done.5.refs_3_, ...), custom_call_target="tpu_custom_call" | custom-call | flops 1811939328 | bytes 4227072 | tf_op jit(solution)/shard_map/score/pallas_call | solution.py:110
  92.0 28.3 %all_to_all.15.parts_ref = bf16[48,24,128]{2,1,0:T(8,128)(2,1)S(1)} all-to-all(bf16[48,24,128]{2,1,0:T(8,128)(2,1)S(1)} %score.1), channel_id=1, replica_groups=mesh['zl'=6,'x'=4,'zh'=2,'y'=8,'c'=2] {'x','zl','zh'}, dimensions={0} | all-to-all | bytes 589824 | tf_op jit(solution)/shard_map/all_to_all | solution.py:195
  120.3 1.0 merge.1
  (13 shorter events, 0.2 us)
Async XLA Ops:
  0.0 17.7 %copy-start.1 = (bf16[64,128]{1,0:T(8,128)(2,1)S(1)}, bf16[64,128]{1,0:T(8,128)(2,1)}, u32[]{:S(2)}) copy-start(bf16[64,128]{1,0:T(8,128)(2,1)} %param.6) | copy-start | bytes 49156
  1.6 57.9 %all-to-all-start = ((bf16[12,16,1024]{2,1,0:T(8,128)(2,1)}), bf16[12,16,1024]{2,1,0:T(8,128)(2,1)S(1)}, u32[]{:S(2)}, u32[]{:S(2)}) async-start(bf16[12,16,1024]{2,1,0:T(8,128)(2,1)} %broadcast_in_dim.37), calls=%async_computation | async-start | bytes 786432 | tf_op jit(solution)/shard_map/all_to_all | solution.py:22
  17.7 3.3 %collective-permute-start = (bf16[64,1152]{1,0:T(8,128)(2,1)S(1)}, bf16[64,1152]{1,0:T(8,128)(2,1)S(1)}, u32[]{:S(2)}, u32[]{:S(2)}) collective-permute-start(bf16[64,1152]{1,0:T(8,128)(2,1)S(1)} %constant_dynamic-update-slice_fusion), channel_id=1, source_target_pairs={{0,1},{1,0},{2,3},{3,2},{4,5},{5,4},{6,7},{7,6},{8,9},{9,8},{10,11... | collective-permute-start | bytes 442376 | tf_op jit(solution)/shard_map/ppermute | solution.py:36
  21.0 29.9 %collective-permute-start.2 = (bf16[128,1152]{1,0:T(8,128)(2,1)S(1)}, bf16[128,1152]{1,0:T(8,128)(2,1)S(1)}, u32[]{:S(2)}, u32[]{:S(2)}) collective-permute-start(bf16[128,1152]{1,0:T(8,128)(2,1)S(1)} %pad_maximum_fusion.1), channel_id=1, source_target_pairs={{0,10},{1,7},{2,12},{3,9},{4,14},{5,11},{6,0},{7,13},{8,2},{9,15},... | collective-permute-start | bytes 884744 | tf_op jit(solution)/shard_map/ppermute | solution.py:32
  27.0 19.6 %collective-permute-start.1 = (bf16[128,1152]{1,0:T(8,128)(2,1)S(1)}, bf16[128,1152]{1,0:T(8,128)(2,1)S(1)}, u32[]{:S(2)}, u32[]{:S(2)}) collective-permute-start(bf16[128,1152]{1,0:T(8,128)(2,1)S(1)} %pad_maximum_fusion.1), channel_id=1, source_target_pairs={{0,4},{1,13},{2,6},{3,15},{4,8},{5,1},{6,10},{7,3},{8,12},{9,5},{1... | collective-permute-start | bytes 884744 | tf_op jit(solution)/shard_map/ppermute | solution.py:32
  29.0 17.7 %collective-permute-start.3 = (bf16[128,1152]{1,0:T(8,128)(2,1)S(1)}, bf16[128,1152]{1,0:T(8,128)(2,1)S(1)}, u32[]{:S(2)}, u32[]{:S(2)}) collective-permute-start(bf16[128,1152]{1,0:T(8,128)(2,1)S(1)} %pad_maximum_fusion.1), channel_id=1, source_target_pairs={{0,2},{1,15},{2,4},{3,1},{4,6},{5,3},{6,8},{7,5},{8,10},{9,7},{10,... | collective-permute-start | bytes 884744 | tf_op jit(solution)/shard_map/ppermute | solution.py:32
  46.7 10.7 %collective-permute-start.4 = (bf16[64,1152]{1,0:T(8,128)(2,1)S(1)}, bf16[64,1152]{1,0:T(8,128)(2,1)S(1)}, u32[]{:S(2)}, u32[]{:S(2)}) collective-permute-start(bf16[64,1152]{1,0:T(8,128)(2,1)S(1)} %slice.20), channel_id=1, source_target_pairs={{0,4},{1,13},{2,6},{3,15},{4,8},{5,1},{6,10},{7,3},{8,12},{9,5},{1... | collective-permute-start | bytes 442376 | tf_op jit(solution)/shard_map/ppermute | solution.py:32
  51.0 15.4 %collective-permute-start.5 = (bf16[320,1152]{1,0:T(8,128)(2,1)S(1)}, bf16[320,1152]{1,0:T(8,128)(2,1)S(1)}, u32[]{:S(2)}, u32[]{:S(2)}) collective-permute-start(bf16[320,1152]{1,0:T(8,128)(2,1)S(1)} %pad_maximum_fusion.refs_1_), channel_id=1, source_target_pairs={{0,1},{1,0},{2,3},{3,2},{4,5},{5,4},{6,7},{7,6},{8,9},{9,8},{10,11... | collective-permute-start | bytes 2211848 | tf_op jit(solution)/shard_map/ppermute | solution.py:36
  57.4 7.8 %collective-permute-start.6 = (bf16[192,1152]{1,0:T(8,128)(2,1)S(1)}, bf16[192,1152]{1,0:T(8,128)(2,1)}, u32[]{:S(2)}, u32[]{:S(2)}) collective-permute-start(bf16[192,1152]{1,0:T(8,128)(2,1)S(1)} %constant_dynamic-update-slice_fusion.2.refs_2_), channel_id=1, source_target_pairs={{0,1},{1,0},{2,3},{3,2},{4,5},{5,4},{6,7},{7,6},{8,9},{9,8},{10,11... | collective-permute-start | bytes 1327112 | tf_op jit(solution)/shard_map/ppermute | solution.py:36
  60.9 25.7 %all-to-all-start.1 = ((bf16[4,192,1024]{2,1,0:T(8,128)(2,1)}), bf16[4,192,1024]{2,1,0:T(8,128)(2,1)S(1)}, u32[]{:S(2)}, u32[]{:S(2)}) async-start(bf16[4,192,1024]{2,1,0:T(8,128)(2,1)} %broadcast_in_dim.39), calls=%async_computation.1 | async-start | bytes 3145728 | tf_op jit(solution)/shard_map/all_to_all | solution.py:22
  86.5 0.9 copy-start

commit v10 on v8

--- a/solution.py
+++ b/solution.py
@@ -65,46 +65,39 @@
 
 
 def score_kernel(
-    queries_ref, own_ref, other_ref, own_bias_ref, other_bias_ref, out_ref, *, width, tile_rows, part_rows, scale
+    queries_ref, own_ref, other_ref, own_bias_ref, other_bias_ref, out_ref, land_ref, *, width, tile_rows, part_rows, scale
 ):
-    rows = queries_ref.shape[0]
-    lands = own_ref.shape[0]
+    lands = land_ref.shape[0]
     tiles = own_bias_ref.shape[1]
     chunk = tiles * tile_rows
+    dests = chunk // part_rows
+    land_ref[: lands // 2, :] = own_ref[...]
+    land_ref[lands // 2 :, :] = other_ref[...]
 
     def step(index):
         start = pl.multiple_of(index * chunk, chunk)
-        queries = queries_ref[pl.ds(start, chunk), :]
-
-        def logits_of(land_ref, bias_ref):
-            logits = lax.dot_general(
-                queries,
-                land_ref[:, :width],
-                (((1,), (1,)), ((), ())),
-                preferred_element_type=jnp.float32,
-            )
-            logits = (logits * scale).reshape(tiles, tile_rows, lands)
-            return (logits + bias_ref[index][:, None, :]).reshape(chunk, lands)
-
-        own = logits_of(own_ref, own_bias_ref)
-        other = logits_of(other_ref, other_bias_ref)
-        row_max = jnp.max(jnp.maximum(own, other), axis=1, keepdims=True)
-        own = jnp.exp(own - row_max)
-        other = jnp.exp(other - row_max)
-        weight_sum = jnp.sum(own + other, axis=1, keepdims=True)
+        logits = lax.dot_general(
+            queries_ref[pl.ds(start, chunk), :],
+            land_ref[:, :width],
+            (((1,), (1,)), ((), ())),
+            preferred_element_type=jnp.float32,
+        )
+        bias = jnp.concatenate([own_bias_ref[index], other_bias_ref[index]], axis=1)
+        logits = (logits * scale).reshape(tiles, tile_rows, lands) + bias[:, None, :]
+        logits = logits.reshape(chunk, lands)
+        row_max = jnp.max(logits, axis=1, keepdims=True)
+        kernel = jnp.exp(logits - row_max)
+        weight_sum = jnp.sum(kernel, axis=1, keepdims=True)
         label_sum = jnp.dot(
-            own.astype(jnp.bfloat16), own_ref[:, width:], preferred_element_type=jnp.float32
-        ) + jnp.dot(
-            other.astype(jnp.bfloat16), other_ref[:, width:], preferred_element_type=jnp.float32
+            kernel.astype(jnp.bfloat16), land_ref[:, width:], preferred_element_type=jnp.float32
         )
-        dests = chunk // part_rows
         place = pl.ds(pl.multiple_of(index * dests, dests), dests)
         scores = (label_sum / weight_sum).astype(jnp.bfloat16)
         out_ref[place, :part_rows, :] = scores.reshape(dests, part_rows, LANES)
         stats = stats_rows(row_max, weight_sum, dests, part_rows)
         out_ref[place, part_rows:, :] = jnp.broadcast_to(stats, (dests, 8, LANES)).astype(jnp.bfloat16)
 
-    pl.loop(0, rows // chunk)(step)
+    pl.loop(0, queries_ref.shape[0] // chunk)(step)
 
 
 def score(queries, own, other, own_bias, other_bias, width, tile_rows, part_rows, scale):
@@ -118,12 +111,13 @@
         out_shape=jax.ShapeDtypeStruct((rows // part_rows, part_rows + 8, classes), jnp.bfloat16),
         in_specs=[VMEM] * 5,
         out_specs=VMEM,
+        scratch_shapes=[pltpu.VMEM((lands, width + classes), jnp.bfloat16)],
         cost_estimate=pl.CostEstimate(
             flops=2 * rows * lands * (width + classes),
             bytes_accessed=2 * (rows * width + lands * (width + classes) + rows * 192),
             transcendentals=rows * lands,
         ),
-        compiler_params=pltpu.CompilerParams(vmem_limit_bytes=24 << 20),
+        compiler_params=pltpu.CompilerParams(vmem_limit_bytes=20 << 20),
         name="score",
     )(queries, own, other, own_bias, other_bias)
 
@@ -177,10 +171,10 @@
     third = send_on(pair, -3)
     first = send_on(pair, 1)
     second = send_on(pair, 2)
-    fourth = send_on(mine, 4)
+    fourth = send_on(second[:tile_lands], 2)
     fourth, listed = lax.optimization_barrier((fourth, listed))
     own = jnp.zeros((Y * tile_lands, width + classes), jnp.bfloat16)
-    for place, tiles in ((0, mine), (5, third), (1, first), (3, second), (7, fourth)):
+    for place, tiles in ((0, mine), (3, second), (5, third), (1, first), (7, fourth)):
         own = lax.dynamic_update_slice_in_dim(own, tiles, place * tile_lands, 0)
     other = swap_cores(own)
     gathered = gather_direct(gathered, "x", X)

time: 116 us -> 114 us (0.983)
  the two profiles are of different devices: /device:TPU:8 before, /device:TPU:2 now
where the time goes in v10:
time: 114 us; the launch traced here: 113 us
  starting transfers between devices  46.6 us (41%)
  blocking collectives  28 us (25%)
  waiting for transfers between devices  26.4 us (23%)
  Pallas kernels  5.84 us (5%)
  local copies, waits for them, and re-layouts  4.95 us (4%)
    all_to_all x1, blocking collectives, local(): parts = lax.all_to_all(parts, ('x',) + Z_AXES, 0, 0, tiled=True)  28 us
    ppermute x4, starting transfers between devices, send_on(): return lax.ppermute(tiles, ('y', 'c'), pairs)  20.8 us
    all_to_all x2, starting transfers between devices, gather_direct(): gathered = lax.all_to_all(copies, axes, 0, 0, tiled=True)  20 us
    all_to_all x2, waiting for transfers between devices, gather_direct(): gathered = lax.all_to_all(copies, axes, 0, 0, tiled=True)  16.5 us
    ppermute x4, waiting for transfers between devices, send_on(): return lax.ppermute(tiles, ('y', 'c'), pairs)  8.67 us
    ppermute x3, starting transfers between devices, swap_cores(): return lax.ppermute(value, 'c', [(0, 1), (1, 0)])  5.75 us
    pallas_call x1, Pallas kernels, score(): pl.pallas_call(lambda *refs: score_kernel(*refs, width=width, tile_rows=t...  4.84 us
    broadcast_in_dim x2, local copies, waits for them, and re-layouts, gather_direct(): copies = jnp.broadcast_to(value[None], (count,) + value.shape)  2.89 us
  transfers between devices with their start and end apart: 9, of which 5 were waited for; matrix products, arithmetic and copies ran while one was open for 4% of the time, Pallas kernels for 0%

profile of v10, /device:TPU:2, one launch (start us, length us, event | category | flops | bytes accessed | tf_op | source)
XLA Modules:
  0.0 113.2 jit_solution(2098825960088808484)
XLA Ops:
  0.0 0.9 constant_dynamic-update-slice_fusion.1
  0.9 0.7 constant_dynamic-update-slice_fusion
  1.6 1.9 %collective-permute-start = (bf16[64,1152]{1,0:T(8,128)(2,1)S(1)}, bf16[64,1152]{1,0:T(8,128)(2,1)S(1)}, u32[]{:S(2)}, u32[]{:S(2)}) collective-permute-start(bf16[64,1152]{1,0:T(8,128)(2,1)S(1)} %constant_dynamic-update-slice_fusion), channel_id=1, source_target_pairs={{0,1},{1,0},{2,3},{3,2},{4,5},{5,4},{6,7},{7,6},{8,9},{9,8},{10,11... | collective-permute-start | bytes 442376 | tf_op jit(solution)/shard_map/ppermute | solution.py:36
  3.6 1.5 %broadcast_in_dim.36 = bf16[12,16,1024]{2,1,0:T(8,128)(2,1)} broadcast(bf16[16,1024]{1,0:T(8,128)(2,1)} %param.4), dimensions={1,2} | broadcast | bytes 425984 | tf_op jit(solution)/shard_map/broadcast_in_dim | solution.py:21
  5.1 15.2 %all-to-all-start = ((bf16[12,16,1024]{2,1,0:T(8,128)(2,1)}), bf16[12,16,1024]{2,1,0:T(8,128)(2,1)S(1)}, u32[]{:S(2)}, u32[]{:S(2)}) async-start(bf16[12,16,1024]{2,1,0:T(8,128)(2,1)} %broadcast_in_dim.36), calls=%async_computation | async-start | bytes 786432 | tf_op jit(solution)/shard_map/all_to_all | solution.py:22
  20.3 0.0 collective-permute-done
  20.4 4.5 %collective-permute-start.1 = (bf16[128,1152]{1,0:T(8,128)(2,1)S(1)}, bf16[128,1152]{1,0:T(8,128)(2,1)S(1)}, u32[]{:S(2)}, u32[]{:S(2)}) collective-permute-start(bf16[128,1152]{1,0:T(8,128)(2,1)S(1)} %pad_maximum_fusion), channel_id=1, source_target_pairs={{0,4},{1,13},{2,6},{3,15},{4,8},{5,1},{6,10},{7,3},{8,12},{9,5},{1... | collective-permute-start | bytes 884744 | tf_op jit(solution)/shard_map/ppermute | solution.py:32
  24.9 0.8 dynamic-slice_convert_fusion
  25.7 0.1 broadcast_in_dim.40
  25.8 0.1 reshape.73
  25.9 5.1 %collective-permute-start.2 = (bf16[128,1152]{1,0:T(8,128)(2,1)S(1)}, bf16[128,1152]{1,0:T(8,128)(2,1)S(1)}, u32[]{:S(2)}, u32[]{:S(2)}) collective-permute-start(bf16[128,1152]{1,0:T(8,128)(2,1)S(1)} %pad_maximum_fusion), channel_id=1, source_target_pairs={{0,10},{1,7},{2,12},{3,9},{4,14},{5,11},{6,0},{7,13},{8,2},{9,15},... | collective-permute-start | bytes 884744 | tf_op jit(solution)/shard_map/ppermute | solution.py:32
  31.0 0.1 fusion.7
  31.2 0.1 dynamic_update_slice.15
  31.2 1.9 %collective-permute-start.3 = (bf16[128,1152]{1,0:T(8,128)(2,1)S(1)}, bf16[128,1152]{1,0:T(8,128)(2,1)S(1)}, u32[]{:S(2)}, u32[]{:S(2)}) collective-permute-start(bf16[128,1152]{1,0:T(8,128)(2,1)S(1)} %pad_maximum_fusion), channel_id=1, source_target_pairs={{0,2},{1,15},{2,4},{3,1},{4,6},{5,3},{6,8},{7,5},{8,10},{9,7},{10,... | collective-permute-start | bytes 884744 | tf_op jit(solution)/shard_map/ppermute | solution.py:32
  33.2 0.0 collective-permute-done.1
  33.2 9.3 %collective-permute-start.4 = (bf16[64,1152]{1,0:T(8,128)(2,1)S(1)}, bf16[64,1152]{1,0:T(8,128)(2,1)S(1)}, u32[]{:S(2)}, u32[]{:S(2)}) collective-permute-start(bf16[64,1152]{1,0:T(8,128)(2,1)S(1)} %slice.8), channel_id=1, source_target_pairs={{0,4},{1,13},{2,6},{3,15},{4,8},{5,1},{6,10},{7,3},{8,12},{9,5},{1... | collective-permute-start | bytes 442376 | tf_op jit(solution)/shard_map/ppermute | solution.py:32
  42.5 3.0 %collective-permute-done.2 = bf16[128,1152]{1,0:T(8,128)(2,1)S(1)} collective-permute-done((bf16[128,1152]{1,0:T(8,128)(2,1)S(1)}, bf16[128,1152]{1,0:T(8,128)(2,1)S(1)}, u32[]{:S(2)}, u32[]{:S(2)}) %collective-permute-start.2) | collective-permute-done | bytes 294944 | tf_op jit(solution)/shard_map/ppermute | solution.py:32
  45.5 1.3 %collective-permute-done.3 = bf16[128,1152]{1,0:T(8,128)(2,1)S(1)} collective-permute-done((bf16[128,1152]{1,0:T(8,128)(2,1)S(1)}, bf16[128,1152]{1,0:T(8,128)(2,1)S(1)}, u32[]{:S(2)}, u32[]{:S(2)}) %collective-permute-start.3) | collective-permute-done | bytes 294944 | tf_op jit(solution)/shard_map/ppermute | solution.py:32
  46.8 4.4 %collective-permute-done.4 = bf16[64,1152]{1,0:T(8,128)(2,1)S(1)} collective-permute-done((bf16[64,1152]{1,0:T(8,128)(2,1)S(1)}, bf16[64,1152]{1,0:T(8,128)(2,1)S(1)}, u32[]{:S(2)}, u32[]{:S(2)}) %collective-permute-start.4) | collective-permute-done | bytes 147488 | tf_op jit(solution)/shard_map/ppermute | solution.py:32
  51.3 1.9 %collective-permute-start.5 = (bf16[512,1152]{1,0:T(8,128)(2,1)S(1)}, bf16[512,1152]{1,0:T(8,128)(2,1)}, u32[]{:S(2)}, u32[]{:S(2)}) collective-permute-start(bf16[512,1152]{1,0:T(8,128)(2,1)S(1)} %constant_dynamic-update-slice_fusion.2.refs_1_), channel_id=1, source_target_pairs={{0,1},{1,0},{2,3},{3,2},{4,5},{5,4},{6,7},{7,6},{8,9},{9,8},{10,11... | collective-permute-start | bytes 3538952 | tf_op jit(solution)/shard_map/ppermute | solution.py:36
  53.2 0.0 all-to-all-done
  53.2 1.3 %broadcast_in_dim.38 = bf16[4,192,1024]{2,1,0:T(8,128)(2,1)} broadcast(bf16[192,1024]{1,0:T(8,128)(2,1)S(1)} %bitcast.11), dimensions={1,2} | broadcast | bytes 1966080 | tf_op jit(solution)/shard_map/broadcast_in_dim | solution.py:21
  54.6 4.8 %all-to-all-start.1 = ((bf16[4,192,1024]{2,1,0:T(8,128)(2,1)}), bf16[4,192,1024]{2,1,0:T(8,128)(2,1)S(1)}, u32[]{:S(2)}, u32[]{:S(2)}) async-start(bf16[4,192,1024]{2,1,0:T(8,128)(2,1)} %broadcast_in_dim.38), calls=%async_computation.1 | async-start | bytes 3145728 | tf_op jit(solution)/shard_map/all_to_all | solution.py:22
  59.4 0.3 multiply_reduce_fusion
  59.7 1.9 %collective-permute-start.6 = (f32[3,8,512]{2,1,0:T(8,128)S(1)}, f32[3,8,512]{2,1,0:T(8,128)S(1)}, u32[]{:S(2)}, u32[]{:S(2)}) collective-permute-start(f32[3,8,512]{2,1,0:T(8,128)S(1)} %bitcast_select_fusion.refs_3_), channel_id=1, source_target_pairs={{0,1},{1,0},{2,3},{3,2},{4,5},{5,4},{6,7},{7,6},{8,9},{9,8},{10,11... | collective-permute-start | bytes 147464 | tf_op jit(solution)/shard_map/ppermute | solution.py:36
  61.6 1.2 %collective-permute-done.6.refs_4_ = f32[3,8,512]{2,1,0:T(8,128)S(1)} collective-permute-done((f32[3,8,512]{2,1,0:T(8,128)S(1)}, f32[3,8,512]{2,1,0:T(8,128)S(1)}, u32[]{:S(2)}, u32[]{:S(2)}) %collective-permute-start.6) | collective-permute-done | bytes 49184 | tf_op jit(solution)/shard_map/ppermute | solution.py:36
  62.8 0.0 collective-permute-done.5.refs_2_
  62.8 16.5 %all-to-all-done.1 = bf16[4,192,1024]{2,1,0:T(8,128)(2,1)S(1)} async-done(((bf16[4,192,1024]{2,1,0:T(8,128)(2,1)}), bf16[4,192,1024]{2,1,0:T(8,128)(2,1)S(1)}, u32[]{:S(2)}, u32[]{:S(2)}) %all-to-all-start.1) | async-done | bytes 1572896 | tf_op jit(solution)/shard_map/all_to_all | solution.py:22
  79.3 4.8 %score.1 = bf16[48,24,128]{2,1,0:T(8,128)(2,1)S(1)} custom-call(bf16[768,1024]{1,0:T(8,128)(2,1)S(1)} %bitcast.10, bf16[512,1152]{1,0:T(8,128)(2,1)S(1)} %constant_dynamic-update-slice_fusion.2.refs_1_, bf16[512,1152]{1,0:T(8,128)(2,1)} %collective-permute-done.5.refs_2_, f32[3,8,512]{2,1,0:T(8,128)S(1)} %bitcast_select_fusion.refs_3_, ...), custom_call_target="tpu_custom_call" | custom-call | flops 1811939328 | bytes 4227072 | tf_op jit(solution)/shard_map/score/pallas_call | solution.py:107
  84.2 28.0 %all_to_all.15.parts_ref = bf16[48,24,128]{2,1,0:T(8,128)(2,1)S(1)} all-to-all(bf16[48,24,128]{2,1,0:T(8,128)(2,1)S(1)} %score.1), channel_id=1, replica_groups=mesh['zl'=6,'x'=4,'zh'=2,'y'=8,'c'=2] {'x','zl','zh'}, dimensions={0} | all-to-all | bytes 589824 | tf_op jit(solution)/shard_map/all_to_all | solution.py:189
  112.2 1.0 merge.1
  (12 shorter events, 0.2 us)
Async XLA Ops:
  1.6 18.7 %collective-permute-start = (bf16[64,1152]{1,0:T(8,128)(2,1)S(1)}, bf16[64,1152]{1,0:T(8,128)(2,1)S(1)}, u32[]{:S(2)}, u32[]{:S(2)}) collective-permute-start(bf16[64,1152]{1,0:T(8,128)(2,1)S(1)} %constant_dynamic-update-slice_fusion), channel_id=1, source_target_pairs={{0,1},{1,0},{2,3},{3,2},{4,5},{5,4},{6,7},{7,6},{8,9},{9,8},{10,11... | collective-permute-start | bytes 442376 | tf_op jit(solution)/shard_map/ppermute | solution.py:36
  5.1 48.1 %all-to-all-start = ((bf16[12,16,1024]{2,1,0:T(8,128)(2,1)}), bf16[12,16,1024]{2,1,0:T(8,128)(2,1)S(1)}, u32[]{:S(2)}, u32[]{:S(2)}) async-start(bf16[12,16,1024]{2,1,0:T(8,128)(2,1)} %broadcast_in_dim.36), calls=%async_computation | async-start | bytes 786432 | tf_op jit(solution)/shard_map/all_to_all | solution.py:22
  20.4 12.8 %collective-permute-start.1 = (bf16[128,1152]{1,0:T(8,128)(2,1)S(1)}, bf16[128,1152]{1,0:T(8,128)(2,1)S(1)}, u32[]{:S(2)}, u32[]{:S(2)}) collective-permute-start(bf16[128,1152]{1,0:T(8,128)(2,1)S(1)} %pad_maximum_fusion), channel_id=1, source_target_pairs={{0,4},{1,13},{2,6},{3,15},{4,8},{5,1},{6,10},{7,3},{8,12},{9,5},{1... | collective-permute-start | bytes 884744 | tf_op jit(solution)/shard_map/ppermute | solution.py:32
  25.9 19.6 %collective-permute-start.2 = (bf16[128,1152]{1,0:T(8,128)(2,1)S(1)}, bf16[128,1152]{1,0:T(8,128)(2,1)S(1)}, u32[]{:S(2)}, u32[]{:S(2)}) collective-permute-start(bf16[128,1152]{1,0:T(8,128)(2,1)S(1)} %pad_maximum_fusion), channel_id=1, source_target_pairs={{0,10},{1,7},{2,12},{3,9},{4,14},{5,11},{6,0},{7,13},{8,2},{9,15},... | collective-permute-start | bytes 884744 | tf_op jit(solution)/shard_map/ppermute | solution.py:32
  31.2 15.5 %collective-permute-start.3 = (bf16[128,1152]{1,0:T(8,128)(2,1)S(1)}, bf16[128,1152]{1,0:T(8,128)(2,1)S(1)}, u32[]{:S(2)}, u32[]{:S(2)}) collective-permute-start(bf16[128,1152]{1,0:T(8,128)(2,1)S(1)} %pad_maximum_fusion), channel_id=1, source_target_pairs={{0,2},{1,15},{2,4},{3,1},{4,6},{5,3},{6,8},{7,5},{8,10},{9,7},{10,... | collective-permute-start | bytes 884744 | tf_op jit(solution)/shard_map/ppermute | solution.py:32
  33.2 18.1 %collective-permute-start.4 = (bf16[64,1152]{1,0:T(8,128)(2,1)S(1)}, bf16[64,1152]{1,0:T(8,128)(2,1)S(1)}, u32[]{:S(2)}, u32[]{:S(2)}) collective-permute-start(bf16[64,1152]{1,0:T(8,128)(2,1)S(1)} %slice.8), channel_id=1, source_target_pairs={{0,4},{1,13},{2,6},{3,15},{4,8},{5,1},{6,10},{7,3},{8,12},{9,5},{1... | collective-permute-start | bytes 442376 | tf_op jit(solution)/shard_map/ppermute | solution.py:32
  51.3 11.5 %collective-permute-start.5 = (bf16[512,1152]{1,0:T(8,128)(2,1)S(1)}, bf16[512,1152]{1,0:T(8,128)(2,1)}, u32[]{:S(2)}, u32[]{:S(2)}) collective-permute-start(bf16[512,1152]{1,0:T(8,128)(2,1)S(1)} %constant_dynamic-update-slice_fusion.2.refs_1_), channel_id=1, source_target_pairs={{0,1},{1,0},{2,3},{3,2},{4,5},{5,4},{6,7},{7,6},{8,9},{9,8},{10,11... | collective-permute-start | bytes 3538952 | tf_op jit(solution)/shard_map/ppermute | solution.py:36
  54.6 24.7 %all-to-all-start.1 = ((bf16[4,192,1024]{2,1,0:T(8,128)(2,1)}), bf16[4,192,1024]{2,1,0:T(8,128)(2,1)S(1)}, u32[]{:S(2)}, u32[]{:S(2)}) async-start(bf16[4,192,1024]{2,1,0:T(8,128)(2,1)} %broadcast_in_dim.38), calls=%async_computation.1 | async-start | bytes 3145728 | tf_op jit(solution)/shard_map/all_to_all | solution.py:22
  59.7 3.1 %collective-permute-start.6 = (f32[3,8,512]{2,1,0:T(8,128)S(1)}, f32[3,8,512]{2,1,0:T(8,128)S(1)}, u32[]{:S(2)}, u32[]{:S(2)}) collective-permute-start(f32[3,8,512]{2,1,0:T(8,128)S(1)} %bitcast_select_fusion.refs_3_), channel_id=1, source_target_pairs={{0,1},{1,0},{2,3},{3,2},{4,5},{5,4},{6,7},{7,6},{8,9},{9,8},{10,11... | collective-permute-start | bytes 147464 | tf_op jit(solution)/shard_map/ppermute | solution.py:36

commit v11 on v10

--- a/solution.py
+++ b/solution.py
@@ -15,6 +15,7 @@
 UNLISTED = -1e30
 LANES = 128
 VMEM = pl.BlockSpec(memory_space=pltpu.VMEM)
+ANYWHERE = pl.BlockSpec(memory_space=pl.ANY)
 
 
 def gather_direct(value, axes, count):
@@ -65,14 +66,20 @@
 
 
 def score_kernel(
-    queries_ref, own_ref, other_ref, own_bias_ref, other_bias_ref, out_ref, land_ref, *, width, tile_rows, part_rows, scale
+    queries_ref, own_ref, other_ref, own_bias_ref, other_bias_ref, out_ref, land_ref, sems, *, width, tile_rows, part_rows, scale
 ):
     lands = land_ref.shape[0]
     tiles = own_bias_ref.shape[1]
     chunk = tiles * tile_rows
     dests = chunk // part_rows
-    land_ref[: lands // 2, :] = own_ref[...]
-    land_ref[lands // 2 :, :] = other_ref[...]
+    copies = [
+        pltpu.make_async_copy(piece, land_ref.at[pl.ds(half * (lands // 2), lands // 2), :], sems.at[half])
+        for half, piece in enumerate((own_ref, other_ref))
+    ]
+    for copy in copies:
+        copy.start()
+    for copy in copies:
+        copy.wait()
 
     def step(index):
         start = pl.multiple_of(index * chunk, chunk)
@@ -109,9 +116,12 @@
             *refs, width=width, tile_rows=tile_rows, part_rows=part_rows, scale=scale
         ),
         out_shape=jax.ShapeDtypeStruct((rows // part_rows, part_rows + 8, classes), jnp.bfloat16),
-        in_specs=[VMEM] * 5,
+        in_specs=[VMEM, ANYWHERE, ANYWHERE, VMEM, VMEM],
         out_specs=VMEM,
-        scratch_shapes=[pltpu.VMEM((lands, width + classes), jnp.bfloat16)],
+        scratch_shapes=[
+            pltpu.VMEM((lands, width + classes), jnp.bfloat16),
+            pltpu.SemaphoreType.DMA((2,)),
+        ],
         cost_estimate=pl.CostEstimate(
             flops=2 * rows * lands * (width + classes),
             bytes_accessed=2 * (rows * width + lands * (width + classes) + rows * 192),
@@ -172,9 +182,9 @@
     first = send_on(pair, 1)
     second = send_on(pair, 2)
     fourth = send_on(second[:tile_lands], 2)
-    fourth, listed = lax.optimization_barrier((fourth, listed))
+    first, listed = lax.optimization_barrier((first, listed))
     own = jnp.zeros((Y * tile_lands, width + classes), jnp.bfloat16)
-    for place, tiles in ((0, mine), (3, second), (5, third), (1, first), (7, fourth)):
+    for place, tiles in ((0, mine), (3, second), (5, third), (7, fourth), (1, first)):
         own = lax.dynamic_update_slice_in_dim(own, tiles, place * tile_lands, 0)
     other = swap_cores(own)
     gathered = gather_direct(gathered, "x", X)

time: 114 us -> 118 us (1.035)
  the two profiles are of different devices: /device:TPU:2 before, /device:TPU:8 now
where the time goes in v11:
time: 118 us; the launch traced here: 117 us
  starting transfers between devices  42 us (36%)
  waiting for transfers between devices  34.1 us (29%)
  blocking collectives  28.5 us (24%)
  Pallas kernels  5.93 us (5%)
  local copies, waits for them, and re-layouts  4.95 us (4%)
    all_to_all x1, blocking collectives, local(): parts = lax.all_to_all(parts, ('x',) + Z_AXES, 0, 0, tiled=True)  28.5 us
    all_to_all x2, starting transfers between devices, gather_direct(): gathered = lax.all_to_all(copies, axes, 0, 0, tiled=True)  19.4 us
    all_to_all x2, waiting for transfers between devices, gather_direct(): gathered = lax.all_to_all(copies, axes, 0, 0, tiled=True)  17.9 us
    ppermute x4, starting transfers between devices, send_on(): return lax.ppermute(tiles, ('y', 'c'), pairs)  16.6 us
    ppermute x4, waiting for transfers between devices, send_on(): return lax.ppermute(tiles, ('y', 'c'), pairs)  15.1 us
    ppermute x3, starting transfers between devices, swap_cores(): return lax.ppermute(value, 'c', [(0, 1), (1, 0)])  5.96 us
    pallas_call x1, Pallas kernels, score(): pl.pallas_call(lambda *refs: score_kernel(*refs, width=width, tile_rows=t...  4.93 us
    broadcast_in_dim x2, local copies, waits for them, and re-layouts, gather_direct(): copies = jnp.broadcast_to(value[None], (count,) + value.shape)  2.89 us
  transfers between devices with their start and end apart: 9, of which 4 were waited for; matrix products, arithmetic and copies ran while one was open for 4% of the time, Pallas kernels for 0%

profile of v11, /device:TPU:8, one launch (start us, length us, event | category | flops | bytes accessed | tf_op | source)
XLA Modules:
  0.0 116.9 jit_solution(12024193003034948128)
XLA Ops:
  0.0 0.9 constant_dynamic-update-slice_fusion.1
  0.9 0.7 constant_dynamic-update-slice_fusion
  1.6 1.9 %collective-permute-start = (bf16[64,1152]{1,0:T(8,128)(2,1)S(1)}, bf16[64,1152]{1,0:T(8,128)(2,1)S(1)}, u32[]{:S(2)}, u32[]{:S(2)}) collective-permute-start(bf16[64,1152]{1,0:T(8,128)(2,1)S(1)} %constant_dynamic-update-slice_fusion), channel_id=1, source_target_pairs={{0,1},{1,0},{2,3},{3,2},{4,5},{5,4},{6,7},{7,6},{8,9},{9,8},{10,11... | collective-permute-start | bytes 442376 | tf_op jit(solution)/shard_map/ppermute | solution.py:37
  3.6 1.5 %broadcast_in_dim.36 = bf16[12,16,1024]{2,1,0:T(8,128)(2,1)} broadcast(bf16[16,1024]{1,0:T(8,128)(2,1)} %param.4), dimensions={1,2} | broadcast | bytes 425984 | tf_op jit(solution)/shard_map/broadcast_in_dim | solution.py:22
  5.1 15.2 %all-to-all-start = ((bf16[12,16,1024]{2,1,0:T(8,128)(2,1)}), bf16[12,16,1024]{2,1,0:T(8,128)(2,1)S(1)}, u32[]{:S(2)}, u32[]{:S(2)}) async-start(bf16[12,16,1024]{2,1,0:T(8,128)(2,1)} %broadcast_in_dim.36), calls=%async_computation | async-start | bytes 786432 | tf_op jit(solution)/shard_map/all_to_all | solution.py:23
  20.3 0.0 collective-permute-done
  20.4 3.5 %collective-permute-start.4 = (bf16[128,1152]{1,0:T(8,128)(2,1)S(1)}, bf16[128,1152]{1,0:T(8,128)(2,1)S(1)}, u32[]{:S(2)}, u32[]{:S(2)}) collective-permute-start(bf16[128,1152]{1,0:T(8,128)(2,1)S(1)} %pad_maximum_fusion), channel_id=1, source_target_pairs={{0,2},{1,15},{2,4},{3,1},{4,6},{5,3},{6,8},{7,5},{8,10},{9,7},{10,... | collective-permute-start | bytes 884744 | tf_op jit(solution)/shard_map/ppermute | solution.py:33
  23.9 5.7 %collective-permute-start.1 = (bf16[128,1152]{1,0:T(8,128)(2,1)S(1)}, bf16[128,1152]{1,0:T(8,128)(2,1)S(1)}, u32[]{:S(2)}, u32[]{:S(2)}) collective-permute-start(bf16[128,1152]{1,0:T(8,128)(2,1)S(1)} %pad_maximum_fusion), channel_id=1, source_target_pairs={{0,4},{1,13},{2,6},{3,15},{4,8},{5,1},{6,10},{7,3},{8,12},{9,5},{1... | collective-permute-start | bytes 884744 | tf_op jit(solution)/shard_map/ppermute | solution.py:33
  29.6 0.8 dynamic-slice_convert_fusion
  30.4 0.1 broadcast_in_dim.40
  30.5 0.1 reshape.73
  30.6 2.1 %collective-permute-start.2 = (bf16[128,1152]{1,0:T(8,128)(2,1)S(1)}, bf16[128,1152]{1,0:T(8,128)(2,1)S(1)}, u32[]{:S(2)}, u32[]{:S(2)}) collective-permute-start(bf16[128,1152]{1,0:T(8,128)(2,1)S(1)} %pad_maximum_fusion), channel_id=1, source_target_pairs={{0,10},{1,7},{2,12},{3,9},{4,14},{5,11},{6,0},{7,13},{8,2},{9,15},... | collective-permute-start | bytes 884744 | tf_op jit(solution)/shard_map/ppermute | solution.py:33
  32.7 0.1 fusion.7
  32.8 0.1 dynamic_update_slice.15
  32.9 0.0 collective-permute-done.4
  32.9 11.4 %collective-permute-done.1 = bf16[128,1152]{1,0:T(8,128)(2,1)S(1)} collective-permute-done((bf16[128,1152]{1,0:T(8,128)(2,1)S(1)}, bf16[128,1152]{1,0:T(8,128)(2,1)S(1)}, u32[]{:S(2)}, u32[]{:S(2)}) %collective-permute-start.1) | collective-permute-done | bytes 294944 | tf_op jit(solution)/shard_map/ppermute | solution.py:33
  44.3 5.3 %collective-permute-start.3 = (bf16[64,1152]{1,0:T(8,128)(2,1)S(1)}, bf16[64,1152]{1,0:T(8,128)(2,1)S(1)}, u32[]{:S(2)}, u32[]{:S(2)}) collective-permute-start(bf16[64,1152]{1,0:T(8,128)(2,1)S(1)} %slice.8), channel_id=1, source_target_pairs={{0,4},{1,13},{2,6},{3,15},{4,8},{5,1},{6,10},{7,3},{8,12},{9,5},{1... | collective-permute-start | bytes 442376 | tf_op jit(solution)/shard_map/ppermute | solution.py:33
  49.6 0.0 collective-permute-done.2
  49.7 3.8 %collective-permute-done.3 = bf16[64,1152]{1,0:T(8,128)(2,1)S(1)} collective-permute-done((bf16[64,1152]{1,0:T(8,128)(2,1)S(1)}, bf16[64,1152]{1,0:T(8,128)(2,1)S(1)}, u32[]{:S(2)}, u32[]{:S(2)}) %collective-permute-start.3) | collective-permute-done | bytes 147488 | tf_op jit(solution)/shard_map/ppermute | solution.py:33
  53.5 1.9 %collective-permute-start.5 = (bf16[512,1152]{1,0:T(8,128)(2,1)S(1)}, bf16[512,1152]{1,0:T(8,128)(2,1)}, u32[]{:S(2)}, u32[]{:S(2)}) collective-permute-start(bf16[512,1152]{1,0:T(8,128)(2,1)S(1)} %constant_dynamic-update-slice_fusion.2.refs_1_), channel_id=1, source_target_pairs={{0,1},{1,0},{2,3},{3,2},{4,5},{5,4},{6,7},{7,6},{8,9},{9,8},{10,11... | collective-permute-start | bytes 3538952 | tf_op jit(solution)/shard_map/ppermute | solution.py:37
  55.4 0.0 all-to-all-done
  55.5 1.3 %broadcast_in_dim.38 = bf16[4,192,1024]{2,1,0:T(8,128)(2,1)} broadcast(bf16[192,1024]{1,0:T(8,128)(2,1)S(1)} %bitcast.11), dimensions={1,2} | broadcast | bytes 1966080 | tf_op jit(solution)/shard_map/broadcast_in_dim | solution.py:22
  56.8 4.3 %all-to-all-start.1 = ((bf16[4,192,1024]{2,1,0:T(8,128)(2,1)}), bf16[4,192,1024]{2,1,0:T(8,128)(2,1)S(1)}, u32[]{:S(2)}, u32[]{:S(2)}) async-start(bf16[4,192,1024]{2,1,0:T(8,128)(2,1)} %broadcast_in_dim.38), calls=%async_computation.1 | async-start | bytes 3145728 | tf_op jit(solution)/shard_map/all_to_all | solution.py:23
  61.1 0.3 multiply_reduce_fusion
  61.4 2.1 %collective-permute-start.6 = (f32[3,8,512]{2,1,0:T(8,128)S(1)}, f32[3,8,512]{2,1,0:T(8,128)S(1)}, u32[]{:S(2)}, u32[]{:S(2)}) collective-permute-start(f32[3,8,512]{2,1,0:T(8,128)S(1)} %bitcast_select_fusion.refs_3_), channel_id=1, source_target_pairs={{0,1},{1,0},{2,3},{3,2},{4,5},{5,4},{6,7},{7,6},{8,9},{9,8},{10,11... | collective-permute-start | bytes 147464 | tf_op jit(solution)/shard_map/ppermute | solution.py:37
  63.5 1.0 collective-permute-done.6.refs_4_
  64.5 0.0 collective-permute-done.5.refs_2_
  64.5 17.9 %all-to-all-done.1 = bf16[4,192,1024]{2,1,0:T(8,128)(2,1)S(1)} async-done(((bf16[4,192,1024]{2,1,0:T(8,128)(2,1)}), bf16[4,192,1024]{2,1,0:T(8,128)(2,1)S(1)}, u32[]{:S(2)}, u32[]{:S(2)}) %all-to-all-start.1) | async-done | bytes 1572896 | tf_op jit(solution)/shard_map/all_to_all | solution.py:23
  82.5 4.9 %score.1 = bf16[48,24,128]{2,1,0:T(8,128)(2,1)S(1)} custom-call(bf16[768,1024]{1,0:T(8,128)(2,1)S(1)} %bitcast.10, bf16[512,1152]{1,0:T(8,128)(2,1)S(1)} %constant_dynamic-update-slice_fusion.2.refs_1_, bf16[512,1152]{1,0:T(8,128)(2,1)} %collective-permute-done.5.refs_2_, f32[3,8,512]{2,1,0:T(8,128)S(1)} %bitcast_select_fusion.refs_3_, ...), custom_call_target="tpu_custom_call" | custom-call | flops 1811939328 | bytes 4227072 | tf_op jit(solution)/shard_map/score/pallas_call | solution.py:114
  87.4 28.5 %all_to_all.15.parts_ref = bf16[48,24,128]{2,1,0:T(8,128)(2,1)S(1)} all-to-all(bf16[48,24,128]{2,1,0:T(8,128)(2,1)S(1)} %score.1), channel_id=1, replica_groups=mesh['zl'=6,'x'=4,'zh'=2,'y'=8,'c'=2] {'x','zl','zh'}, dimensions={0} | all-to-all | bytes 589824 | tf_op jit(solution)/shard_map/all_to_all | solution.py:199
  115.9 1.0 merge.1
  (12 shorter events, 0.2 us)
Async XLA Ops:
  1.6 18.7 %collective-permute-start = (bf16[64,1152]{1,0:T(8,128)(2,1)S(1)}, bf16[64,1152]{1,0:T(8,128)(2,1)S(1)}, u32[]{:S(2)}, u32[]{:S(2)}) collective-permute-start(bf16[64,1152]{1,0:T(8,128)(2,1)S(1)} %constant_dynamic-update-slice_fusion), channel_id=1, source_target_pairs={{0,1},{1,0},{2,3},{3,2},{4,5},{5,4},{6,7},{7,6},{8,9},{9,8},{10,11... | collective-permute-start | bytes 442376 | tf_op jit(solution)/shard_map/ppermute | solution.py:37
  5.1 50.3 %all-to-all-start = ((bf16[12,16,1024]{2,1,0:T(8,128)(2,1)}), bf16[12,16,1024]{2,1,0:T(8,128)(2,1)S(1)}, u32[]{:S(2)}, u32[]{:S(2)}) async-start(bf16[12,16,1024]{2,1,0:T(8,128)(2,1)} %broadcast_in_dim.36), calls=%async_computation | async-start | bytes 786432 | tf_op jit(solution)/shard_map/all_to_all | solution.py:23
  20.4 12.6 %collective-permute-start.4 = (bf16[128,1152]{1,0:T(8,128)(2,1)S(1)}, bf16[128,1152]{1,0:T(8,128)(2,1)S(1)}, u32[]{:S(2)}, u32[]{:S(2)}) collective-permute-start(bf16[128,1152]{1,0:T(8,128)(2,1)S(1)} %pad_maximum_fusion), channel_id=1, source_target_pairs={{0,2},{1,15},{2,4},{3,1},{4,6},{5,3},{6,8},{7,5},{8,10},{9,7},{10,... | collective-permute-start | bytes 884744 | tf_op jit(solution)/shard_map/ppermute | solution.py:33
  23.9 20.4 %collective-permute-start.1 = (bf16[128,1152]{1,0:T(8,128)(2,1)S(1)}, bf16[128,1152]{1,0:T(8,128)(2,1)S(1)}, u32[]{:S(2)}, u32[]{:S(2)}) collective-permute-start(bf16[128,1152]{1,0:T(8,128)(2,1)S(1)} %pad_maximum_fusion), channel_id=1, source_target_pairs={{0,4},{1,13},{2,6},{3,15},{4,8},{5,1},{6,10},{7,3},{8,12},{9,5},{1... | collective-permute-start | bytes 884744 | tf_op jit(solution)/shard_map/ppermute | solution.py:33
  30.6 19.1 %collective-permute-start.2 = (bf16[128,1152]{1,0:T(8,128)(2,1)S(1)}, bf16[128,1152]{1,0:T(8,128)(2,1)S(1)}, u32[]{:S(2)}, u32[]{:S(2)}) collective-permute-start(bf16[128,1152]{1,0:T(8,128)(2,1)S(1)} %pad_maximum_fusion), channel_id=1, source_target_pairs={{0,10},{1,7},{2,12},{3,9},{4,14},{5,11},{6,0},{7,13},{8,2},{9,15},... | collective-permute-start | bytes 884744 | tf_op jit(solution)/shard_map/ppermute | solution.py:33
  44.3 9.1 %collective-permute-start.3 = (bf16[64,1152]{1,0:T(8,128)(2,1)S(1)}, bf16[64,1152]{1,0:T(8,128)(2,1)S(1)}, u32[]{:S(2)}, u32[]{:S(2)}) collective-permute-start(bf16[64,1152]{1,0:T(8,128)(2,1)S(1)} %slice.8), channel_id=1, source_target_pairs={{0,4},{1,13},{2,6},{3,15},{4,8},{5,1},{6,10},{7,3},{8,12},{9,5},{1... | collective-permute-start | bytes 442376 | tf_op jit(solution)/shard_map/ppermute | solution.py:33
  53.5 11.0 %collective-permute-start.5 = (bf16[512,1152]{1,0:T(8,128)(2,1)S(1)}, bf16[512,1152]{1,0:T(8,128)(2,1)}, u32[]{:S(2)}, u32[]{:S(2)}) collective-permute-start(bf16[512,1152]{1,0:T(8,128)(2,1)S(1)} %constant_dynamic-update-slice_fusion.2.refs_1_), channel_id=1, source_target_pairs={{0,1},{1,0},{2,3},{3,2},{4,5},{5,4},{6,7},{7,6},{8,9},{9,8},{10,11... | collective-permute-start | bytes 3538952 | tf_op jit(solution)/shard_map/ppermute | solution.py:37
  56.8 25.7 %all-to-all-start.1 = ((bf16[4,192,1024]{2,1,0:T(8,128)(2,1)}), bf16[4,192,1024]{2,1,0:T(8,128)(2,1)S(1)}, u32[]{:S(2)}, u32[]{:S(2)}) async-start(bf16[4,192,1024]{2,1,0:T(8,128)(2,1)} %broadcast_in_dim.38), calls=%async_computation.1 | async-start | bytes 3145728 | tf_op jit(solution)/shard_map/all_to_all | solution.py:23
  61.4 3.1 %collective-permute-start.6 = (f32[3,8,512]{2,1,0:T(8,128)S(1)}, f32[3,8,512]{2,1,0:T(8,128)S(1)}, u32[]{:S(2)}, u32[]{:S(2)}) collective-permute-start(f32[3,8,512]{2,1,0:T(8,128)S(1)} %bitcast_select_fusion.refs_3_), channel_id=1, source_target_pairs={{0,1},{1,0},{2,3},{3,2},{4,5},{5,4},{6,7},{7,6},{8,9},{9,8},{10,11... | collective-permute-start | bytes 147464 | tf_op jit(solution)/shard_map/ppermute | solution.py:37

commit v12 on v8

--- a/solution.py
+++ b/solution.py
@@ -104,7 +104,7 @@
         stats = stats_rows(row_max, weight_sum, dests, part_rows)
         out_ref[place, part_rows:, :] = jnp.broadcast_to(stats, (dests, 8, LANES)).astype(jnp.bfloat16)
 
-    pl.loop(0, rows // chunk)(step)
+    pl.loop(0, rows // chunk, unroll=True)(step)
 
 
 def score(queries, own, other, own_bias, other_bias, width, tile_rows, part_rows, scale):
@@ -177,10 +177,10 @@
     third = send_on(pair, -3)
     first = send_on(pair, 1)
     second = send_on(pair, 2)
-    fourth = send_on(mine, 4)
+    fourth = send_on(second[:tile_lands], 2)
     fourth, listed = lax.optimization_barrier((fourth, listed))
     own = jnp.zeros((Y * tile_lands, width + classes), jnp.bfloat16)
-    for place, tiles in ((0, mine), (5, third), (1, first), (3, second), (7, fourth)):
+    for place, tiles in ((0, mine), (3, second), (5, third), (1, first), (7, fourth)):
         own = lax.dynamic_update_slice_in_dim(own, tiles, place * tile_lands, 0)
     other = swap_cores(own)
     gathered = gather_direct(gathered, "x", X)

time: 116 us -> 113 us (0.974)
  the two profiles are of different devices: /device:TPU:8 before, /device:TPU:2 now
where the time goes in v12:
time: 113 us
  starting transfers between devices  46.6 us (41%)
  blocking collectives  28 us (25%)
  waiting for transfers between devices  26.4 us (23%)
  Pallas kernels  5.26 us (5%)
  local copies, waits for them, and re-layouts  4.95 us (4%)
    all_to_all x1, blocking collectives, local(): parts = lax.all_to_all(parts, ('x',) + Z_AXES, 0, 0, tiled=True)  28 us
    ppermute x4, starting transfers between devices, send_on(): return lax.ppermute(tiles, ('y', 'c'), pairs)  20.8 us
    all_to_all x2, starting transfers between devices, gather_direct(): gathered = lax.all_to_all(copies, axes, 0, 0, tiled=True)  20 us
    all_to_all x2, waiting for transfers between devices, gather_direct(): gathered = lax.all_to_all(copies, axes, 0, 0, tiled=True)  16.5 us
    ppermute x4, waiting for transfers between devices, send_on(): return lax.ppermute(tiles, ('y', 'c'), pairs)  8.67 us
    ppermute x3, starting transfers between devices, swap_cores(): return lax.ppermute(value, 'c', [(0, 1), (1, 0)])  5.75 us
    pallas_call x1, Pallas kernels, score(): pl.pallas_call(lambda *refs: score_kernel(*refs, width=width, tile_rows=t...  4.26 us
    broadcast_in_dim x2, local copies, waits for them, and re-layouts, gather_direct(): copies = jnp.broadcast_to(value[None], (count,) + value.shape)  2.89 us
  transfers between devices with their start and end apart: 9, of which 5 were waited for; matrix products, arithmetic and copies ran while one was open for 4% of the time, Pallas kernels for 0%

profile of v12, /device:TPU:2, one launch (start us, length us, event | category | flops | bytes accessed | tf_op | source)
XLA Modules:
  0.0 112.6 jit_solution(10216302013978065395)
XLA Ops:
  0.0 0.9 constant_dynamic-update-slice_fusion.1
  0.9 0.7 constant_dynamic-update-slice_fusion
  1.6 1.9 %collective-permute-start = (bf16[64,1152]{1,0:T(8,128)(2,1)S(1)}, bf16[64,1152]{1,0:T(8,128)(2,1)S(1)}, u32[]{:S(2)}, u32[]{:S(2)}) collective-permute-start(bf16[64,1152]{1,0:T(8,128)(2,1)S(1)} %constant_dynamic-update-slice_fusion), channel_id=1, source_target_pairs={{0,1},{1,0},{2,3},{3,2},{4,5},{5,4},{6,7},{7,6},{8,9},{9,8},{10,11... | collective-permute-start | bytes 442376 | tf_op jit(solution)/shard_map/ppermute | solution.py:36
  3.6 1.5 %broadcast_in_dim.36 = bf16[12,16,1024]{2,1,0:T(8,128)(2,1)} broadcast(bf16[16,1024]{1,0:T(8,128)(2,1)} %param.4), dimensions={1,2} | broadcast | bytes 425984 | tf_op jit(solution)/shard_map/broadcast_in_dim | solution.py:21
  5.1 15.2 %all-to-all-start = ((bf16[12,16,1024]{2,1,0:T(8,128)(2,1)}), bf16[12,16,1024]{2,1,0:T(8,128)(2,1)S(1)}, u32[]{:S(2)}, u32[]{:S(2)}) async-start(bf16[12,16,1024]{2,1,0:T(8,128)(2,1)} %broadcast_in_dim.36), calls=%async_computation | async-start | bytes 786432 | tf_op jit(solution)/shard_map/all_to_all | solution.py:22
  20.3 0.0 collective-permute-done
  20.4 4.5 %collective-permute-start.1 = (bf16[128,1152]{1,0:T(8,128)(2,1)S(1)}, bf16[128,1152]{1,0:T(8,128)(2,1)S(1)}, u32[]{:S(2)}, u32[]{:S(2)}) collective-permute-start(bf16[128,1152]{1,0:T(8,128)(2,1)S(1)} %pad_maximum_fusion), channel_id=1, source_target_pairs={{0,4},{1,13},{2,6},{3,15},{4,8},{5,1},{6,10},{7,3},{8,12},{9,5},{1... | collective-permute-start | bytes 884744 | tf_op jit(solution)/shard_map/ppermute | solution.py:32
  24.9 0.8 dynamic-slice_convert_fusion
  25.7 0.1 broadcast_in_dim.40
  25.8 0.1 reshape.73
  25.9 5.1 %collective-permute-start.2 = (bf16[128,1152]{1,0:T(8,128)(2,1)S(1)}, bf16[128,1152]{1,0:T(8,128)(2,1)S(1)}, u32[]{:S(2)}, u32[]{:S(2)}) collective-permute-start(bf16[128,1152]{1,0:T(8,128)(2,1)S(1)} %pad_maximum_fusion), channel_id=1, source_target_pairs={{0,10},{1,7},{2,12},{3,9},{4,14},{5,11},{6,0},{7,13},{8,2},{9,15},... | collective-permute-start | bytes 884744 | tf_op jit(solution)/shard_map/ppermute | solution.py:32
  31.0 0.1 fusion.7
  31.2 0.1 dynamic_update_slice.15
  31.2 1.9 %collective-permute-start.3 = (bf16[128,1152]{1,0:T(8,128)(2,1)S(1)}, bf16[128,1152]{1,0:T(8,128)(2,1)S(1)}, u32[]{:S(2)}, u32[]{:S(2)}) collective-permute-start(bf16[128,1152]{1,0:T(8,128)(2,1)S(1)} %pad_maximum_fusion), channel_id=1, source_target_pairs={{0,2},{1,15},{2,4},{3,1},{4,6},{5,3},{6,8},{7,5},{8,10},{9,7},{10,... | collective-permute-start | bytes 884744 | tf_op jit(solution)/shard_map/ppermute | solution.py:32
  33.2 0.0 collective-permute-done.1
  33.2 9.3 %collective-permute-start.4 = (bf16[64,1152]{1,0:T(8,128)(2,1)S(1)}, bf16[64,1152]{1,0:T(8,128)(2,1)S(1)}, u32[]{:S(2)}, u32[]{:S(2)}) collective-permute-start(bf16[64,1152]{1,0:T(8,128)(2,1)S(1)} %slice.8), channel_id=1, source_target_pairs={{0,4},{1,13},{2,6},{3,15},{4,8},{5,1},{6,10},{7,3},{8,12},{9,5},{1... | collective-permute-start | bytes 442376 | tf_op jit(solution)/shard_map/ppermute | solution.py:32
  42.5 3.0 %collective-permute-done.2 = bf16[128,1152]{1,0:T(8,128)(2,1)S(1)} collective-permute-done((bf16[128,1152]{1,0:T(8,128)(2,1)S(1)}, bf16[128,1152]{1,0:T(8,128)(2,1)S(1)}, u32[]{:S(2)}, u32[]{:S(2)}) %collective-permute-start.2) | collective-permute-done | bytes 294944 | tf_op jit(solution)/shard_map/ppermute | solution.py:32
  45.5 1.3 %collective-permute-done.3 = bf16[128,1152]{1,0:T(8,128)(2,1)S(1)} collective-permute-done((bf16[128,1152]{1,0:T(8,128)(2,1)S(1)}, bf16[128,1152]{1,0:T(8,128)(2,1)S(1)}, u32[]{:S(2)}, u32[]{:S(2)}) %collective-permute-start.3) | collective-permute-done | bytes 294944 | tf_op jit(solution)/shard_map/ppermute | solution.py:32
  46.8 4.4 %collective-permute-done.4 = bf16[64,1152]{1,0:T(8,128)(2,1)S(1)} collective-permute-done((bf16[64,1152]{1,0:T(8,128)(2,1)S(1)}, bf16[64,1152]{1,0:T(8,128)(2,1)S(1)}, u32[]{:S(2)}, u32[]{:S(2)}) %collective-permute-start.4) | collective-permute-done | bytes 147488 | tf_op jit(solution)/shard_map/ppermute | solution.py:32
  51.3 1.9 %collective-permute-start.5 = (bf16[512,1152]{1,0:T(8,128)(2,1)S(1)}, bf16[512,1152]{1,0:T(8,128)(2,1)}, u32[]{:S(2)}, u32[]{:S(2)}) collective-permute-start(bf16[512,1152]{1,0:T(8,128)(2,1)S(1)} %constant_dynamic-update-slice_fusion.2.refs_1_), channel_id=1, source_target_pairs={{0,1},{1,0},{2,3},{3,2},{4,5},{5,4},{6,7},{7,6},{8,9},{9,8},{10,11... | collective-permute-start | bytes 3538952 | tf_op jit(solution)/shard_map/ppermute | solution.py:36
  53.2 0.0 all-to-all-done
  53.2 1.3 %broadcast_in_dim.38 = bf16[4,192,1024]{2,1,0:T(8,128)(2,1)} broadcast(bf16[192,1024]{1,0:T(8,128)(2,1)S(1)} %bitcast.11), dimensions={1,2} | broadcast | bytes 1966080 | tf_op jit(solution)/shard_map/broadcast_in_dim | solution.py:21
  54.6 4.8 %all-to-all-start.1 = ((bf16[4,192,1024]{2,1,0:T(8,128)(2,1)}), bf16[4,192,1024]{2,1,0:T(8,128)(2,1)S(1)}, u32[]{:S(2)}, u32[]{:S(2)}) async-start(bf16[4,192,1024]{2,1,0:T(8,128)(2,1)} %broadcast_in_dim.38), calls=%async_computation.1 | async-start | bytes 3145728 | tf_op jit(solution)/shard_map/all_to_all | solution.py:22
  59.4 0.3 multiply_reduce_fusion
  59.7 1.9 %collective-permute-start.6 = (f32[3,8,512]{2,1,0:T(8,128)S(1)}, f32[3,8,512]{2,1,0:T(8,128)S(1)}, u32[]{:S(2)}, u32[]{:S(2)}) collective-permute-start(f32[3,8,512]{2,1,0:T(8,128)S(1)} %bitcast_select_fusion.refs_3_), channel_id=1, source_target_pairs={{0,1},{1,0},{2,3},{3,2},{4,5},{5,4},{6,7},{7,6},{8,9},{9,8},{10,11... | collective-permute-start | bytes 147464 | tf_op jit(solution)/shard_map/ppermute | solution.py:36
  61.6 1.2 %collective-permute-done.6.refs_4_ = f32[3,8,512]{2,1,0:T(8,128)S(1)} collective-permute-done((f32[3,8,512]{2,1,0:T(8,128)S(1)}, f32[3,8,512]{2,1,0:T(8,128)S(1)}, u32[]{:S(2)}, u32[]{:S(2)}) %collective-permute-start.6) | collective-permute-done | bytes 49184 | tf_op jit(solution)/shard_map/ppermute | solution.py:36
  62.8 0.0 collective-permute-done.5.refs_2_
  62.8 16.5 %all-to-all-done.1 = bf16[4,192,1024]{2,1,0:T(8,128)(2,1)S(1)} async-done(((bf16[4,192,1024]{2,1,0:T(8,128)(2,1)}), bf16[4,192,1024]{2,1,0:T(8,128)(2,1)S(1)}, u32[]{:S(2)}, u32[]{:S(2)}) %all-to-all-start.1) | async-done | bytes 1572896 | tf_op jit(solution)/shard_map/all_to_all | solution.py:22
  79.3 4.3 %score.1 = bf16[48,24,128]{2,1,0:T(8,128)(2,1)S(1)} custom-call(bf16[768,1024]{1,0:T(8,128)(2,1)S(1)} %bitcast.10, bf16[512,1152]{1,0:T(8,128)(2,1)S(1)} %constant_dynamic-update-slice_fusion.2.refs_1_, bf16[512,1152]{1,0:T(8,128)(2,1)} %collective-permute-done.5.refs_2_, f32[3,8,512]{2,1,0:T(8,128)S(1)} %bitcast_select_fusion.refs_3_, ...), custom_call_target="tpu_custom_call" | custom-call | flops 1811939328 | bytes 4227072 | tf_op jit(solution)/shard_map/score/pallas_call | solution.py:114
  83.6 28.0 %all_to_all.15.parts_ref = bf16[48,24,128]{2,1,0:T(8,128)(2,1)S(1)} all-to-all(bf16[48,24,128]{2,1,0:T(8,128)(2,1)S(1)} %score.1), channel_id=1, replica_groups=mesh['zl'=6,'x'=4,'zh'=2,'y'=8,'c'=2] {'x','zl','zh'}, dimensions={0} | all-to-all | bytes 589824 | tf_op jit(solution)/shard_map/all_to_all | solution.py:195
  111.6 1.0 merge.1
  (12 shorter events, 0.2 us)
Async XLA Ops:
  1.6 18.7 %collective-permute-start = (bf16[64,1152]{1,0:T(8,128)(2,1)S(1)}, bf16[64,1152]{1,0:T(8,128)(2,1)S(1)}, u32[]{:S(2)}, u32[]{:S(2)}) collective-permute-start(bf16[64,1152]{1,0:T(8,128)(2,1)S(1)} %constant_dynamic-update-slice_fusion), channel_id=1, source_target_pairs={{0,1},{1,0},{2,3},{3,2},{4,5},{5,4},{6,7},{7,6},{8,9},{9,8},{10,11... | collective-permute-start | bytes 442376 | tf_op jit(solution)/shard_map/ppermute | solution.py:36
  5.1 48.1 %all-to-all-start = ((bf16[12,16,1024]{2,1,0:T(8,128)(2,1)}), bf16[12,16,1024]{2,1,0:T(8,128)(2,1)S(1)}, u32[]{:S(2)}, u32[]{:S(2)}) async-start(bf16[12,16,1024]{2,1,0:T(8,128)(2,1)} %broadcast_in_dim.36), calls=%async_computation | async-start | bytes 786432 | tf_op jit(solution)/shard_map/all_to_all | solution.py:22
  20.4 12.8 %collective-permute-start.1 = (bf16[128,1152]{1,0:T(8,128)(2,1)S(1)}, bf16[128,1152]{1,0:T(8,128)(2,1)S(1)}, u32[]{:S(2)}, u32[]{:S(2)}) collective-permute-start(bf16[128,1152]{1,0:T(8,128)(2,1)S(1)} %pad_maximum_fusion), channel_id=1, source_target_pairs={{0,4},{1,13},{2,6},{3,15},{4,8},{5,1},{6,10},{7,3},{8,12},{9,5},{1... | collective-permute-start | bytes 884744 | tf_op jit(solution)/shard_map/ppermute | solution.py:32
  25.9 19.6 %collective-permute-start.2 = (bf16[128,1152]{1,0:T(8,128)(2,1)S(1)}, bf16[128,1152]{1,0:T(8,128)(2,1)S(1)}, u32[]{:S(2)}, u32[]{:S(2)}) collective-permute-start(bf16[128,1152]{1,0:T(8,128)(2,1)S(1)} %pad_maximum_fusion), channel_id=1, source_target_pairs={{0,10},{1,7},{2,12},{3,9},{4,14},{5,11},{6,0},{7,13},{8,2},{9,15},... | collective-permute-start | bytes 884744 | tf_op jit(solution)/shard_map/ppermute | solution.py:32
  31.2 15.5 %collective-permute-start.3 = (bf16[128,1152]{1,0:T(8,128)(2,1)S(1)}, bf16[128,1152]{1,0:T(8,128)(2,1)S(1)}, u32[]{:S(2)}, u32[]{:S(2)}) collective-permute-start(bf16[128,1152]{1,0:T(8,128)(2,1)S(1)} %pad_maximum_fusion), channel_id=1, source_target_pairs={{0,2},{1,15},{2,4},{3,1},{4,6},{5,3},{6,8},{7,5},{8,10},{9,7},{10,... | collective-permute-start | bytes 884744 | tf_op jit(solution)/shard_map/ppermute | solution.py:32
  33.2 18.1 %collective-permute-start.4 = (bf16[64,1152]{1,0:T(8,128)(2,1)S(1)}, bf16[64,1152]{1,0:T(8,128)(2,1)S(1)}, u32[]{:S(2)}, u32[]{:S(2)}) collective-permute-start(bf16[64,1152]{1,0:T(8,128)(2,1)S(1)} %slice.8), channel_id=1, source_target_pairs={{0,4},{1,13},{2,6},{3,15},{4,8},{5,1},{6,10},{7,3},{8,12},{9,5},{1... | collective-permute-start | bytes 442376 | tf_op jit(solution)/shard_map/ppermute | solution.py:32
  51.3 11.5 %collective-permute-start.5 = (bf16[512,1152]{1,0:T(8,128)(2,1)S(1)}, bf16[512,1152]{1,0:T(8,128)(2,1)}, u32[]{:S(2)}, u32[]{:S(2)}) collective-permute-start(bf16[512,1152]{1,0:T(8,128)(2,1)S(1)} %constant_dynamic-update-slice_fusion.2.refs_1_), channel_id=1, source_target_pairs={{0,1},{1,0},{2,3},{3,2},{4,5},{5,4},{6,7},{7,6},{8,9},{9,8},{10,11... | collective-permute-start | bytes 3538952 | tf_op jit(solution)/shard_map/ppermute | solution.py:36
  54.6 24.7 %all-to-all-start.1 = ((bf16[4,192,1024]{2,1,0:T(8,128)(2,1)}), bf16[4,192,1024]{2,1,0:T(8,128)(2,1)S(1)}, u32[]{:S(2)}, u32[]{:S(2)}) async-start(bf16[4,192,1024]{2,1,0:T(8,128)(2,1)} %broadcast_in_dim.38), calls=%async_computation.1 | async-start | bytes 3145728 | tf_op jit(solution)/shard_map/all_to_all | solution.py:22
  59.7 3.1 %collective-permute-start.6 = (f32[3,8,512]{2,1,0:T(8,128)S(1)}, f32[3,8,512]{2,1,0:T(8,128)S(1)}, u32[]{:S(2)}, u32[]{:S(2)}) collective-permute-start(f32[3,8,512]{2,1,0:T(8,128)S(1)} %bitcast_select_fusion.refs_3_), channel_id=1, source_target_pairs={{0,1},{1,0},{2,3},{3,2},{4,5},{5,4},{6,7},{7,6},{8,9},{9,8},{10,11... | collective-permute-start | bytes 147464 | tf_op jit(solution)/shard_map/ppermute | solution.py:36
